TPU v7x, 512 devices: a whole 4x8x8 slice. The times are simulated.
512 devices in a mesh: seq: 32 (over x, y), head: 16 (over z, core).
Axes of the slice: x: 4, y: 8, z: 8, core: 2. Of those that a mesh axis runs over, the one named last changes fastest.
Arguments:
- queries: bfloat16 [65536, 2048], P(('seq', 'head')), may hold values from -6 to 6
- keys: bfloat16 [65536, 2048], P(('seq', 'head')), may hold values from -6 to 6
- values: bfloat16 [65536, 2048], P(('seq', 'head')), may hold values from -6 to 6
- log_decay: bfloat16 [65536, 16], P(('seq', 'head')), may hold values from -0.6 to 0, as said below
- out_weight: bfloat16 [2048, 2048], P(('seq', 'head')), may hold values from -0.125 to 0.125
Outputs:
- mixed_out: bfloat16 [65536, 2048], P(('seq', 'head'))
Inputs may be any that keep to these rules, and one draw needn't show every extreme that they name: `log_decay`: every entry is at most zero.
All inputs are finite; a program needn't handle non-finite values.
Results may differ from a plain program's by a relative error of at most 0.0054.
Values may be sent and summed in bfloat16 or wider, within the bound.
No kernel may reach another device: no remote copies, remote signals or barrier semaphores. Data moves between devices by JAX's collectives and lax.ppermute only.
A program may use at most 64 MiB of HBM per device.

v0:
```python
import jax
import jax.numpy as jnp
from jax import lax
from jax.sharding import PartitionSpec as P

SPAN = 256


def entering(x, axis, combine, identity):
    count, place = (lax.axis_size(axis), lax.axis_index(axis))
    everything = jax.tree.map(lambda part: lax.all_gather(part, axis), x)
    start = jax.tree.map(
        lambda part, zero: jnp.broadcast_to(jnp.asarray(zero, part.dtype), part.shape), x, identity
    )

    def turn(k, before):
        reached = k < place
        new = combine(before, jax.tree.map(lambda part: part[k], everything))
        return jax.tree.map(lambda a, b: jnp.where(reached, a, b), new, before)

    return lax.fori_loop(0, count, turn, start)


def local(queries, keys, values, log_decay, out_weight):
    queries_loc, keys_loc, values_loc, decay_loc = (
        lax.all_to_all(queries, "head", split_axis=1, concat_axis=0, tiled=True),
        lax.all_to_all(keys, "head", split_axis=1, concat_axis=0, tiled=True),
        lax.all_to_all(values, "head", split_axis=1, concat_axis=0, tiled=True),
        lax.all_to_all(log_decay, "head", split_axis=1, concat_axis=0, tiled=True),
    )
    shard_rows = queries_loc.shape[0]
    head_count = decay_loc.shape[1]
    head_dim = queries_loc.shape[1] // head_count
    block_count = shard_rows // SPAN
    queries_blk = queries_loc.reshape(block_count, SPAN, head_count, head_dim)
    keys_blk = keys_loc.reshape(block_count, SPAN, head_count, head_dim)
    values_blk = values_loc.reshape(block_count, SPAN, head_count, head_dim)
    within = jnp.cumsum(
        decay_loc.reshape(block_count, SPAN, head_count).astype(jnp.float32), axis=1
    )
    block_decay = within[:, -1, :]
    within_t = jnp.transpose(within, (0, 2, 1))
    causal = lax.broadcasted_iota(jnp.int32, (SPAN, SPAN), 0) >= lax.broadcasted_iota(
        jnp.int32, (SPAN, SPAN), 1
    )
    differences = within_t[:, :, :, None] - within_t[:, :, None, :]
    decay_mask = jnp.exp(jnp.where(causal[None, None], differences, -jnp.inf))
    scores = jnp.einsum(
        "nthd,nshd->nhts", queries_blk, keys_blk, preferred_element_type=jnp.float32
    )
    weights = (scores * decay_mask).astype(jnp.bfloat16)
    local_part = jnp.einsum(
        "nhts,nshd->nthd", weights, values_blk, preferred_element_type=jnp.float32
    )
    scaled_keys = (
        jnp.exp(block_decay[:, None, :] - within)[..., None] * keys_blk.astype(jnp.float32)
    ).astype(jnp.bfloat16)
    block_state = jnp.einsum(
        "nshd,nshe->nhde", scaled_keys, values_blk, preferred_element_type=jnp.float32
    )
    decay_incl = jnp.cumsum(block_decay, axis=0)
    decay_excl = decay_incl - block_decay
    block_index = lax.broadcasted_iota(jnp.int32, (block_count, block_count), 0)
    earlier_blocks = block_index > lax.broadcasted_iota(jnp.int32, (block_count, block_count), 1)
    pair_gaps = decay_excl[:, None, :] - decay_incl[None, :, :]
    block_weights = jnp.exp(jnp.where(earlier_blocks[:, :, None], pair_gaps, -jnp.inf))
    prior_states = jnp.einsum(
        "cjh,jhde->chde", block_weights, block_state, precision=lax.Precision.HIGHEST
    )
    total_decay = decay_incl[-1]
    final_state = jnp.einsum(
        "jh,jhde->hde",
        jnp.exp(total_decay[None, :] - decay_incl),
        block_state,
        precision=lax.Precision.HIGHEST,
    )

    def link(earlier, later):
        return (jnp.exp(later[1])[:, None, None] * earlier[0] + later[0], earlier[1] + later[1])

    incoming, _ = entering(
        (final_state, total_decay),
        "seq",
        link,
        (jnp.zeros_like(final_state), jnp.zeros_like(total_decay)),
    )
    full_states = prior_states + jnp.exp(decay_excl)[:, :, None, None] * incoming[None]
    scaled_queries = queries_blk.astype(jnp.float32) * jnp.exp(within)[..., None]
    carried_part = jnp.einsum(
        "nthd,nhde->nthe", scaled_queries, full_states, precision=lax.Precision.HIGHEST
    )
    combined = local_part + carried_part
    normed = (
        combined * lax.rsqrt(jnp.mean(combined * combined, axis=-1, keepdims=True) + 1e-05)
    ).astype(jnp.bfloat16)
    normed = normed.reshape(shard_rows, head_count * head_dim)
    restored = lax.all_to_all(normed, "head", split_axis=0, concat_axis=1, tiled=True)
    projected = jnp.dot(
        restored,
        lax.all_gather(out_weight, ("seq", "head"), axis=0, tiled=True),
        preferred_element_type=jnp.float32,
    )
    return projected.astype(jnp.bfloat16)


def solution(mesh):
    placed = (
        P(("seq", "head"), None),
        P(("seq", "head"), None),
        P(("seq", "head"), None),
        P(("seq", "head"), None),
        P(("seq", "head"), None),
    )
    return jax.shard_map(
        local, mesh=mesh, in_specs=placed, out_specs=P(("seq", "head"), None), check_vma=False
    )
```

profile of v0, /device:TPU:1, one launch (start us, length us, event | category | flops | bytes accessed | tf_op | source)
XLA Modules:
  0.0 307.7 jit_solution(8402958771548732288)
XLA Ops:
  6.5 1.3 copy.47
  7.9 11.8 %all-to-all-start.2 = ((bf16[128,16,1]{0,2,1:T(2,128)(2,1)}), bf16[128,16,1]{0,2,1:T(2,128)(2,1)S(1)}, u32[]{:S(2)}, u32[]{:S(2)}) async-start(bf16[128,16,1]{0,2,1:T(2,128)(2,1)} %copy.47), calls=%async_computation.2 | async-start | bytes 16384 | tf_op jit(solution)/shard_map/all_to_all | solution.py:29
  19.7 2.0 copy.45
  21.7 4.9 %all-to-all-done.2 = bf16[128,16,1]{0,2,1:T(2,128)(2,1)S(1)} async-done(((bf16[128,16,1]{0,2,1:T(2,128)(2,1)}), bf16[128,16,1]{0,2,1:T(2,128)(2,1)S(1)}, u32[]{:S(2)}, u32[]{:S(2)}) %all-to-all-start.2) | async-done | bytes 4128 | tf_op jit(solution)/shard_map/all_to_all | solution.py:29
  26.7 4.0 %all-to-all-start.1 = ((bf16[128,16,128]{0,2,1:T(8,128)(2,1)}), bf16[128,16,128]{0,2,1:T(8,128)(2,1)S(1)}, u32[]{:S(2)}, u32[]{:S(2)}) async-start(bf16[128,16,128]{0,2,1:T(8,128)(2,1)} %bitcast.2), calls=%async_computation.1 | async-start | bytes 1048576 | tf_op jit(solution)/shard_map/all_to_all | solution.py:27
  30.7 0.9 copy_bitcast_fusion
  32.4 15.6 %all-to-all-done.1 = bf16[128,16,128]{0,2,1:T(8,128)(2,1)S(1)} async-done(((bf16[128,16,128]{0,2,1:T(8,128)(2,1)}), bf16[128,16,128]{0,2,1:T(8,128)(2,1)S(1)}, u32[]{:S(2)}, u32[]{:S(2)}) %all-to-all-start.1) | async-done | bytes 524320 | tf_op jit(solution)/shard_map/all_to_all | solution.py:27
  48.0 3.5 %all-to-all-start.3 = ((bf16[128,16,128]{2,0,1:T(8,128)(2,1)}), bf16[128,16,128]{2,0,1:T(8,128)(2,1)S(1)}, u32[]{:S(2)}, u32[]{:S(2)}) async-start(bf16[128,16,128]{2,0,1:T(8,128)(2,1)} %copy_bitcast_fusion), calls=%async_computation.3 | async-start | bytes 1048576 | tf_op jit(solution)/shard_map/all_to_all | solution.py:28
  53.0 15.1 %all-to-all-done.3 = bf16[128,16,128]{2,0,1:T(8,128)(2,1)S(1)} async-done(((bf16[128,16,128]{2,0,1:T(8,128)(2,1)}), bf16[128,16,128]{2,0,1:T(8,128)(2,1)S(1)}, u32[]{:S(2)}, u32[]{:S(2)}) %all-to-all-start.3) | async-done | bytes 524320 | tf_op jit(solution)/shard_map/all_to_all | solution.py:28
  68.1 0.8 fusion.14
  68.9 2.0 fusion.18
  71.0 0.7 all-gather.7.cloned.1.call-update
  71.7 0.9 copy_bitcast_fusion.1
  72.6 3.5 %all-to-all-start = ((bf16[128,16,128]{2,0,1:T(8,128)(2,1)}), bf16[128,16,128]{2,0,1:T(8,128)(2,1)S(1)}, u32[]{:S(2)}, u32[]{:S(2)}) async-start(bf16[128,16,128]{2,0,1:T(8,128)(2,1)} %copy_bitcast_fusion.1), calls=%async_computation | async-start | bytes 1048576 | tf_op jit(solution)/shard_map/all_to_all | solution.py:26
  76.1 1.3 dynamic-slice
  77.5 1.1 bitcast_dynamic-update-slice_fusion
  78.7 61.9 %all-reduce = f32[32]{0:T(128)S(1)} all-reduce(f32[32]{0:T(128)S(1)} %bitcast_dynamic-update-slice_fusion), channel_id=1, replica_groups=mesh['seq'=32,'head'=16] {'seq'}, use_global_device_ids=true, to_apply=%add | all-reduce | flops 32 | bytes 256
  140.8 5.6 %all-gather.5.cloned.1.call-done = f32[4096,128]{1,0:T(8,128)} async-done(((f32[128,128]{1,0:T(8,128)}), f32[4096,128]{1,0:T(8,128)}) %all-gather.5.cloned.1.call-update) | async-done | bytes 2097168 | tf_op jit(solution)/shard_map/all_gather | solution.py:11
  146.4 64.9 %while.14 = (s32[]{:T(128)}, f32[1,128,128]{2,1,0:T(8,128)S(1)}, s32[]{:T(128)}, f32[32,1]{0,1:T(1,128)S(1)}, f32[32,1,128,128]{3,2,1,0:T(8,128)}, /*index=5*/s32[]{:T(128)}, s32[]{:T(128)}) while((s32[]{:T(128)}, f32[1,128,128]{2,1,0:T(8,128)S(1)}, s32[]{:T(128)}, f32[32,1]{0,1:T(1,128)S(1)}, f32[32,1,128,128]{3,2,1,0:T(8,128)}, ...), condition=%wide.region_4.5_spmd.clone, body=%wide.region_3.4_spmd.clone.sunk | while | flops 65540 | bytes 196733 | solution.py:21
  147.0 1.4 fusion.49
  149.0 1.4 fusion.49
  151.0 1.4 fusion.49
  153.0 1.4 fusion.49
  154.5 0.6 fusion.48
  155.1 1.4 fusion.49
  157.1 1.4 fusion.49
  159.1 1.4 fusion.49
  160.6 0.6 fusion.48
  161.2 1.4 fusion.49
  163.2 1.4 fusion.49
  165.2 1.4 fusion.49
  167.3 1.4 fusion.49
  169.3 1.4 fusion.49
  171.3 1.4 fusion.49
  173.3 1.4 fusion.49
  175.4 1.4 fusion.49
  177.4 1.4 fusion.49
  179.4 1.4 fusion.49
  181.5 1.4 fusion.49
  183.5 1.4 fusion.49
  185.5 1.4 fusion.49
  187.6 1.4 fusion.49
  189.6 1.4 fusion.49
  191.6 1.4 fusion.49
  193.6 1.4 fusion.49
  195.7 1.4 fusion.49
  197.7 1.4 fusion.49
  199.1 0.6 fusion.48
  199.7 1.4 fusion.49
  201.8 1.4 fusion.49
  203.8 1.4 fusion.49
  205.2 0.6 fusion.48
  205.8 1.4 fusion.49
  207.8 1.4 fusion.49
  209.9 1.4 fusion.49
  211.3 0.9 fusion.6
  212.2 2.2 fusion.7
  214.4 3.2 %multiply_reduce_fusion = (f32[8,256]{1,0:T(8,128)S(1)}, f32[8,1,128,256]{2,3,0,1:T(8,128)}) fusion(f32[8,128,256]{1,2,0:T(8,128)} %fusion.7, bf16[8,256,128]{2,1,0:T(8,128)(2,1)S(1)} %bitcast.101, bf16[8,256,128]{2,1,0:T(8,128)(2,1)S(1)} %bitcast.107, bf16[8,256,128]{2,1,0:T(8,128)(2,1)S(1)} %bitcast.103, f32[8,256]{1,0:T(8,128)S(1)} %get-tuple-element.129, ...), kind=kOutput, calls=%fused_computation.13 | convolution fusion | flops 271316992 | bytes 3751936 | tf_op jit(solution)/shard_map/nhts,nshd->nthd/dot_general | solution.py:52
  217.6 1.6 multiply_convert_fusion.1
  219.2 1.0 copy.55
  220.2 14.9 %all-to-all-start.4 = ((bf16[16,128,128]{1,2,0:T(8,128)(2,1)}), bf16[16,128,128]{1,2,0:T(8,128)(2,1)S(1)}, u32[]{:S(2)}, u32[]{:S(2)}) async-start(bf16[16,128,128]{1,2,0:T(8,128)(2,1)} %copy.55), calls=%async_computation.4 | async-start | bytes 1048576 | tf_op jit(solution)/shard_map/all_to_all | solution.py:97
  235.1 47.8 %all-gather.7.cloned.1.call-done = bf16[512,4,2048]{2,1,0:T(4,128)(2,1)} async-done(((bf16[1,4,2048]{2,1,0:T(4,128)(2,1)}), bf16[512,4,2048]{2,1,0:T(4,128)(2,1)}) %all-gather.7.cloned.1.call-update) | async-done | bytes 8388624 | tf_op jit(solution)/shard_map/all_gather | solution.py:100
  282.9 12.5 %reshape.334 = bf16[2048,2048]{1,0:T(8,128)(2,1)} reshape(bf16[512,4,2048]{2,1,0:T(4,128)(2,1)} %all-gather.7.cloned.1.call-done) | data formatting | bytes 16777216
  295.4 5.5 %convolution_convert_fusion = bf16[128,2048]{1,0:T(8,128)(2,1)} fusion(bf16[128,2048]{0,1:T(8,128)(2,1)S(1)} %bitcast.98, bf16[2048,2048]{1,0:T(8,128)(2,1)} %reshape.334), kind=kOutput, calls=%fused_computation.3 | convolution fusion | flops 1074003968 | bytes 9437184 | tf_op jit(solution)/shard_map/dot_general | solution.py:98
  (57 shorter events, 19.1 us)
Async XLA Ops:
  6.5 24.2 %copy-start = (bf16[128,2048]{1,0:T(8,128)(2,1)S(1)}, bf16[128,2048]{1,0:T(8,128)(2,1)}, u32[]{:S(2)}) copy-start(bf16[128,2048]{1,0:T(8,128)(2,1)} %param.9) | copy-start | bytes 1572868
  7.9 18.8 %all-to-all-start.2 = ((bf16[128,16,1]{0,2,1:T(2,128)(2,1)}), bf16[128,16,1]{0,2,1:T(2,128)(2,1)S(1)}, u32[]{:S(2)}, u32[]{:S(2)}) async-start(bf16[128,16,1]{0,2,1:T(2,128)(2,1)} %copy.47), calls=%async_computation.2 | async-start | bytes 16384 | tf_op jit(solution)/shard_map/all_to_all | solution.py:29
  26.7 21.3 %all-to-all-start.1 = ((bf16[128,16,128]{0,2,1:T(8,128)(2,1)}), bf16[128,16,128]{0,2,1:T(8,128)(2,1)S(1)}, u32[]{:S(2)}, u32[]{:S(2)}) async-start(bf16[128,16,128]{0,2,1:T(8,128)(2,1)} %bitcast.2), calls=%async_computation.1 | async-start | bytes 1048576 | tf_op jit(solution)/shard_map/all_to_all | solution.py:27
  32.4 39.3 %copy-start.1 = (bf16[128,2048]{1,0:T(8,128)(2,1)S(1)}, bf16[128,2048]{1,0:T(8,128)(2,1)}, u32[]{:S(2)}) copy-start(bf16[128,2048]{1,0:T(8,128)(2,1)} %param.7) | copy-start | bytes 1572868
  48.0 20.1 %all-to-all-start.3 = ((bf16[128,16,128]{2,0,1:T(8,128)(2,1)}), bf16[128,16,128]{2,0,1:T(8,128)(2,1)S(1)}, u32[]{:S(2)}, u32[]{:S(2)}) async-start(bf16[128,16,128]{2,0,1:T(8,128)(2,1)} %copy_bitcast_fusion), calls=%async_computation.3 | async-start | bytes 1048576 | tf_op jit(solution)/shard_map/all_to_all | solution.py:28
  51.5 94.9 %all-gather.5.cloned.1.call-start = ((), (), s32[]{:S(2)}) async-start(), calls=%async_computation.5 | async-start | bytes 2162688 | tf_op jit(solution)/shard_map/all_gather | solution.py:11
  70.9 211.9 %all-gather.7.cloned.1.call-start = ((), (), s32[]{:S(2)}) async-start(), calls=%async_computation.6 | async-start | bytes 8404992 | tf_op jit(solution)/shard_map/all_gather | solution.py:100
  72.6 139.6 %all-to-all-start = ((bf16[128,16,128]{2,0,1:T(8,128)(2,1)}), bf16[128,16,128]{2,0,1:T(8,128)(2,1)S(1)}, u32[]{:S(2)}, u32[]{:S(2)}) async-start(bf16[128,16,128]{2,0,1:T(8,128)(2,1)} %copy_bitcast_fusion.1), calls=%async_computation | async-start | bytes 1048576 | tf_op jit(solution)/shard_map/all_to_all | solution.py:26
  220.2 75.2 %all-to-all-start.4 = ((bf16[16,128,128]{1,2,0:T(8,128)(2,1)}), bf16[16,128,128]{1,2,0:T(8,128)(2,1)S(1)}, u32[]{:S(2)}, u32[]{:S(2)}) async-start(bf16[16,128,128]{1,2,0:T(8,128)(2,1)} %copy.55), calls=%async_computation.4 | async-start | bytes 1048576 | tf_op jit(solution)/shard_map/all_to_all | solution.py:97
Sparse Core Ops, SparseCore 0:
  71.1 75.2 all-gather.4
  150.9 131.8 all-gather.6
where the time goes:
time: 310 us; the launch traced here: 308 us
  waiting for transfers between devices  89.7 us (29%)
  blocking collectives  61.9 us (20%)
  other arithmetic  48.3 us (16%)
  local copies, waits for them, and re-layouts  41.1 us (13%)
  starting transfers between devices  37.7 us (12%)
  matrix products  14.5 us (5%)
  between operations  13.5 us (4%)
    unnamed x1, blocking collectives  61.9 us
    all_gather x1, waiting for transfers between devices, local(): lax.all_gather(out_weight, ('seq', 'head'), axis=0, tiled=True)  47.8 us
    select_n x32, other arithmetic, turn(): return jax.tree.map(lambda a, b: jnp.where(reached, a, b), new, before)  45.4 us
    exp x32, local copies, waits for them, and re-layouts, link(): jnp.exp(later[1])[:, None, None] * earlier[0] + later[0]  18.8 us
    unnamed x9, local copies, waits for them, and re-layouts  16.9 us
    all_to_all x1, waiting for transfers between devices, local(): lax.all_to_all(keys, 'head', split_axis=1, concat_axis=0, tiled=True)  15.6 us
    all_to_all x1, waiting for transfers between devices, local(): lax.all_to_all(values, 'head', split_axis=1, concat_axis=0, tiled=True)  15.1 us
    all_to_all x1, starting transfers between devices, local(): lax.all_to_all(normed, 'head', split_axis=0, concat_axis=1, tiled=True)  14.9 us
  transfers between devices with their start and end apart: 7, of which 5 were waited for; matrix products, arithmetic and copies ran while one was open for 31% of the time, Pallas kernels for 0%

commit v1 on v0

v1 whole, which is shorter than its diff:
```python
import jax
import jax.numpy as jnp
from jax import lax
from jax.experimental import pallas as pl
from jax.experimental.pallas import tpu as pltpu
from jax.sharding import PartitionSpec as P

HD = 128
PAD = 8
BF16 = jnp.bfloat16
F32 = jnp.float32
VMEM = pltpu.CompilerParams(vmem_limit_bytes=40 * 1024 * 1024)


def ones_below(rows):
    return (
        lax.broadcasted_iota(jnp.int32, (rows, rows), 0)
        >= lax.broadcasted_iota(jnp.int32, (rows, rows), 1)
    ).astype(BF16)


def dot(a, b, ca, cb):
    return lax.dot_general(a, b, (((ca,), (cb,)), ((), ())), preferred_element_type=F32)


def within_rows(decay_t):
    return dot(decay_t, ones_below(decay_t.shape[1]), 1, 1)


def within_cols(decay_t):
    return dot(ones_below(decay_t.shape[1]), decay_t, 1, 1)


def states_kernel(decay_ref, keys_ref, values_ref, out_ref):
    heads, count = decay_ref.shape
    within = within_rows(decay_ref[...])
    total = within[:, count - 1 : count]
    coef = jnp.exp(total - within)
    row = lax.broadcasted_iota(jnp.int32, (PAD, HD), 0)
    for h in range(heads):
        cols = slice(h * HD, (h + 1) * HD)
        keys_t = keys_ref[:, cols].astype(F32).T * coef[h : h + 1, :]
        state = dot(keys_t.astype(BF16), values_ref[:, cols], 1, 0)
        out_ref[h, :HD, :] = state.astype(BF16)
        whole = jnp.broadcast_to(total[h : h + 1, :], (PAD, HD))
        high = whole.astype(BF16).astype(F32)
        middle = (whole - high).astype(BF16).astype(F32)
        low = whole - high - middle
        parts = jnp.where(row == 0, high, jnp.where(row == 1, middle, jnp.where(row == 2, low, 0.0)))
        out_ref[h, HD:, :] = parts.astype(BF16)


def total_of(ref, i):
    parts = ref[i, HD:, :].astype(F32)
    return parts[0:1, :] + parts[1:2, :] + parts[2:3, :]


def group_kernel(group_ref, out_ref, work_ref):
    chunks = out_ref.shape[0]
    rows = HD // chunks
    state = jnp.zeros((HD, HD), F32)
    total = jnp.zeros((1, HD), F32)
    for i in range(group_ref.shape[0]):
        step = total_of(group_ref, i)
        state = jnp.exp(step) * state + group_ref[i, :HD, :].astype(F32)
        total = total + step
    work_ref[...] = state
    for j in range(chunks):
        out_ref[j, :rows, :] = work_ref[rows * j : rows * (j + 1), :]
        out_ref[j, rows:, :] = jnp.broadcast_to(total, (PAD - rows, HD))


def scan_kernel(in_ref, out_ref):
    rows = out_ref.shape[1]
    state = jnp.zeros((rows, HD), F32)
    for i in range(in_ref.shape[0]):
        out_ref[i] = state
        state = jnp.exp(in_ref[i, rows : rows + 1, :]) * state + in_ref[i, :rows, :]


def prior_kernel(chunks_ref, group_ref, out_ref, work_ref):
    chunks, rows, _ = chunks_ref.shape
    for j in range(chunks):
        work_ref[rows * j : rows * (j + 1), :] = chunks_ref[j]
    state = work_ref[...]
    for i in range(group_ref.shape[0]):
        out_ref[i] = state.astype(BF16)
        state = jnp.exp(total_of(group_ref, i)) * state + group_ref[i, :HD, :].astype(F32)


def local_kernel(decay_ref, queries_ref, keys_ref, values_ref, out_ref):
    heads, count = decay_ref.shape
    rows = within_rows(decay_ref[...])
    cols = within_cols(decay_ref[...])
    causal = lax.broadcasted_iota(jnp.int32, (count, count), 0) >= lax.broadcasted_iota(
        jnp.int32, (count, count), 1
    )
    for h in range(heads):
        part = slice(h * HD, (h + 1) * HD)
        scores = dot(queries_ref[:, part], keys_ref[:, part], 1, 1)
        gaps = cols[:, h : h + 1] - rows[h : h + 1, :]
        decay = jnp.exp(jnp.where(causal, gaps, -jnp.inf))
        weights = (scores * decay).astype(BF16)
        out_ref[:, part] = dot(weights, values_ref[:, part], 1, 0)


def norm_kernel(decay_ref, queries_ref, local_ref, prior_ref, out_ref):
    heads = decay_ref.shape[0]
    scale = jnp.exp(within_cols(decay_ref[...]))
    place = lax.broadcasted_iota(jnp.int32, (HD, HD), 1)
    source = lax.broadcasted_iota(jnp.int32, (HD, HD), 0)
    quarter = HD // 8
    wanted = (place // 4 % 2) * (4 * quarter) + (place // 8) * 4 + place % 4
    reorder = (source == wanted).astype(BF16)
    for h in range(heads):
        part = slice(h * HD, (h + 1) * HD)
        carried = dot(queries_ref[:, part], prior_ref[h], 1, 0) * scale[:, h : h + 1]
        combined = local_ref[:, part] + carried
        square = jnp.mean(combined * combined, axis=-1, keepdims=True)
        normed = (combined * lax.rsqrt(square + 1e-05)).astype(BF16)
        out_ref[:, part] = dot(normed, reorder, 1, 0).astype(BF16)


def project_kernel(normed_ref, weight_ref, out_ref, rows_ref, sems):
    heads = weight_ref.shape[1]

    def copy(h):
        return pltpu.make_async_copy(weight_ref.at[:, h], rows_ref.at[h], sems.at[h])

    for h in range(heads):
        copy(h).start()
    acc = jnp.zeros(out_ref.shape, F32)
    for h in range(0, heads, 2):
        copy(h).wait()
        copy(h + 1).wait()
        rows = rows_ref[h : h + 2].reshape(2 * HD, out_ref.shape[1])
        acc = acc + dot(normed_ref[:, h * HD : (h + 2) * HD], rows, 1, 0)
    out_ref[...] = acc.astype(BF16)


def shape(*dims, kind=F32):
    return jax.ShapeDtypeStruct(dims, kind)


def mix(queries, keys, values, log_decay, out_weight):
    count, width = queries.shape
    heads = log_decay.shape[1]
    groups = lax.axis_size("seq")
    members = lax.axis_size("head")
    decay_t = log_decay.T

    weight_rows = out_weight.shape[0]
    spread = jnp.broadcast_to(out_weight[None], (groups, weight_rows, width))
    spread = lax.all_to_all(spread, "seq", split_axis=0, concat_axis=0, tiled=True)
    spread = spread.reshape(groups * weight_rows, width)
    weight = lax.all_gather(spread, "head", axis=0, tiled=True)

    own = pl.pallas_call(
        states_kernel, out_shape=shape(heads, HD + PAD, HD, kind=BF16), compiler_params=VMEM
    )(decay_t, keys, values)
    group = lax.all_to_all(own, "head", split_axis=0, concat_axis=0, tiled=True)
    local_part = pl.pallas_call(
        local_kernel, out_shape=shape(count, width), compiler_params=VMEM
    )(decay_t, queries, keys, values)
    chunks = pl.pallas_call(
        group_kernel,
        out_shape=shape(groups, PAD, HD),
        scratch_shapes=[pltpu.VMEM((HD, HD), F32)],
        compiler_params=VMEM,
    )(group)
    chunks = lax.all_to_all(chunks, "seq", split_axis=0, concat_axis=0, tiled=True)
    chunks = pl.pallas_call(
        scan_kernel, out_shape=shape(groups, HD // groups, HD), compiler_params=VMEM
    )(chunks)
    chunks = lax.all_to_all(chunks, "seq", split_axis=0, concat_axis=0, tiled=True)
    prior = pl.pallas_call(
        prior_kernel,
        out_shape=shape(members, HD, HD, kind=BF16),
        scratch_shapes=[pltpu.VMEM((HD, HD), F32)],
        compiler_params=VMEM,
    )(chunks, group)
    prior = lax.all_to_all(prior, "head", split_axis=0, concat_axis=0, tiled=True)
    normed = pl.pallas_call(
        norm_kernel, out_shape=shape(count, width, kind=BF16), compiler_params=VMEM
    )(decay_t, queries, local_part, prior)
    runs = 2 * weight_rows
    weight = weight.reshape(members, groups // 2, runs, width)
    weight = pltpu.with_memory_space_constraint(weight, pltpu.HBM)
    vmem = pl.BlockSpec(memory_space=pltpu.VMEM)
    return pl.pallas_call(
        project_kernel,
        out_shape=shape(count, width, kind=BF16),
        in_specs=[vmem, pl.BlockSpec(memory_space=pltpu.HBM)],
        out_specs=vmem,
        scratch_shapes=[
            pltpu.VMEM((heads, members, runs, width), BF16),
            pltpu.SemaphoreType.DMA((heads,)),
        ],
        compiler_params=VMEM,
    )(normed, weight)


def solution(mesh):
    placed = P(("seq", "head"), None)
    return jax.shard_map(mix, mesh=mesh, in_specs=(placed,) * 5, out_specs=placed, check_vma=False)
```

time: 310 us -> 139 us (0.45)
  waiting for transfers between devices: 89.7 us -> 14.8 us
  other arithmetic: 48.3 us -> 0 us
  local copies, waits for them, and re-layouts: 41.1 us -> 4.78 us
  starting transfers between devices: 37.7 us -> 5.96 us
  blocking collectives: 61.9 us -> 89.4 us
  matrix products: 14.5 us -> 0 us
  Pallas kernels: 0 us -> 10.5 us
    all_to_all x0 -> x4, blocking collectives: none -> 89.4 us  [the longest x1 37.5 us: mix(): group = lax.all_to_all(own, 'head', split_axis=0, concat_axis=0, tiled=True)]
    unnamed x1 -> x0, blocking collectives: 61.9 us -> none
    all_gather x2 -> x1, waiting for transfers between devices: 53.4 us -> 0.02 us  [mix(): weight = lax.all_gather(spread, 'head', axis=0, tiled=True)]
    select_n x32 -> x0, other arithmetic: 45.4 us -> none  [turn(): return jax.tree.map(lambda a, b: jnp.where(reached, a, b), new, before)]
    all_to_all x5 -> x1, starting transfers between devices: 37.7 us -> 5.93 us  [mix(): lax.all_to_all(prior, 'head', split_axis=0, concat_axis=0, tiled=True)]
    all_to_all x5 -> x1, waiting for transfers between devices: 35.6 us -> 14.8 us  [mix(): lax.all_to_all(prior, 'head', split_axis=0, concat_axis=0, tiled=True)]
    exp x32 -> x0, local copies, waits for them, and re-layouts: 18.8 us -> none  [link(): jnp.exp(later[1])[:, None, None] * earlier[0] + later[0]]
    dot_general x6 -> x0, matrix products: 14.5 us -> none  [the longest x1 5.46 us: local(): jnp.dot(restored, lax.all_gather(out_weight, ('seq', 'head'), axis=0, til...]
  transfers between devices with their start and end apart: 7 -> 2, of which waited for: 5 -> 1; matrix products, arithmetic and copies ran while one was open for 31% -> 0% of each run, Pallas kernels for 0% -> 4%
where the time goes in v1:
time: 139 us
  blocking collectives  89.4 us (64%)
  waiting for transfers between devices  14.8 us (11%)
  between operations  13.5 us (10%)
  Pallas kernels  10.5 us (8%)
  starting transfers between devices  5.96 us (4%)
  local copies, waits for them, and re-layouts  4.78 us (3%)
    all_to_all x1, blocking collectives, mix(): group = lax.all_to_all(own, 'head', split_axis=0, concat_axis=0, tiled=True)  37.5 us
    all_to_all x2, blocking collectives, mix(): lax.all_to_all(chunks, 'seq', split_axis=0, concat_axis=0, tiled=True)  27.1 us
    all_to_all x1, blocking collectives, mix(): lax.all_to_all(spread, 'seq', split_axis=0, concat_axis=0, tiled=True)  24.8 us
    all_to_all x1, waiting for transfers between devices, mix(): lax.all_to_all(prior, 'head', split_axis=0, concat_axis=0, tiled=True)  14.8 us
    all_to_all x1, starting transfers between devices, mix(): lax.all_to_all(prior, 'head', split_axis=0, concat_axis=0, tiled=True)  5.93 us
    pallas_call x1, Pallas kernels, mix(): pl.pallas_call(project_kernel, out_shape=shape(count, width, kind=BF16),...  4.63 us
  transfers between devices with their start and end apart: 2, of which 1 were waited for; matrix products, arithmetic and copies ran while one was open for 0% of the time, Pallas kernels for 4%

profile of v1, /device:TPU:1, one launch (start us, length us, event | category | flops | bytes accessed | tf_op | source)
XLA Modules:
  0.0 138.9 jit_solution(17068247020361853073)
XLA Ops:
  6.5 0.0 copy-start.6
  6.5 0.0 copy-start.1
  6.5 0.0 copy-start.3
  6.5 0.0 copy-start.4
  6.5 0.0 all-gather.2.cloned.1.call-start
  6.6 1.1 broadcast_in_dim.2
  7.7 24.8 %all_to_all.25 = bf16[32,4,2048]{2,1,0:T(4,128)(2,1)S(1)} all-to-all(bf16[32,4,2048]{2,1,0:T(4,128)(2,1)S(1)} %broadcast_in_dim.2), channel_id=1, replica_groups=mesh['seq'=32,'head'=16] {'seq'}, dimensions={0} | all-to-all | bytes 1048576 | tf_op jit(solution)/shard_map/all_to_all | solution.py:154
  32.5 0.9 reshape.7
  33.4 0.0 all-gather.2.cloned.1.call-update
  33.4 0.0 copy-start
  33.4 1.0 copy-done
  34.5 0.0 copy-start.2
  34.5 1.0 copy-done.2
  35.5 0.0 copy-start.5
  35.5 0.7 copy-done.5
  36.2 0.6 shard_map.56
  36.8 37.5 %all_to_all.26.group_ref = bf16[16,136,128]{2,1,0:T(8,128)(2,1)S(1)} all-to-all(bf16[16,136,128]{2,1,0:T(8,128)(2,1)S(1)} %shard_map.56), channel_id=1, replica_groups=mesh['seq'=32,'head'=16] {'head'}, dimensions={0} | all-to-all | bytes 1114112 | tf_op jit(solution)/shard_map/all_to_all | solution.py:161
  74.2 0.1 shard_map.57
  74.4 14.0 %all_to_all.27.in_ref = f32[32,8,128]{2,1,0:T(8,128)S(1)} all-to-all(f32[32,8,128]{2,1,0:T(8,128)S(1)} %shard_map.57), channel_id=1, replica_groups=mesh['seq'=32,'head'=16] {'seq'}, dimensions={0} | all-to-all | bytes 262144 | tf_op jit(solution)/shard_map/all_to_all | solution.py:171
  88.4 0.1 shard_map.58
  88.5 13.1 %all_to_all.28.chunks_ref = f32[32,4,128]{2,1,0:T(4,128)S(1)} all-to-all(f32[32,4,128]{2,1,0:T(4,128)S(1)} %shard_map.58), channel_id=1, replica_groups=mesh['seq'=32,'head'=16] {'seq'}, dimensions={0} | all-to-all | bytes 131072 | tf_op jit(solution)/shard_map/all_to_all | solution.py:175
  101.5 0.9 shard_map.59
  102.5 5.9 %all-to-all-start.3 = ((bf16[16,128,128]{2,1,0:T(8,128)(2,1)}), bf16[16,128,128]{2,1,0:T(8,128)(2,1)S(1)}, u32[]{:S(2)}, u32[]{:S(2)}) async-start(bf16[16,128,128]{2,1,0:T(8,128)(2,1)} %shard_map.59), calls=%async_computation.3 | async-start | bytes 1048576 | tf_op jit(solution)/shard_map/all_to_all | solution.py:182
  108.4 0.0 copy-done.6
  108.4 0.0 copy-done.1
  108.4 0.0 copy-done.3
  108.4 0.0 copy-done.4
  108.5 2.5 %shard_map.55.local_ref = f32[128,2048]{1,0:T(8,128)S(1)} custom-call(bf16[16,128]{1,0:T(8,128)(2,1)S(1)} %bitcast.3, bf16[128,2048]{1,0:T(8,128)(2,1)S(1)} %copy-done.4, bf16[128,2048]{1,0:T(8,128)(2,1)S(1)} %copy-done.1, bf16[128,2048]{1,0:T(8,128)(2,1)S(1)} %copy-done.3), custom_call_target="tpu_custom_call" | custom-call | tf_op jit(solution)/shard_map/pallas_call | solution.py:162
  111.0 14.8 %all-to-all-done.3.prior_ref = bf16[16,128,128]{2,1,0:T(8,128)(2,1)S(1)} async-done(((bf16[16,128,128]{2,1,0:T(8,128)(2,1)}), bf16[16,128,128]{2,1,0:T(8,128)(2,1)S(1)}, u32[]{:S(2)}, u32[]{:S(2)}) %all-to-all-start.3) | async-done | bytes 524320 | tf_op jit(solution)/shard_map/all_to_all | solution.py:182
  125.7 1.6 %shard_map.60.normed_ref = bf16[128,2048]{1,0:T(8,128)(2,1)S(1)} custom-call(bf16[16,128]{1,0:T(8,128)(2,1)S(1)} %bitcast.4, bf16[128,2048]{1,0:T(8,128)(2,1)S(1)} %copy-done.4, f32[128,2048]{1,0:T(8,128)S(1)} %shard_map.55.local_ref, bf16[16,128,128]{2,1,0:T(8,128)(2,1)S(1)} %all-to-all-done.3.prior_ref), custom_call_target="tpu_custom_call" | custom-call | tf_op jit(solution)/shard_map/pallas_call | solution.py:183
  127.4 0.0 all-gather.2.cloned.1.call-done
  127.4 4.6 %shard_map.61 = bf16[128,2048]{1,0:T(8,128)(2,1)} custom-call(bf16[128,2048]{1,0:T(8,128)(2,1)S(1)} %shard_map.60.normed_ref, bf16[16,16,8,2048]{3,2,1,0:T(8,128)(2,1)} %bitcast.5), custom_call_target="tpu_custom_call" | custom-call | tf_op jit(solution)/shard_map/pallas_call | solution.py:190
Async XLA Ops:
  6.5 101.9 %copy-start.6 = (bf16[128,16]{0,1:T(8,128)(2,1)S(1)}, bf16[128,16]{0,1:T(8,128)(2,1)}, u32[]{:S(2)}) copy-start(bf16[128,16]{0,1:T(8,128)(2,1)} %param.8) | copy-start | bytes 12292
  6.5 101.9 %copy-start.1 = (bf16[128,2048]{1,0:T(8,128)(2,1)S(1)}, bf16[128,2048]{1,0:T(8,128)(2,1)}, u32[]{:S(2)}) copy-start(bf16[128,2048]{1,0:T(8,128)(2,1)} %keys_ref.3) | copy-start | bytes 1572868
  6.5 101.9 %copy-start.3 = (bf16[128,2048]{1,0:T(8,128)(2,1)S(1)}, bf16[128,2048]{1,0:T(8,128)(2,1)}, u32[]{:S(2)}) copy-start(bf16[128,2048]{1,0:T(8,128)(2,1)} %values_ref.3) | copy-start | bytes 1572868
  6.5 101.9 %copy-start.4 = (bf16[128,2048]{1,0:T(8,128)(2,1)S(1)}, bf16[128,2048]{1,0:T(8,128)(2,1)}, u32[]{:S(2)}) copy-start(bf16[128,2048]{1,0:T(8,128)(2,1)} %queries_ref.3) | copy-start | bytes 1572868
  6.5 120.8 %all-gather.2.cloned.1.call-start = ((), (), s32[]{:S(2)}) async-start(), calls=%async_computation.5 | async-start | bytes 8912896 | tf_op jit(solution)/shard_map/all_gather | solution.py:156
  33.4 1.0 copy-start
  34.5 1.0 copy-start.2
  35.5 0.7 copy-start.5
  102.5 23.2 %all-to-all-start.3 = ((bf16[16,128,128]{2,1,0:T(8,128)(2,1)}), bf16[16,128,128]{2,1,0:T(8,128)(2,1)S(1)}, u32[]{:S(2)}, u32[]{:S(2)}) async-start(bf16[16,128,128]{2,1,0:T(8,128)(2,1)} %shard_map.59), calls=%async_computation.3 | async-start | bytes 1048576 | tf_op jit(solution)/shard_map/all_to_all | solution.py:182
Sparse Core Ops, SparseCore 0:
  33.6 73.5 all-gather.1

commit v2 on v1

--- a/solution.py
+++ b/solution.py
@@ -7,6 +7,7 @@
 
 HD = 128
 PAD = 8
+NEAR = 32
 BF16 = jnp.bfloat16
 F32 = jnp.float32
 VMEM = pltpu.CompilerParams(vmem_limit_bytes=40 * 1024 * 1024)
@@ -31,61 +32,63 @@
     return dot(ones_below(decay_t.shape[1]), decay_t, 1, 1)
 
 
+def parts_of(total):
+    row = lax.broadcasted_iota(jnp.int32, (PAD, HD), 0)
+    whole = jnp.broadcast_to(total, (PAD, HD))
+    high = whole.astype(BF16).astype(F32)
+    middle = (whole - high).astype(BF16).astype(F32)
+    low = whole - high - middle
+    parts = jnp.where(row == 0, high, jnp.where(row == 1, middle, jnp.where(row == 2, low, 0.0)))
+    return parts.astype(BF16)
+
+
+def total_of(ref, i):
+    parts = ref[i, ref.shape[1] - PAD :, :].astype(F32)
+    return parts[0:1, :] + parts[1:2, :] + parts[2:3, :]
+
+
 def states_kernel(decay_ref, keys_ref, values_ref, out_ref):
     heads, count = decay_ref.shape
+    pieces = out_ref.shape[0] // heads
+    rows = HD // pieces
     within = within_rows(decay_ref[...])
     total = within[:, count - 1 : count]
     coef = jnp.exp(total - within)
-    row = lax.broadcasted_iota(jnp.int32, (PAD, HD), 0)
     for h in range(heads):
         cols = slice(h * HD, (h + 1) * HD)
         keys_t = keys_ref[:, cols].astype(F32).T * coef[h : h + 1, :]
-        state = dot(keys_t.astype(BF16), values_ref[:, cols], 1, 0)
-        out_ref[h, :HD, :] = state.astype(BF16)
-        whole = jnp.broadcast_to(total[h : h + 1, :], (PAD, HD))
-        high = whole.astype(BF16).astype(F32)
-        middle = (whole - high).astype(BF16).astype(F32)
-        low = whole - high - middle
-        parts = jnp.where(row == 0, high, jnp.where(row == 1, middle, jnp.where(row == 2, low, 0.0)))
-        out_ref[h, HD:, :] = parts.astype(BF16)
-
-
-def total_of(ref, i):
-    parts = ref[i, HD:, :].astype(F32)
-    return parts[0:1, :] + parts[1:2, :] + parts[2:3, :]
-
-
-def group_kernel(group_ref, out_ref, work_ref):
-    chunks = out_ref.shape[0]
-    rows = HD // chunks
-    state = jnp.zeros((HD, HD), F32)
+        state = dot(keys_t.astype(BF16), values_ref[:, cols], 1, 0).astype(BF16)
+        parts = parts_of(total[h : h + 1, :])
+        for j in range(pieces):
+            out_ref[h * pieces + j, :rows, :] = state[rows * j : rows * (j + 1), :]
+            out_ref[h * pieces + j, rows:, :] = parts
+
+
+def group_kernel(group_ref, out_ref):
+    rows = group_ref.shape[1] - PAD
+    state = jnp.zeros((rows, HD), F32)
     total = jnp.zeros((1, HD), F32)
     for i in range(group_ref.shape[0]):
         step = total_of(group_ref, i)
-        state = jnp.exp(step) * state + group_ref[i, :HD, :].astype(F32)
+        state = jnp.exp(step) * state + group_ref[i, :rows, :].astype(F32)
         total = total + step
-    work_ref[...] = state
-    for j in range(chunks):
-        out_ref[j, :rows, :] = work_ref[rows * j : rows * (j + 1), :]
-        out_ref[j, rows:, :] = jnp.broadcast_to(total, (PAD - rows, HD))
-
-
-def scan_kernel(in_ref, out_ref):
+    state = state.astype(BF16)
+    parts = parts_of(total)
+    for j in range(out_ref.shape[0]):
+        out_ref[j, :rows, :] = state
+        out_ref[j, rows:, :] = parts
+
+
+def prior_kernel(place_ref, totals_ref, group_ref, out_ref):
     rows = out_ref.shape[1]
+    place = place_ref[0]
     state = jnp.zeros((rows, HD), F32)
-    for i in range(in_ref.shape[0]):
-        out_ref[i] = state
-        state = jnp.exp(in_ref[i, rows : rows + 1, :]) * state + in_ref[i, :rows, :]
-
-
-def prior_kernel(chunks_ref, group_ref, out_ref, work_ref):
-    chunks, rows, _ = chunks_ref.shape
-    for j in range(chunks):
-        work_ref[rows * j : rows * (j + 1), :] = chunks_ref[j]
-    state = work_ref[...]
+    for i in range(totals_ref.shape[0]):
+        later = jnp.exp(total_of(totals_ref, i)) * state + totals_ref[i, :rows, :].astype(F32)
+        state = jnp.where(i < place, later, state)
     for i in range(group_ref.shape[0]):
         out_ref[i] = state.astype(BF16)
-        state = jnp.exp(total_of(group_ref, i)) * state + group_ref[i, :HD, :].astype(F32)
+        state = jnp.exp(total_of(group_ref, i)) * state + group_ref[i, :rows, :].astype(F32)
 
 
 def local_kernel(decay_ref, queries_ref, keys_ref, values_ref, out_ref):
@@ -138,6 +141,12 @@
     out_ref[...] = acc.astype(BF16)
 
 
+def swap(x, within):
+    return lax.all_to_all(
+        x, ("seq", "head"), split_axis=0, concat_axis=0, axis_index_groups=within, tiled=True
+    )
+
+
 def shape(*dims, kind=F32):
     return jax.ShapeDtypeStruct(dims, kind)
 
@@ -148,6 +157,11 @@
     groups = lax.axis_size("seq")
     members = lax.axis_size("head")
     decay_t = log_decay.T
+    size = NEAR
+    rows = HD * heads // size
+    devices = groups * members
+    near = [list(range(i, i + size)) for i in range(0, devices, size)]
+    far = [list(range(i, devices, size)) for i in range(size)]
 
     weight_rows = out_weight.shape[0]
     spread = jnp.broadcast_to(out_weight[None], (groups, weight_rows, width))
@@ -156,37 +170,34 @@
     weight = lax.all_gather(spread, "head", axis=0, tiled=True)
 
     own = pl.pallas_call(
-        states_kernel, out_shape=shape(heads, HD + PAD, HD, kind=BF16), compiler_params=VMEM
+        states_kernel, out_shape=shape(size, rows + PAD, HD, kind=BF16), compiler_params=VMEM
     )(decay_t, keys, values)
-    group = lax.all_to_all(own, "head", split_axis=0, concat_axis=0, tiled=True)
+    group = swap(own, near)
     local_part = pl.pallas_call(
         local_kernel, out_shape=shape(count, width), compiler_params=VMEM
     )(decay_t, queries, keys, values)
-    chunks = pl.pallas_call(
+    totals = pl.pallas_call(
         group_kernel,
-        out_shape=shape(groups, PAD, HD),
-        scratch_shapes=[pltpu.VMEM((HD, HD), F32)],
+        out_shape=shape(len(far[0]), rows + PAD, HD, kind=BF16),
         compiler_params=VMEM,
     )(group)
-    chunks = lax.all_to_all(chunks, "seq", split_axis=0, concat_axis=0, tiled=True)
-    chunks = pl.pallas_call(
-        scan_kernel, out_shape=shape(groups, HD // groups, HD), compiler_params=VMEM
-    )(chunks)
-    chunks = lax.all_to_all(chunks, "seq", split_axis=0, concat_axis=0, tiled=True)
+    totals = swap(totals, far)
+    place = (lax.axis_index("seq") * members + lax.axis_index("head")) // size
+    vmem = pl.BlockSpec(memory_space=pltpu.VMEM)
     prior = pl.pallas_call(
         prior_kernel,
-        out_shape=shape(members, HD, HD, kind=BF16),
-        scratch_shapes=[pltpu.VMEM((HD, HD), F32)],
+        in_specs=[pl.BlockSpec(memory_space=pltpu.SMEM), vmem, vmem],
+        out_specs=vmem,
+        out_shape=shape(size, rows, HD, kind=BF16),
         compiler_params=VMEM,
-    )(chunks, group)
-    prior = lax.all_to_all(prior, "head", split_axis=0, concat_axis=0, tiled=True)
+    )(place.reshape(1), totals, group)
+    prior = swap(prior, near).reshape(heads, HD, HD)
     normed = pl.pallas_call(
         norm_kernel, out_shape=shape(count, width, kind=BF16), compiler_params=VMEM
     )(decay_t, queries, local_part, prior)
     runs = 2 * weight_rows
     weight = weight.reshape(members, groups // 2, runs, width)
     weight = pltpu.with_memory_space_constraint(weight, pltpu.HBM)
-    vmem = pl.BlockSpec(memory_space=pltpu.VMEM)
     return pl.pallas_call(
         project_kernel,
         out_shape=shape(count, width, kind=BF16),

time: 139 us -> 132 us (0.950)
  blocking collectives: 89.4 us -> 60.4 us
  waiting for transfers between devices: 14.8 us -> 30.2 us
  starting transfers between devices: 5.96 us -> 11.4 us
    all_to_all x3 -> x1, blocking collectives: 64.5 us -> 35.6 us  [swap(): lax.all_to_all(x, ('seq', 'head'), split_axis=0, concat_axis=0, axis_inde...]
    all_to_all x1 -> x2, waiting for transfers between devices: 14.8 us -> 28.4 us  [swap(): lax.all_to_all(x, ('seq', 'head'), split_axis=0, concat_axis=0, axis_inde...]
    all_to_all x1 -> x2, starting transfers between devices: 5.93 us -> 11.3 us  [swap(): lax.all_to_all(x, ('seq', 'head'), split_axis=0, concat_axis=0, axis_inde...]
    all_gather x1, waiting for transfers between devices: 0.02 us -> 1.81 us  [mix(): weight = lax.all_gather(spread, 'head', axis=0, tiled=True)]
  transfers between devices with their start and end apart: 2 -> 3, of which waited for: 1 -> 3; matrix products, arithmetic and copies ran while one was open for 0% -> 0% of each run, Pallas kernels for 4% -> 5%
where the time goes in v2:
time: 132 us
  blocking collectives  60.4 us (46%)
  waiting for transfers between devices  30.2 us (23%)
  between operations  13.5 us (10%)
  starting transfers between devices  11.4 us (9%)
  Pallas kernels  11.3 us (9%)
  local copies, waits for them, and re-layouts  4.79 us (4%)
    all_to_all x1, blocking collectives, swap(): lax.all_to_all(x, ('seq', 'head'), split_axis=0, concat_axis=0, axis_inde...  35.6 us
    all_to_all x2, waiting for transfers between devices, swap(): lax.all_to_all(x, ('seq', 'head'), split_axis=0, concat_axis=0, axis_inde...  28.4 us
    all_to_all x1, blocking collectives, mix(): lax.all_to_all(spread, 'seq', split_axis=0, concat_axis=0, tiled=True)  24.8 us
    all_to_all x2, starting transfers between devices, swap(): lax.all_to_all(x, ('seq', 'head'), split_axis=0, concat_axis=0, axis_inde...  11.3 us
    pallas_call x1, Pallas kernels, mix(): pl.pallas_call(project_kernel, out_shape=shape(count, width, kind=BF16),...  4.63 us
    unnamed x14, local copies, waits for them, and re-layouts  2.78 us
  transfers between devices with their start and end apart: 3, of which 3 were waited for; matrix products, arithmetic and copies ran while one was open for 0% of the time, Pallas kernels for 5%

profile of v2, /device:TPU:1, one launch (start us, length us, event | category | flops | bytes accessed | tf_op | source)
XLA Modules:
  0.0 131.6 jit_solution(7198986285611686917)
XLA Ops:
  6.5 0.0 copy-start.6
  6.5 0.0 copy-start.1
  6.5 0.0 copy-start.3
  6.5 0.0 copy-start.4
  6.5 0.0 all-gather.2.cloned.1.call-start
  6.6 1.1 broadcast_in_dim.2
  7.7 24.8 %all_to_all.20 = bf16[32,4,2048]{2,1,0:T(4,128)(2,1)S(1)} all-to-all(bf16[32,4,2048]{2,1,0:T(4,128)(2,1)S(1)} %broadcast_in_dim.2), channel_id=1, replica_groups=mesh['seq'=32,'head'=16] {'seq'}, dimensions={0} | all-to-all | bytes 1048576 | tf_op jit(solution)/shard_map/all_to_all | solution.py:168
  32.5 1.0 reshape.15
  33.4 0.0 all-gather.2.cloned.1.call-update
  33.4 0.0 copy-start
  33.5 1.0 copy-done
  34.5 0.0 copy-start.2
  34.5 1.0 copy-done.2
  35.5 0.0 copy-start.5
  35.5 0.7 copy-done.5
  36.2 0.6 shard_map.56
  36.8 35.6 %all_to_all.21.group_ref = bf16[32,72,128]{2,1,0:T(8,128)(2,1)S(1)} all-to-all(bf16[32,72,128]{2,1,0:T(8,128)(2,1)S(1)} %shard_map.56), channel_id=1, replica_groups={{0,1,2,3,4,5,6,7,8,9,10,11,12,13,14,15,16,17,18,19,20,21,22,23,24,25,26..., dimensions={0} | all-to-all | bytes 1179648 | tf_op jit(solution)/shard_map/all_to_all | solution.py:145
  72.4 0.9 shard_map.57
  73.3 3.5 %all-to-all-start.1 = ((bf16[16,72,128]{2,1,0:T(8,128)(2,1)}), bf16[16,72,128]{2,1,0:T(8,128)(2,1)S(1)}, u32[]{:S(2)}, u32[]{:S(2)}) async-start(bf16[16,72,128]{2,1,0:T(8,128)(2,1)} %shard_map.57), calls=%async_computation.1 | async-start | bytes 589824 | tf_op jit(solution)/shard_map/all_to_all | solution.py:145
  76.8 12.5 %all-to-all-done.1.totals_ref = bf16[16,72,128]{2,1,0:T(8,128)(2,1)S(1)} async-done(((bf16[16,72,128]{2,1,0:T(8,128)(2,1)}), bf16[16,72,128]{2,1,0:T(8,128)(2,1)S(1)}, u32[]{:S(2)}, u32[]{:S(2)}) %all-to-all-start.1) | async-done | bytes 294944 | tf_op jit(solution)/shard_map/all_to_all | solution.py:145
  89.3 1.0 shard_map.58
  90.3 7.8 %all-to-all-start.2 = ((bf16[32,64,128]{2,1,0:T(8,128)(2,1)}), bf16[32,64,128]{2,1,0:T(8,128)(2,1)S(1)}, u32[]{:S(2)}, u32[]{:S(2)}) async-start(bf16[32,64,128]{2,1,0:T(8,128)(2,1)} %shard_map.58), calls=%async_computation.2 | async-start | bytes 1048576 | tf_op jit(solution)/shard_map/all_to_all | solution.py:145
  98.1 0.0 copy-done.6
  98.1 0.0 copy-done.1
  98.2 0.0 copy-done.3
  98.2 0.0 copy-done.4
  98.2 2.5 %shard_map.55.local_ref = f32[128,2048]{1,0:T(8,128)S(1)} custom-call(bf16[16,128]{1,0:T(8,128)(2,1)S(1)} %bitcast.6, bf16[128,2048]{1,0:T(8,128)(2,1)S(1)} %copy-done.4, bf16[128,2048]{1,0:T(8,128)(2,1)S(1)} %copy-done.1, bf16[128,2048]{1,0:T(8,128)(2,1)S(1)} %copy-done.3), custom_call_target="tpu_custom_call" | custom-call | tf_op jit(solution)/shard_map/pallas_call | solution.py:176
  100.7 16.0 %all-to-all-done.2 = bf16[32,64,128]{2,1,0:T(8,128)(2,1)S(1)} async-done(((bf16[32,64,128]{2,1,0:T(8,128)(2,1)}), bf16[32,64,128]{2,1,0:T(8,128)(2,1)S(1)}, u32[]{:S(2)}, u32[]{:S(2)}) %all-to-all-start.2) | async-done | bytes 524320 | tf_op jit(solution)/shard_map/all_to_all | solution.py:145
  116.7 1.6 %shard_map.59.normed_ref = bf16[128,2048]{1,0:T(8,128)(2,1)S(1)} custom-call(bf16[16,128]{1,0:T(8,128)(2,1)S(1)} %bitcast.7, bf16[128,2048]{1,0:T(8,128)(2,1)S(1)} %copy-done.4, f32[128,2048]{1,0:T(8,128)S(1)} %shard_map.55.local_ref, bf16[16,128,128]{2,1,0:T(8,128)(2,1)S(1)} %bitcast.4), custom_call_target="tpu_custom_call" | custom-call | tf_op jit(solution)/shard_map/pallas_call | solution.py:195
  118.3 1.8 %all-gather.2.cloned.1.call-done = bf16[2048,2048]{1,0:T(8,128)(2,1)} async-done(((bf16[128,2048]{1,0:T(8,128)(2,1)}), bf16[2048,2048]{1,0:T(8,128)(2,1)}) %all-gather.2.cloned.1.call-update) | async-done | bytes 8388624 | tf_op jit(solution)/shard_map/all_gather | solution.py:170
  120.1 4.6 %shard_map.60 = bf16[128,2048]{1,0:T(8,128)(2,1)} custom-call(bf16[128,2048]{1,0:T(8,128)(2,1)S(1)} %shard_map.59.normed_ref, bf16[16,16,8,2048]{3,2,1,0:T(8,128)(2,1)} %bitcast.8), custom_call_target="tpu_custom_call" | custom-call | tf_op jit(solution)/shard_map/pallas_call | solution.py:201
Async XLA Ops:
  6.5 91.6 %copy-start.6 = (bf16[128,16]{0,1:T(8,128)(2,1)S(1)}, bf16[128,16]{0,1:T(8,128)(2,1)}, u32[]{:S(2)}) copy-start(bf16[128,16]{0,1:T(8,128)(2,1)} %param.8) | copy-start | bytes 12292
  6.5 91.6 %copy-start.1 = (bf16[128,2048]{1,0:T(8,128)(2,1)S(1)}, bf16[128,2048]{1,0:T(8,128)(2,1)}, u32[]{:S(2)}) copy-start(bf16[128,2048]{1,0:T(8,128)(2,1)} %keys_ref.3) | copy-start | bytes 1572868
  6.5 91.6 %copy-start.3 = (bf16[128,2048]{1,0:T(8,128)(2,1)S(1)}, bf16[128,2048]{1,0:T(8,128)(2,1)}, u32[]{:S(2)}) copy-start(bf16[128,2048]{1,0:T(8,128)(2,1)} %values_ref.3) | copy-start | bytes 1572868
  6.5 91.6 %copy-start.4 = (bf16[128,2048]{1,0:T(8,128)(2,1)S(1)}, bf16[128,2048]{1,0:T(8,128)(2,1)}, u32[]{:S(2)}) copy-start(bf16[128,2048]{1,0:T(8,128)(2,1)} %queries_ref.3) | copy-start | bytes 1572868
  6.5 113.6 %all-gather.2.cloned.1.call-start = ((), (), s32[]{:S(2)}) async-start(), calls=%async_computation.4 | async-start | bytes 8912896 | tf_op jit(solution)/shard_map/all_gather | solution.py:170
  33.4 1.0 copy-start
  34.5 1.0 copy-start.2
  35.5 0.7 copy-start.5
  73.3 16.0 %all-to-all-start.1 = ((bf16[16,72,128]{2,1,0:T(8,128)(2,1)}), bf16[16,72,128]{2,1,0:T(8,128)(2,1)S(1)}, u32[]{:S(2)}, u32[]{:S(2)}) async-start(bf16[16,72,128]{2,1,0:T(8,128)(2,1)} %shard_map.57), calls=%async_computation.1 | async-start | bytes 589824 | tf_op jit(solution)/shard_map/all_to_all | solution.py:145
  90.3 26.3 %all-to-all-start.2 = ((bf16[32,64,128]{2,1,0:T(8,128)(2,1)}), bf16[32,64,128]{2,1,0:T(8,128)(2,1)S(1)}, u32[]{:S(2)}, u32[]{:S(2)}) async-start(bf16[32,64,128]{2,1,0:T(8,128)(2,1)} %shard_map.58), calls=%async_computation.2 | async-start | bytes 1048576 | tf_op jit(solution)/shard_map/all_to_all | solution.py:145
Sparse Core Ops, SparseCore 0:
  33.6 86.4 all-gather.1

commit v3 on v2

v3 whole, which is shorter than its diff:
```python
import jax
import jax.numpy as jnp
from jax import lax
from jax.experimental import pallas as pl
from jax.experimental.pallas import tpu as pltpu
from jax.sharding import PartitionSpec as P

HD = 128
PAD = 8
NEAR = 16
BF16 = jnp.bfloat16
F32 = jnp.float32
VMEM = pltpu.CompilerParams(vmem_limit_bytes=40 * 1024 * 1024)


def ones_below(rows):
    return (
        lax.broadcasted_iota(jnp.int32, (rows, rows), 0)
        >= lax.broadcasted_iota(jnp.int32, (rows, rows), 1)
    ).astype(BF16)


def dot(a, b, ca, cb):
    return lax.dot_general(a, b, (((ca,), (cb,)), ((), ())), preferred_element_type=F32)


def within_rows(decay_t):
    return dot(decay_t, ones_below(decay_t.shape[1]), 1, 1)


def within_cols(decay_t):
    return dot(ones_below(decay_t.shape[1]), decay_t, 1, 1)


def parts_of(total):
    row = lax.broadcasted_iota(jnp.int32, (PAD, HD), 0)
    whole = jnp.broadcast_to(total, (PAD, HD))
    high = whole.astype(BF16).astype(F32)
    middle = (whole - high).astype(BF16).astype(F32)
    low = whole - high - middle
    parts = jnp.where(row == 0, high, jnp.where(row == 1, middle, jnp.where(row == 2, low, 0.0)))
    return parts.astype(BF16)


def total_of(ref, i):
    parts = ref[i, ref.shape[1] - PAD :, :].astype(F32)
    return parts[0:1, :] + parts[1:2, :] + parts[2:3, :]


def pack_kernel(core_ref, decay_ref, queries_ref, keys_ref, values_ref, own_ref, other_ref):
    first = core_ref[0] == 0
    half = (own_ref.shape[0] - 1) // 3
    for n, ref in enumerate((keys_ref, values_ref, queries_ref)):
        for h in range(half):
            low = ref[:, h * HD : (h + 1) * HD]
            high = ref[:, (half + h) * HD : (half + h + 1) * HD]
            own_ref[n * half + h] = jnp.where(first, low, high)
            other_ref[n * half + h] = jnp.where(first, high, low)
    low = decay_ref[:half, :].astype(F32)
    high = decay_ref[half:, :].astype(F32)
    rest = jnp.zeros((HD - half, HD), F32)
    kept = jnp.concatenate([jnp.where(first, low, high), rest], axis=0)
    sent = jnp.concatenate([jnp.where(first, high, low), rest], axis=0)
    own_ref[3 * half] = kept.astype(BF16)
    other_ref[3 * half] = sent.astype(BF16)


def both(first, own_ref, other_ref, i):
    own, other = own_ref[i], other_ref[i]
    return jnp.where(first, own, other), jnp.where(first, other, own)


def tokens(first, own_ref, other_ref, i):
    return jnp.concatenate(both(first, own_ref, other_ref, i), axis=0)


def decays(first, own_ref, other_ref):
    half = (own_ref.shape[0] - 1) // 3
    early, late = both(first, own_ref, other_ref, 3 * half)
    return jnp.concatenate([early[:half, :], late[:half, :]], axis=1)


def states_kernel(core_ref, own_ref, other_ref, out_ref):
    first = core_ref[0] == 0
    heads = (own_ref.shape[0] - 1) // 3
    pieces = out_ref.shape[0] // heads
    rows = HD // pieces
    decay_t = decays(first, own_ref, other_ref)
    count = decay_t.shape[1]
    within = within_rows(decay_t)
    total = within[:, count - 1 : count]
    coef = jnp.exp(total - within)
    for h in range(heads):
        keys_t = tokens(first, own_ref, other_ref, h).astype(F32).T * coef[h : h + 1, :]
        values = tokens(first, own_ref, other_ref, heads + h)
        state = dot(keys_t.astype(BF16), values, 1, 0).astype(BF16)
        parts = parts_of(total[h : h + 1, :])
        for j in range(pieces):
            out_ref[h * pieces + j, :rows, :] = state[rows * j : rows * (j + 1), :]
            out_ref[h * pieces + j, rows:, :] = parts


def group_kernel(group_ref, out_ref):
    rows = group_ref.shape[1] - PAD
    state = jnp.zeros((rows, HD), F32)
    total = jnp.zeros((1, HD), F32)
    for i in range(group_ref.shape[0]):
        step = total_of(group_ref, i)
        state = jnp.exp(step) * state + group_ref[i, :rows, :].astype(F32)
        total = total + step
    state = state.astype(BF16)
    parts = parts_of(total)
    for j in range(out_ref.shape[0]):
        out_ref[j, :rows, :] = state
        out_ref[j, rows:, :] = parts


def prior_kernel(place_ref, totals_ref, group_ref, out_ref):
    rows = out_ref.shape[1]
    place = place_ref[0]
    state = jnp.zeros((rows, HD), F32)
    for i in range(totals_ref.shape[0]):
        later = jnp.exp(total_of(totals_ref, i)) * state + totals_ref[i, :rows, :].astype(F32)
        state = jnp.where(i < place, later, state)
    for i in range(group_ref.shape[0]):
        out_ref[i] = state.astype(BF16)
        state = jnp.exp(total_of(group_ref, i)) * state + group_ref[i, :rows, :].astype(F32)


def local_kernel(core_ref, own_ref, other_ref, out_ref):
    first = core_ref[0] == 0
    heads, count, _ = out_ref.shape
    decay_t = decays(first, own_ref, other_ref)
    rows = within_rows(decay_t)
    cols = within_cols(decay_t)
    causal = lax.broadcasted_iota(jnp.int32, (count, count), 0) >= lax.broadcasted_iota(
        jnp.int32, (count, count), 1
    )
    for h in range(heads):
        keys = tokens(first, own_ref, other_ref, h)
        values = tokens(first, own_ref, other_ref, heads + h)
        queries = tokens(first, own_ref, other_ref, 2 * heads + h)
        scores = dot(queries, keys, 1, 1)
        gaps = cols[:, h : h + 1] - rows[h : h + 1, :]
        decay = jnp.exp(jnp.where(causal, gaps, -jnp.inf))
        weights = (scores * decay).astype(BF16)
        out_ref[h] = dot(weights, values, 1, 0)


def norm_kernel(core_ref, own_ref, other_ref, local_ref, prior_ref, keep_ref, send_ref):
    first = core_ref[0] == 0
    heads = local_ref.shape[0]
    count = keep_ref.shape[1]
    scale = jnp.exp(within_cols(decays(first, own_ref, other_ref)))
    place = lax.broadcasted_iota(jnp.int32, (HD, HD), 1)
    source = lax.broadcasted_iota(jnp.int32, (HD, HD), 0)
    wanted = (place // 4 % 2) * (HD // 2) + (place // 8) * 4 + place % 4
    reorder = (source == wanted).astype(BF16)
    for h in range(heads):
        queries = tokens(first, own_ref, other_ref, 2 * heads + h)
        carried = dot(queries, prior_ref[h], 1, 0) * scale[:, h : h + 1]
        combined = local_ref[h] + carried
        square = jnp.mean(combined * combined, axis=-1, keepdims=True)
        normed = (combined * lax.rsqrt(square + 1e-05)).astype(BF16)
        normed = dot(normed, reorder, 1, 0).astype(BF16)
        keep_ref[h] = jnp.where(first, normed[:count], normed[count:])
        send_ref[h] = jnp.where(first, normed[count:], normed[:count])


def project_kernel(core_ref, kept_ref, got_ref, weight_ref, out_ref, rows_ref, sems):
    first = core_ref[0] == 0
    heads = weight_ref.shape[1]
    half = heads // 2

    def copy(h):
        return pltpu.make_async_copy(weight_ref.at[:, h], rows_ref.at[h], sems.at[h])

    def normed(h):
        low, high = both(first, kept_ref, got_ref, h % half)
        return low if h < half else high

    for h in range(heads):
        copy(h).start()
    acc = jnp.zeros(out_ref.shape, F32)
    for h in range(0, heads, 2):
        copy(h).wait()
        copy(h + 1).wait()
        rows = rows_ref[h : h + 2].reshape(2 * HD, out_ref.shape[1])
        acc = acc + dot(jnp.concatenate([normed(h), normed(h + 1)], axis=1), rows, 1, 0)
    out_ref[...] = acc.astype(BF16)


def swap(x, within):
    return lax.all_to_all(
        x, ("seq", "head"), split_axis=0, concat_axis=0, axis_index_groups=within, tiled=True
    )


def shape(*dims, kind=F32):
    return jax.ShapeDtypeStruct(dims, kind)


def call(kernel, out, *args, **options):
    vmem = pl.BlockSpec(memory_space=pltpu.VMEM)
    smem = pl.BlockSpec(memory_space=pltpu.SMEM)
    return pl.pallas_call(
        kernel,
        out_shape=out,
        in_specs=[smem] + [vmem] * (len(args) - 1),
        out_specs=jax.tree.map(lambda _: vmem, out),
        compiler_params=VMEM,
        **options,
    )(*args)


def mix(queries, keys, values, log_decay, out_weight):
    count, width = queries.shape
    heads = log_decay.shape[1]
    half = heads // 2
    groups = lax.axis_size("seq")
    members = lax.axis_size("head")
    decay_t = log_decay.T
    devices = groups * members
    size = 2 * NEAR
    rows = HD * half // NEAR
    near = [list(range(i + c, i + size, 2)) for i in range(0, devices, size) for c in range(2)]
    far = [list(range(i, devices, size)) for i in range(size)]
    partner = [(i, i ^ 1) for i in range(members)]
    core = (lax.axis_index("head") & 1).reshape(1)
    place = (lax.axis_index("seq") // (size // members)).reshape(1)

    weight_rows = out_weight.shape[0]
    spread = jnp.broadcast_to(out_weight[None], (groups, weight_rows, width))
    spread = lax.all_to_all(spread, "seq", split_axis=0, concat_axis=0, tiled=True)
    spread = spread.reshape(groups * weight_rows, width)
    weight = lax.all_gather(spread, "head", axis=0, tiled=True)

    pair = shape(3 * half + 1, count, HD, kind=BF16)
    own, other = call(pack_kernel, (pair, pair), core, decay_t, queries, keys, values)
    other = lax.ppermute(other, "head", partner)
    states = call(states_kernel, shape(NEAR, rows + PAD, HD, kind=BF16), core, own, other)
    local_part = call(local_kernel, shape(half, 2 * count, HD), core, own, other)
    group = swap(states, near)
    totals = pl.pallas_call(
        group_kernel,
        out_shape=shape(len(far[0]), rows + PAD, HD, kind=BF16),
        compiler_params=VMEM,
    )(group)
    totals = swap(totals, far)
    prior = call(prior_kernel, shape(NEAR, rows, HD, kind=BF16), place, totals, group)
    prior = swap(prior, near).reshape(half, HD, HD)
    normed = shape(half, count, HD, kind=BF16)
    kept, sent = call(norm_kernel, (normed, normed), core, own, other, local_part, prior)
    got = lax.ppermute(sent, "head", partner)
    weight = weight.reshape(members, groups // 2, 2 * weight_rows, width)
    weight = pltpu.with_memory_space_constraint(weight, pltpu.HBM)
    vmem = pl.BlockSpec(memory_space=pltpu.VMEM)
    return pl.pallas_call(
        project_kernel,
        out_shape=shape(count, width, kind=BF16),
        in_specs=[
            pl.BlockSpec(memory_space=pltpu.SMEM),
            vmem,
            vmem,
            pl.BlockSpec(memory_space=pltpu.HBM),
        ],
        out_specs=vmem,
        scratch_shapes=[
            pltpu.VMEM((heads, members, 2 * weight_rows, width), BF16),
            pltpu.SemaphoreType.DMA((heads,)),
        ],
        compiler_params=VMEM,
    )(core, kept, got, weight)


def solution(mesh):
    placed = P(("seq", "head"), None)
    return jax.shard_map(mix, mesh=mesh, in_specs=(placed,) * 5, out_specs=placed, check_vma=False)
```

time: 132 us -> 122 us (0.924)
  blocking collectives: 60.4 us -> 47.2 us
  starting transfers between devices: 11.4 us -> 21 us
  waiting for transfers between devices: 30.2 us -> 24.2 us
  Pallas kernels: 11.3 us -> 9.35 us
    all_to_all x1, blocking collectives: 35.6 us -> 22.4 us  [swap(): lax.all_to_all(x, ('seq', 'head'), split_axis=0, concat_axis=0, axis_inde...]
    ppermute x0 -> x2, starting transfers between devices: none -> 10 us  [the longest x1 5.04 us: mix(): other = lax.ppermute(other, 'head', partner)]
    all_to_all x2, waiting for transfers between devices: 28.4 us -> 21.2 us  [swap(): lax.all_to_all(x, ('seq', 'head'), split_axis=0, concat_axis=0, axis_inde...]
    ppermute x0 -> x2, waiting for transfers between devices: none -> 3.08 us  [the longest x1 1.94 us: mix(): other = lax.ppermute(other, 'head', partner)]
    pallas_call x4 -> x5, Pallas kernels: 5.75 us -> 3.91 us  [call(): pl.pallas_call(kernel, out_shape=out, in_specs=[smem] + [vmem] * (len(arg...]
    all_gather x1, waiting for transfers between devices: 1.81 us -> 0.01 us  [mix(): weight = lax.all_gather(spread, 'head', axis=0, tiled=True)]
    unnamed x14 -> x8, local copies, waits for them, and re-layouts: 2.78 us -> 3.81 us
  transfers between devices with their start and end apart: 3 -> 5, of which waited for: 3 -> 4; matrix products, arithmetic and copies ran while one was open for 0% -> 0% of each run, Pallas kernels for 5% -> 4%
where the time goes in v3:
time: 122 us; the launch traced here: 121 us
  blocking collectives  47.2 us (39%)
  waiting for transfers between devices  24.2 us (20%)
  starting transfers between devices  21 us (17%)
  between operations  13.5 us (11%)
  Pallas kernels  9.35 us (8%)
  local copies, waits for them, and re-layouts  5.66 us (5%)
    all_to_all x1, blocking collectives, mix(): lax.all_to_all(spread, 'seq', split_axis=0, concat_axis=0, tiled=True)  24.8 us
    all_to_all x1, blocking collectives, swap(): lax.all_to_all(x, ('seq', 'head'), split_axis=0, concat_axis=0, axis_inde...  22.4 us
    all_to_all x2, waiting for transfers between devices, swap(): lax.all_to_all(x, ('seq', 'head'), split_axis=0, concat_axis=0, axis_inde...  21.2 us
    all_to_all x2, starting transfers between devices, swap(): lax.all_to_all(x, ('seq', 'head'), split_axis=0, concat_axis=0, axis_inde...  11 us
    ppermute x1, starting transfers between devices, mix(): other = lax.ppermute(other, 'head', partner)  5.04 us
    ppermute x1, starting transfers between devices, mix(): got = lax.ppermute(sent, 'head', partner)  4.98 us
    pallas_call x1, Pallas kernels, mix(): pl.pallas_call(project_kernel, out_shape=shape(count, width, kind=BF16),...  4.63 us
    pallas_call x5, Pallas kernels, call(): pl.pallas_call(kernel, out_shape=out, in_specs=[smem] + [vmem] * (len(arg...  3.91 us
  transfers between devices with their start and end apart: 5, of which 4 were waited for; matrix products, arithmetic and copies ran while one was open for 0% of the time, Pallas kernels for 4%

profile of v3, /device:TPU:1, one launch (start us, length us, event | category | flops | bytes accessed | tf_op | source)
XLA Modules:
  0.0 121.1 jit_solution(13307571354168117422)
XLA Ops:
  6.5 0.0 all-gather.2.cloned.1.call-start
  6.5 0.9 broadcast_in_dim.2
  7.5 24.8 %all_to_all.20 = bf16[32,4,2048]{2,1,0:T(4,128)(2,1)S(1)} all-to-all(bf16[32,4,2048]{2,1,0:T(4,128)(2,1)S(1)} %broadcast_in_dim.2), channel_id=1, replica_groups=mesh['seq'=32,'head'=16] {'seq'}, dimensions={0} | all-to-all | bytes 1048576 | tf_op jit(solution)/shard_map/all_to_all | solution.py:234
  32.3 0.9 reshape.19
  33.2 0.0 all-gather.2.cloned.1.call-update
  33.3 0.0 copy-start
  33.3 1.0 copy-done
  34.3 0.0 copy-start.1
  34.3 1.0 copy-done.1
  35.3 0.0 copy-start.2
  35.3 1.0 copy-done.2
  36.4 0.0 copy-start.3
  36.4 0.7 copy-done.3
  37.1 0.3 shard_map.55
  37.4 5.0 %collective-permute-start = (bf16[25,128,128]{2,1,0:T(8,128)(2,1)S(1)}, bf16[25,128,128]{2,1,0:T(8,128)(2,1)S(1)}, u32[]{:S(2)}, u32[]{:S(2)}) collective-permute-start(bf16[25,128,128]{2,1,0:T(8,128)(2,1)S(1)} %get-tuple-element.10), channel_id=1, source_target_pairs={{0,1},{1,0},{2,3},{3,2},{4,5},{5,4},{6,7},{7,6},{8,9},{9,8},{10,11... | collective-permute-start | bytes 2457608 | tf_op jit(solution)/shard_map/ppermute | solution.py:240
  42.4 1.9 %collective-permute-done.other_ref = bf16[25,128,128]{2,1,0:T(8,128)(2,1)S(1)} collective-permute-done((bf16[25,128,128]{2,1,0:T(8,128)(2,1)S(1)}, bf16[25,128,128]{2,1,0:T(8,128)(2,1)S(1)}, u32[]{:S(2)}, u32[]{:S(2)}) %collective-permute-start) | collective-permute-done | bytes 819232 | tf_op jit(solution)/shard_map/ppermute | solution.py:240
  44.3 0.6 shard_map.57
  44.9 22.4 %all_to_all.21.group_ref = bf16[16,72,128]{2,1,0:T(8,128)(2,1)S(1)} all-to-all(bf16[16,72,128]{2,1,0:T(8,128)(2,1)S(1)} %shard_map.57), channel_id=1, replica_groups={{0,2,4,6,8,10,12,14,16,18,20,22,24,26,28,30},{1,3,5,7,9,11,13,15,17,19,..., dimensions={0} | all-to-all | bytes 589824 | tf_op jit(solution)/shard_map/all_to_all | solution.py:194
  67.4 0.8 shard_map.58
  68.2 3.5 %all-to-all-start.1 = ((bf16[16,72,128]{2,1,0:T(8,128)(2,1)}), bf16[16,72,128]{2,1,0:T(8,128)(2,1)S(1)}, u32[]{:S(2)}, u32[]{:S(2)}) async-start(bf16[16,72,128]{2,1,0:T(8,128)(2,1)} %shard_map.58), calls=%async_computation.1 | async-start | bytes 589824 | tf_op jit(solution)/shard_map/all_to_all | solution.py:194
  71.7 12.6 %all-to-all-done.1.totals_ref = bf16[16,72,128]{2,1,0:T(8,128)(2,1)S(1)} async-done(((bf16[16,72,128]{2,1,0:T(8,128)(2,1)}), bf16[16,72,128]{2,1,0:T(8,128)(2,1)S(1)}, u32[]{:S(2)}, u32[]{:S(2)}) %all-to-all-start.1) | async-done | bytes 294944 | tf_op jit(solution)/shard_map/all_to_all | solution.py:194
  84.3 0.9 shard_map.59
  85.2 7.5 %all-to-all-start.2 = ((bf16[16,64,128]{2,1,0:T(8,128)(2,1)}), bf16[16,64,128]{2,1,0:T(8,128)(2,1)S(1)}, u32[]{:S(2)}, u32[]{:S(2)}) async-start(bf16[16,64,128]{2,1,0:T(8,128)(2,1)} %shard_map.59), calls=%async_computation.2 | async-start | bytes 524288 | tf_op jit(solution)/shard_map/all_to_all | solution.py:194
  92.7 0.9 shard_map.56.local_ref
  93.6 8.6 %all-to-all-done.2 = bf16[16,64,128]{2,1,0:T(8,128)(2,1)S(1)} async-done(((bf16[16,64,128]{2,1,0:T(8,128)(2,1)}), bf16[16,64,128]{2,1,0:T(8,128)(2,1)S(1)}, u32[]{:S(2)}, u32[]{:S(2)}) %all-to-all-start.2) | async-done | bytes 262176 | tf_op jit(solution)/shard_map/all_to_all | solution.py:194
  102.2 1.3 %shard_map.60 = (bf16[8,128,128]{2,1,0:T(8,128)(2,1)S(1)}, bf16[8,128,128]{2,1,0:T(8,128)(2,1)S(1)}) custom-call(s32[1]{0:T(128)} %bitcast.core_ref, bf16[25,128,128]{2,1,0:T(8,128)(2,1)S(1)} %get-tuple-element.9.own_ref, bf16[25,128,128]{2,1,0:T(8,128)(2,1)S(1)} %collective-permute-done.other_ref, f32[8,256,128]{2,1,0:T(8,128)S(1)} %shard_map.56.local_ref, ...), custom_call_target="tpu_custom_call" | custom-call | tf_op jit(solution)/shard_map/pallas_call | solution.py:206
  103.4 5.0 %collective-permute-start.1 = (bf16[8,128,128]{2,1,0:T(8,128)(2,1)S(1)}, bf16[8,128,128]{2,1,0:T(8,128)(2,1)S(1)}, u32[]{:S(2)}, u32[]{:S(2)}) collective-permute-start(bf16[8,128,128]{2,1,0:T(8,128)(2,1)S(1)} %get-tuple-element.12), channel_id=1, source_target_pairs={{0,1},{1,0},{2,3},{3,2},{4,5},{5,4},{6,7},{7,6},{8,9},{9,8},{10,11... | collective-permute-start | bytes 786440 | tf_op jit(solution)/shard_map/ppermute | solution.py:254
  108.4 1.1 collective-permute-done.1.got_ref
  109.6 0.0 all-gather.2.cloned.1.call-done
  109.6 4.6 %shard_map.61 = bf16[128,2048]{1,0:T(8,128)(2,1)} custom-call(s32[1]{0:T(128)} %bitcast.core_ref, bf16[8,128,128]{2,1,0:T(8,128)(2,1)S(1)} %get-tuple-element.11.kept_ref, bf16[8,128,128]{2,1,0:T(8,128)(2,1)S(1)} %collective-permute-done.1.got_ref, bf16[16,16,8,2048]{3,2,1,0:T(8,128)(2,1)} %bitcast.7), custom_call_target="tpu_custom_call" | custom-call | tf_op jit(solution)/shard_map/pallas_call | solution.py:258
Async XLA Ops:
  6.5 103.0 %all-gather.2.cloned.1.call-start = ((), (), s32[]{:S(2)}) async-start(), calls=%async_computation.4 | async-start | bytes 8912896 | tf_op jit(solution)/shard_map/all_gather | solution.py:236
  33.3 1.0 copy-start
  34.3 1.0 copy-start.1
  35.3 1.0 copy-start.2
  36.4 0.7 copy-start.3
  37.4 7.0 %collective-permute-start = (bf16[25,128,128]{2,1,0:T(8,128)(2,1)S(1)}, bf16[25,128,128]{2,1,0:T(8,128)(2,1)S(1)}, u32[]{:S(2)}, u32[]{:S(2)}) collective-permute-start(bf16[25,128,128]{2,1,0:T(8,128)(2,1)S(1)} %get-tuple-element.10), channel_id=1, source_target_pairs={{0,1},{1,0},{2,3},{3,2},{4,5},{5,4},{6,7},{7,6},{8,9},{9,8},{10,11... | collective-permute-start | bytes 2457608 | tf_op jit(solution)/shard_map/ppermute | solution.py:240
  68.2 16.1 %all-to-all-start.1 = ((bf16[16,72,128]{2,1,0:T(8,128)(2,1)}), bf16[16,72,128]{2,1,0:T(8,128)(2,1)S(1)}, u32[]{:S(2)}, u32[]{:S(2)}) async-start(bf16[16,72,128]{2,1,0:T(8,128)(2,1)} %shard_map.58), calls=%async_computation.1 | async-start | bytes 589824 | tf_op jit(solution)/shard_map/all_to_all | solution.py:194
  85.2 16.9 %all-to-all-start.2 = ((bf16[16,64,128]{2,1,0:T(8,128)(2,1)}), bf16[16,64,128]{2,1,0:T(8,128)(2,1)S(1)}, u32[]{:S(2)}, u32[]{:S(2)}) async-start(bf16[16,64,128]{2,1,0:T(8,128)(2,1)} %shard_map.59), calls=%async_computation.2 | async-start | bytes 524288 | tf_op jit(solution)/shard_map/all_to_all | solution.py:194
  103.4 6.1 %collective-permute-start.1 = (bf16[8,128,128]{2,1,0:T(8,128)(2,1)S(1)}, bf16[8,128,128]{2,1,0:T(8,128)(2,1)S(1)}, u32[]{:S(2)}, u32[]{:S(2)}) collective-permute-start(bf16[8,128,128]{2,1,0:T(8,128)(2,1)S(1)} %get-tuple-element.12), channel_id=1, source_target_pairs={{0,1},{1,0},{2,3},{3,2},{4,5},{5,4},{6,7},{7,6},{8,9},{9,8},{10,11... | collective-permute-start | bytes 786440 | tf_op jit(solution)/shard_map/ppermute | solution.py:254
Sparse Core Ops, SparseCore 0:
  33.4 74.5 all-gather.1

commit v4 on v3

--- a/solution.py
+++ b/solution.py
@@ -8,9 +8,11 @@
 HD = 128
 PAD = 8
 NEAR = 16
+RUN = 4
 BF16 = jnp.bfloat16
 F32 = jnp.float32
-VMEM = pltpu.CompilerParams(vmem_limit_bytes=40 * 1024 * 1024)
+VMEM = pltpu.CompilerParams(vmem_limit_bytes=12 * 1024 * 1024)
+LARGE = pltpu.CompilerParams(vmem_limit_bytes=20 * 1024 * 1024)
 
 
 def ones_below(rows):
@@ -45,6 +47,17 @@
 def total_of(ref, i):
     parts = ref[i, ref.shape[1] - PAD :, :].astype(F32)
     return parts[0:1, :] + parts[1:2, :] + parts[2:3, :]
+
+
+def spread_kernel(weight_ref, out_ref):
+    for i in range(out_ref.shape[0]):
+        out_ref[i] = weight_ref[...]
+
+
+def merge_kernel(in_ref, out_ref):
+    for i in range(0, in_ref.shape[0], 2):
+        pair = jnp.concatenate([in_ref[i], in_ref[i + 1]], axis=0)
+        out_ref[4 * i : 4 * i + 8, :] = pair
 
 
 def pack_kernel(core_ref, decay_ref, queries_ref, keys_ref, values_ref, own_ref, other_ref):
@@ -182,11 +195,12 @@
     for h in range(heads):
         copy(h).start()
     acc = jnp.zeros(out_ref.shape, F32)
-    for h in range(0, heads, 2):
-        copy(h).wait()
-        copy(h + 1).wait()
-        rows = rows_ref[h : h + 2].reshape(2 * HD, out_ref.shape[1])
-        acc = acc + dot(jnp.concatenate([normed(h), normed(h + 1)], axis=1), rows, 1, 0)
+    for h in range(0, heads, RUN):
+        run = range(h, h + RUN)
+        for i in run:
+            copy(i).wait()
+        rows = rows_ref[h : h + RUN].reshape(RUN * HD, out_ref.shape[1])
+        acc = acc + dot(jnp.concatenate([normed(i) for i in run], axis=1), rows, 1, 0)
     out_ref[...] = acc.astype(BF16)
 
 
@@ -230,9 +244,13 @@
     place = (lax.axis_index("seq") // (size // members)).reshape(1)
 
     weight_rows = out_weight.shape[0]
-    spread = jnp.broadcast_to(out_weight[None], (groups, weight_rows, width))
+    spread = pl.pallas_call(
+        spread_kernel, out_shape=shape(groups, weight_rows, width, kind=BF16), compiler_params=VMEM
+    )(out_weight)
     spread = lax.all_to_all(spread, "seq", split_axis=0, concat_axis=0, tiled=True)
-    spread = spread.reshape(groups * weight_rows, width)
+    spread = pl.pallas_call(
+        merge_kernel, out_shape=shape(groups * weight_rows, width, kind=BF16), compiler_params=VMEM
+    )(spread)
     weight = lax.all_gather(spread, "head", axis=0, tiled=True)
 
     pair = shape(3 * half + 1, count, HD, kind=BF16)
@@ -269,7 +287,7 @@
             pltpu.VMEM((heads, members, 2 * weight_rows, width), BF16),
             pltpu.SemaphoreType.DMA((heads,)),
         ],
-        compiler_params=VMEM,
+        compiler_params=LARGE,
     )(core, kept, got, weight)
 
 

time: 122 us -> 122 us (level)
    unnamed x8 -> x10, local copies, waits for them, and re-layouts: 3.81 us -> 4.52 us
where the time goes in v4:
time: 122 us; the launch traced here: 121 us
  blocking collectives  47.2 us (39%)
  waiting for transfers between devices  24.2 us (20%)
  starting transfers between devices  21 us (17%)
  between operations  13.5 us (11%)
  Pallas kernels  10.4 us (9%)
  local copies, waits for them, and re-layouts  4.52 us (4%)
    all_to_all x1, blocking collectives, mix(): lax.all_to_all(spread, 'seq', split_axis=0, concat_axis=0, tiled=True)  24.8 us
    all_to_all x1, blocking collectives, swap(): lax.all_to_all(x, ('seq', 'head'), split_axis=0, concat_axis=0, axis_inde...  22.4 us
    all_to_all x2, waiting for transfers between devices, swap(): lax.all_to_all(x, ('seq', 'head'), split_axis=0, concat_axis=0, axis_inde...  21.2 us
    all_to_all x2, starting transfers between devices, swap(): lax.all_to_all(x, ('seq', 'head'), split_axis=0, concat_axis=0, axis_inde...  11 us
    ppermute x1, starting transfers between devices, mix(): other = lax.ppermute(other, 'head', partner)  5.04 us
    ppermute x1, starting transfers between devices, mix(): got = lax.ppermute(sent, 'head', partner)  4.97 us
    pallas_call x1, Pallas kernels, mix(): pl.pallas_call(project_kernel, out_shape=shape(count, width, kind=BF16),...  4.77 us
    unnamed x10, local copies, waits for them, and re-layouts  4.52 us
  transfers between devices with their start and end apart: 5, of which 4 were waited for; matrix products, arithmetic and copies ran while one was open for 0% of the time, Pallas kernels for 4%

profile of v4, /device:TPU:1, one launch (start us, length us, event | category | flops | bytes accessed | tf_op | source)
XLA Modules:
  0.0 121.0 jit_solution(12934771315339184662)
XLA Ops:
  6.5 0.0 all-gather.2.cloned.1.call-start
  6.5 0.0 copy-start.3
  6.5 0.7 copy-done.3
  7.3 24.8 %all_to_all.20.in_ref = bf16[32,4,2048]{2,1,0:T(4,128)(2,1)S(1)} all-to-all(bf16[32,4,2048]{2,1,0:T(4,128)(2,1)S(1)} %shard_map.61), channel_id=1, replica_groups=mesh['seq'=32,'head'=16] {'seq'}, dimensions={0} | all-to-all | bytes 1048576 | tf_op jit(solution)/shard_map/all_to_all | solution.py:250
  32.1 0.9 shard_map.62
  33.0 0.0 all-gather.2.cloned.1.call-update
  33.1 0.0 copy-start
  33.1 1.0 copy-done
  34.1 0.0 copy-start.1
  34.1 1.0 copy-done.1
  35.2 0.0 copy-start.2
  35.2 1.0 copy-done.2
  36.2 0.0 copy-start.4
  36.2 0.7 copy-done.4
  36.9 0.3 shard_map.55
  37.2 5.0 %collective-permute-start = (bf16[25,128,128]{2,1,0:T(8,128)(2,1)S(1)}, bf16[25,128,128]{2,1,0:T(8,128)(2,1)S(1)}, u32[]{:S(2)}, u32[]{:S(2)}) collective-permute-start(bf16[25,128,128]{2,1,0:T(8,128)(2,1)S(1)} %get-tuple-element.10), channel_id=1, source_target_pairs={{0,1},{1,0},{2,3},{3,2},{4,5},{5,4},{6,7},{7,6},{8,9},{9,8},{10,11... | collective-permute-start | bytes 2457608 | tf_op jit(solution)/shard_map/ppermute | solution.py:258
  42.2 1.9 %collective-permute-done.other_ref = bf16[25,128,128]{2,1,0:T(8,128)(2,1)S(1)} collective-permute-done((bf16[25,128,128]{2,1,0:T(8,128)(2,1)S(1)}, bf16[25,128,128]{2,1,0:T(8,128)(2,1)S(1)}, u32[]{:S(2)}, u32[]{:S(2)}) %collective-permute-start) | collective-permute-done | bytes 819232 | tf_op jit(solution)/shard_map/ppermute | solution.py:258
  44.2 0.6 shard_map.57
  44.8 22.4 %all_to_all.21.group_ref = bf16[16,72,128]{2,1,0:T(8,128)(2,1)S(1)} all-to-all(bf16[16,72,128]{2,1,0:T(8,128)(2,1)S(1)} %shard_map.57), channel_id=1, replica_groups={{0,2,4,6,8,10,12,14,16,18,20,22,24,26,28,30},{1,3,5,7,9,11,13,15,17,19,..., dimensions={0} | all-to-all | bytes 589824 | tf_op jit(solution)/shard_map/all_to_all | solution.py:208
  67.2 0.8 shard_map.58
  68.0 3.5 %all-to-all-start.1 = ((bf16[16,72,128]{2,1,0:T(8,128)(2,1)}), bf16[16,72,128]{2,1,0:T(8,128)(2,1)S(1)}, u32[]{:S(2)}, u32[]{:S(2)}) async-start(bf16[16,72,128]{2,1,0:T(8,128)(2,1)} %shard_map.58), calls=%async_computation.1 | async-start | bytes 589824 | tf_op jit(solution)/shard_map/all_to_all | solution.py:208
  71.6 12.6 %all-to-all-done.1.totals_ref = bf16[16,72,128]{2,1,0:T(8,128)(2,1)S(1)} async-done(((bf16[16,72,128]{2,1,0:T(8,128)(2,1)}), bf16[16,72,128]{2,1,0:T(8,128)(2,1)S(1)}, u32[]{:S(2)}, u32[]{:S(2)}) %all-to-all-start.1) | async-done | bytes 294944 | tf_op jit(solution)/shard_map/all_to_all | solution.py:208
  84.2 0.9 shard_map.59
  85.0 7.5 %all-to-all-start.2 = ((bf16[16,64,128]{2,1,0:T(8,128)(2,1)}), bf16[16,64,128]{2,1,0:T(8,128)(2,1)S(1)}, u32[]{:S(2)}, u32[]{:S(2)}) async-start(bf16[16,64,128]{2,1,0:T(8,128)(2,1)} %shard_map.59), calls=%async_computation.2 | async-start | bytes 524288 | tf_op jit(solution)/shard_map/all_to_all | solution.py:208
  92.5 0.9 shard_map.56.local_ref
  93.4 8.6 %all-to-all-done.2 = bf16[16,64,128]{2,1,0:T(8,128)(2,1)S(1)} async-done(((bf16[16,64,128]{2,1,0:T(8,128)(2,1)}), bf16[16,64,128]{2,1,0:T(8,128)(2,1)S(1)}, u32[]{:S(2)}, u32[]{:S(2)}) %all-to-all-start.2) | async-done | bytes 262176 | tf_op jit(solution)/shard_map/all_to_all | solution.py:208
  102.0 1.3 %shard_map.60 = (bf16[8,128,128]{2,1,0:T(8,128)(2,1)S(1)}, bf16[8,128,128]{2,1,0:T(8,128)(2,1)S(1)}) custom-call(s32[1]{0:T(128)} %bitcast.core_ref, bf16[25,128,128]{2,1,0:T(8,128)(2,1)S(1)} %get-tuple-element.9.own_ref, bf16[25,128,128]{2,1,0:T(8,128)(2,1)S(1)} %collective-permute-done.other_ref, f32[8,256,128]{2,1,0:T(8,128)S(1)} %shard_map.56.local_ref, ...), custom_call_target="tpu_custom_call" | custom-call | tf_op jit(solution)/shard_map/pallas_call | solution.py:220
  103.2 5.0 %collective-permute-start.1 = (bf16[8,128,128]{2,1,0:T(8,128)(2,1)S(1)}, bf16[8,128,128]{2,1,0:T(8,128)(2,1)S(1)}, u32[]{:S(2)}, u32[]{:S(2)}) collective-permute-start(bf16[8,128,128]{2,1,0:T(8,128)(2,1)S(1)} %get-tuple-element.12), channel_id=1, source_target_pairs={{0,1},{1,0},{2,3},{3,2},{4,5},{5,4},{6,7},{7,6},{8,9},{9,8},{10,11... | collective-permute-start | bytes 786440 | tf_op jit(solution)/shard_map/ppermute | solution.py:272
  108.2 1.1 collective-permute-done.1.got_ref
  109.4 0.0 all-gather.2.cloned.1.call-done
  109.4 4.8 %shard_map.63 = bf16[128,2048]{1,0:T(8,128)(2,1)} custom-call(s32[1]{0:T(128)} %bitcast.core_ref, bf16[8,128,128]{2,1,0:T(8,128)(2,1)S(1)} %get-tuple-element.11.kept_ref, bf16[8,128,128]{2,1,0:T(8,128)(2,1)S(1)} %collective-permute-done.1.got_ref, bf16[16,16,8,2048]{3,2,1,0:T(8,128)(2,1)} %bitcast.7), custom_call_target="tpu_custom_call" | custom-call | tf_op jit(solution)/shard_map/pallas_call | solution.py:276
  (1 shorter events, 0.0 us)
Async XLA Ops:
  6.5 102.8 %all-gather.2.cloned.1.call-start = ((), (), s32[]{:S(2)}) async-start(), calls=%async_computation.4 | async-start | bytes 8912896 | tf_op jit(solution)/shard_map/all_gather | solution.py:254
  6.5 0.7 copy-start.3
  33.1 1.0 copy-start
  34.1 1.0 copy-start.1
  35.2 1.0 copy-start.2
  36.2 0.7 copy-start.4
  37.2 7.0 %collective-permute-start = (bf16[25,128,128]{2,1,0:T(8,128)(2,1)S(1)}, bf16[25,128,128]{2,1,0:T(8,128)(2,1)S(1)}, u32[]{:S(2)}, u32[]{:S(2)}) collective-permute-start(bf16[25,128,128]{2,1,0:T(8,128)(2,1)S(1)} %get-tuple-element.10), channel_id=1, source_target_pairs={{0,1},{1,0},{2,3},{3,2},{4,5},{5,4},{6,7},{7,6},{8,9},{9,8},{10,11... | collective-permute-start | bytes 2457608 | tf_op jit(solution)/shard_map/ppermute | solution.py:258
  68.0 16.1 %all-to-all-start.1 = ((bf16[16,72,128]{2,1,0:T(8,128)(2,1)}), bf16[16,72,128]{2,1,0:T(8,128)(2,1)S(1)}, u32[]{:S(2)}, u32[]{:S(2)}) async-start(bf16[16,72,128]{2,1,0:T(8,128)(2,1)} %shard_map.58), calls=%async_computation.1 | async-start | bytes 589824 | tf_op jit(solution)/shard_map/all_to_all | solution.py:208
  85.0 16.9 %all-to-all-start.2 = ((bf16[16,64,128]{2,1,0:T(8,128)(2,1)}), bf16[16,64,128]{2,1,0:T(8,128)(2,1)S(1)}, u32[]{:S(2)}, u32[]{:S(2)}) async-start(bf16[16,64,128]{2,1,0:T(8,128)(2,1)} %shard_map.59), calls=%async_computation.2 | async-start | bytes 524288 | tf_op jit(solution)/shard_map/all_to_all | solution.py:208
  103.2 6.1 %collective-permute-start.1 = (bf16[8,128,128]{2,1,0:T(8,128)(2,1)S(1)}, bf16[8,128,128]{2,1,0:T(8,128)(2,1)S(1)}, u32[]{:S(2)}, u32[]{:S(2)}) collective-permute-start(bf16[8,128,128]{2,1,0:T(8,128)(2,1)S(1)} %get-tuple-element.12), channel_id=1, source_target_pairs={{0,1},{1,0},{2,3},{3,2},{4,5},{5,4},{6,7},{7,6},{8,9},{9,8},{10,11... | collective-permute-start | bytes 786440 | tf_op jit(solution)/shard_map/ppermute | solution.py:272
Sparse Core Ops, SparseCore 0:
  33.2 74.5 all-gather.1

commit v5 on v4

--- a/solution.py
+++ b/solution.py
@@ -8,7 +8,8 @@
 HD = 128
 PAD = 8
 NEAR = 16
-RUN = 4
+RUN = 2
+ROW = 8
 BF16 = jnp.bfloat16
 F32 = jnp.float32
 VMEM = pltpu.CompilerParams(vmem_limit_bytes=12 * 1024 * 1024)
@@ -167,7 +168,7 @@
     scale = jnp.exp(within_cols(decays(first, own_ref, other_ref)))
     place = lax.broadcasted_iota(jnp.int32, (HD, HD), 1)
     source = lax.broadcasted_iota(jnp.int32, (HD, HD), 0)
-    wanted = (place // 4 % 2) * (HD // 2) + (place // 8) * 4 + place % 4
+    wanted = (place // 64) * 64 + (place % 32 // 4) * 8 + (place // 32 % 2) * 4 + place % 4
     reorder = (source == wanted).astype(BF16)
     for h in range(heads):
         queries = tokens(first, own_ref, other_ref, 2 * heads + h)
@@ -182,11 +183,13 @@
 
 def project_kernel(core_ref, kept_ref, got_ref, weight_ref, out_ref, rows_ref, sems):
     first = core_ref[0] == 0
-    heads = weight_ref.shape[1]
+    heads = rows_ref.shape[0]
     half = heads // 2
+    lines = weight_ref.shape[0]
 
     def copy(h):
-        return pltpu.make_async_copy(weight_ref.at[:, h], rows_ref.at[h], sems.at[h])
+        source = weight_ref.at[h % lines, :, h // lines]
+        return pltpu.make_async_copy(source, rows_ref.at[h], sems.at[h])
 
     def normed(h):
         low, high = both(first, kept_ref, got_ref, h % half)
@@ -239,6 +242,22 @@
     rows = HD * half // NEAR
     near = [list(range(i + c, i + size, 2)) for i in range(0, devices, size) for c in range(2)]
     far = [list(range(i, devices, size)) for i in range(size)]
+    lanes = groups // ROW
+    chips = members // 2
+
+    def device(x, y, z, c):
+        return (x * ROW + y) * members + 2 * z + c
+
+    plane = [
+        [device(x, y, z, c) for x in range(lanes) for z in range(chips)]
+        for y in range(ROW)
+        for c in range(2)
+    ]
+    ring = [
+        [device(x, y, z, c) for y in range(ROW) for c in range(2)]
+        for x in range(lanes)
+        for z in range(chips)
+    ]
     partner = [(i, i ^ 1) for i in range(members)]
     core = (lax.axis_index("head") & 1).reshape(1)
     place = (lax.axis_index("seq") // (size // members)).reshape(1)
@@ -247,11 +266,13 @@
     spread = pl.pallas_call(
         spread_kernel, out_shape=shape(groups, weight_rows, width, kind=BF16), compiler_params=VMEM
     )(out_weight)
-    spread = lax.all_to_all(spread, "seq", split_axis=0, concat_axis=0, tiled=True)
+    spread = swap(spread, plane)
     spread = pl.pallas_call(
         merge_kernel, out_shape=shape(groups * weight_rows, width, kind=BF16), compiler_params=VMEM
     )(spread)
-    weight = lax.all_gather(spread, "head", axis=0, tiled=True)
+    weight = lax.all_gather(
+        spread, ("seq", "head"), axis=0, axis_index_groups=ring, tiled=True
+    )
 
     pair = shape(3 * half + 1, count, HD, kind=BF16)
     own, other = call(pack_kernel, (pair, pair), core, decay_t, queries, keys, values)
@@ -270,7 +291,8 @@
     normed = shape(half, count, HD, kind=BF16)
     kept, sent = call(norm_kernel, (normed, normed), core, own, other, local_part, prior)
     got = lax.ppermute(sent, "head", partner)
-    weight = weight.reshape(members, groups // 2, 2 * weight_rows, width)
+    run = chips * weight_rows
+    weight = weight.reshape(ROW // 2, 4, lanes, run, width)
     weight = pltpu.with_memory_space_constraint(weight, pltpu.HBM)
     vmem = pl.BlockSpec(memory_space=pltpu.VMEM)
     return pl.pallas_call(
@@ -284,7 +306,7 @@
         ],
         out_specs=vmem,
         scratch_shapes=[
-            pltpu.VMEM((heads, members, 2 * weight_rows, width), BF16),
+            pltpu.VMEM((heads, 4, run, width), BF16),
             pltpu.SemaphoreType.DMA((heads,)),
         ],
         compiler_params=LARGE,

time: 122 us -> 125 us (1.025)
  waiting for transfers between devices: 24.2 us -> 29.9 us
  blocking collectives: 47.2 us -> 45 us
    all_to_all x1 -> x0, blocking collectives: 24.8 us -> none  [mix(): lax.all_to_all(spread, 'seq', split_axis=0, concat_axis=0, tiled=True)]
    all_to_all x1 -> x2, blocking collectives: 22.4 us -> 45 us  [swap(): lax.all_to_all(x, ('seq', 'head'), split_axis=0, concat_axis=0, axis_inde...]
    all_to_all x2, waiting for transfers between devices: 21.2 us -> 26.8 us  [swap(): lax.all_to_all(x, ('seq', 'head'), split_axis=0, concat_axis=0, axis_inde...]
where the time goes in v5:
time: 125 us; the launch traced here: 124 us
  blocking collectives  45 us (36%)
  waiting for transfers between devices  29.9 us (24%)
  starting transfers between devices  20.7 us (17%)
  between operations  13.5 us (11%)
  Pallas kernels  10.3 us (8%)
  local copies, waits for them, and re-layouts  4.52 us (4%)
    all_to_all x2, blocking collectives, swap(): lax.all_to_all(x, ('seq', 'head'), split_axis=0, concat_axis=0, axis_inde...  45 us
    all_to_all x2, waiting for transfers between devices, swap(): lax.all_to_all(x, ('seq', 'head'), split_axis=0, concat_axis=0, axis_inde...  26.8 us
    all_to_all x2, starting transfers between devices, swap(): lax.all_to_all(x, ('seq', 'head'), split_axis=0, concat_axis=0, axis_inde...  10.9 us
    ppermute x1, starting transfers between devices, mix(): other = lax.ppermute(other, 'head', partner)  5.04 us
    ppermute x1, starting transfers between devices, mix(): got = lax.ppermute(sent, 'head', partner)  4.82 us
    pallas_call x1, Pallas kernels, mix(): pl.pallas_call(project_kernel, out_shape=shape(count, width, kind=BF16),...  4.61 us
    unnamed x10, local copies, waits for them, and re-layouts  4.52 us
    pallas_call x5, Pallas kernels, call(): pl.pallas_call(kernel, out_shape=out, in_specs=[smem] + [vmem] * (len(arg...  3.88 us
  transfers between devices with their start and end apart: 5, of which 4 were waited for; matrix products, arithmetic and copies ran while one was open for 0% of the time, Pallas kernels for 4%

profile of v5, /device:TPU:1, one launch (start us, length us, event | category | flops | bytes accessed | tf_op | source)
XLA Modules:
  0.0 123.9 jit_solution(10820853367979042317)
XLA Ops:
  6.5 0.0 all-gather.2.cloned.1.call-start
  6.5 0.0 copy-start.3
  6.5 0.7 copy-done.3
  7.3 28.0 %all_to_all.20.in_ref = bf16[32,4,2048]{2,1,0:T(4,128)(2,1)S(1)} all-to-all(bf16[32,4,2048]{2,1,0:T(4,128)(2,1)S(1)} %shard_map.61), channel_id=1, replica_groups={{0,2,4,6,8,10,12,14,128,130,132,134,136,138,140,142,256,258,260,262,264..., dimensions={0} | all-to-all | bytes 1048576 | tf_op jit(solution)/shard_map/all_to_all | solution.py:211
  35.3 0.9 shard_map.62
  36.3 0.0 all-gather.2.cloned.1.call-update
  36.3 0.0 copy-start
  36.3 1.0 copy-done
  37.3 0.0 copy-start.1
  37.3 1.0 copy-done.1
  38.4 0.0 copy-start.2
  38.4 1.0 copy-done.2
  39.4 0.0 copy-start.4
  39.4 0.7 copy-done.4
  40.1 0.3 shard_map.55
  40.4 5.0 %collective-permute-start = (bf16[25,128,128]{2,1,0:T(8,128)(2,1)S(1)}, bf16[25,128,128]{2,1,0:T(8,128)(2,1)S(1)}, u32[]{:S(2)}, u32[]{:S(2)}) collective-permute-start(bf16[25,128,128]{2,1,0:T(8,128)(2,1)S(1)} %get-tuple-element.10), channel_id=1, source_target_pairs={{0,1},{1,0},{2,3},{3,2},{4,5},{5,4},{6,7},{7,6},{8,9},{9,8},{10,11... | collective-permute-start | bytes 2457608 | tf_op jit(solution)/shard_map/ppermute | solution.py:279
  45.4 1.9 %collective-permute-done.other_ref = bf16[25,128,128]{2,1,0:T(8,128)(2,1)S(1)} collective-permute-done((bf16[25,128,128]{2,1,0:T(8,128)(2,1)S(1)}, bf16[25,128,128]{2,1,0:T(8,128)(2,1)S(1)}, u32[]{:S(2)}, u32[]{:S(2)}) %collective-permute-start) | collective-permute-done | bytes 819232 | tf_op jit(solution)/shard_map/ppermute | solution.py:279
  47.4 0.6 shard_map.57
  48.0 17.0 %all_to_all.21.group_ref = bf16[16,72,128]{2,1,0:T(8,128)(2,1)S(1)} all-to-all(bf16[16,72,128]{2,1,0:T(8,128)(2,1)S(1)} %shard_map.57), channel_id=1, replica_groups={{0,2,4,6,8,10,12,14,16,18,20,22,24,26,28,30},{1,3,5,7,9,11,13,15,17,19,..., dimensions={0} | all-to-all | bytes 589824 | tf_op jit(solution)/shard_map/all_to_all | solution.py:211
  65.0 0.8 shard_map.58
  65.8 6.8 %all-to-all-start.1 = ((bf16[16,72,128]{2,1,0:T(8,128)(2,1)}), bf16[16,72,128]{2,1,0:T(8,128)(2,1)S(1)}, u32[]{:S(2)}, u32[]{:S(2)}) async-start(bf16[16,72,128]{2,1,0:T(8,128)(2,1)} %shard_map.58), calls=%async_computation.1 | async-start | bytes 589824 | tf_op jit(solution)/shard_map/all_to_all | solution.py:211
  72.6 17.0 %all-to-all-done.1.totals_ref = bf16[16,72,128]{2,1,0:T(8,128)(2,1)S(1)} async-done(((bf16[16,72,128]{2,1,0:T(8,128)(2,1)}), bf16[16,72,128]{2,1,0:T(8,128)(2,1)S(1)}, u32[]{:S(2)}, u32[]{:S(2)}) %all-to-all-start.1) | async-done | bytes 294944 | tf_op jit(solution)/shard_map/all_to_all | solution.py:211
  89.6 0.9 shard_map.59
  90.5 4.0 %all-to-all-start.2 = ((bf16[16,64,128]{2,1,0:T(8,128)(2,1)}), bf16[16,64,128]{2,1,0:T(8,128)(2,1)S(1)}, u32[]{:S(2)}, u32[]{:S(2)}) async-start(bf16[16,64,128]{2,1,0:T(8,128)(2,1)} %shard_map.59), calls=%async_computation.2 | async-start | bytes 524288 | tf_op jit(solution)/shard_map/all_to_all | solution.py:211
  94.6 0.9 shard_map.56.local_ref
  95.5 9.8 %all-to-all-done.2 = bf16[16,64,128]{2,1,0:T(8,128)(2,1)S(1)} async-done(((bf16[16,64,128]{2,1,0:T(8,128)(2,1)}), bf16[16,64,128]{2,1,0:T(8,128)(2,1)S(1)}, u32[]{:S(2)}, u32[]{:S(2)}) %all-to-all-start.2) | async-done | bytes 262176 | tf_op jit(solution)/shard_map/all_to_all | solution.py:211
  105.2 1.2 %shard_map.60 = (bf16[8,128,128]{2,1,0:T(8,128)(2,1)S(1)}, bf16[8,128,128]{2,1,0:T(8,128)(2,1)S(1)}) custom-call(s32[1]{0:T(128)} %bitcast.core_ref, bf16[25,128,128]{2,1,0:T(8,128)(2,1)S(1)} %get-tuple-element.9.own_ref, bf16[25,128,128]{2,1,0:T(8,128)(2,1)S(1)} %collective-permute-done.other_ref, f32[8,256,128]{2,1,0:T(8,128)S(1)} %shard_map.56.local_ref, ...), custom_call_target="tpu_custom_call" | custom-call | tf_op jit(solution)/shard_map/pallas_call | solution.py:223
  106.5 4.8 %collective-permute-start.1 = (bf16[8,128,128]{2,1,0:T(8,128)(2,1)S(1)}, bf16[8,128,128]{2,1,0:T(8,128)(2,1)S(1)}, u32[]{:S(2)}, u32[]{:S(2)}) collective-permute-start(bf16[8,128,128]{2,1,0:T(8,128)(2,1)S(1)} %get-tuple-element.12), channel_id=1, source_target_pairs={{0,1},{1,0},{2,3},{3,2},{4,5},{5,4},{6,7},{7,6},{8,9},{9,8},{10,11... | collective-permute-start | bytes 786440 | tf_op jit(solution)/shard_map/ppermute | solution.py:293
  111.3 1.1 collective-permute-done.1.got_ref
  112.5 0.0 all-gather.2.cloned.1.call-done
  112.5 4.6 %shard_map.63 = bf16[128,2048]{1,0:T(8,128)(2,1)} custom-call(s32[1]{0:T(128)} %bitcast.core_ref, bf16[8,128,128]{2,1,0:T(8,128)(2,1)S(1)} %get-tuple-element.11.kept_ref, bf16[8,128,128]{2,1,0:T(8,128)(2,1)S(1)} %collective-permute-done.1.got_ref, bf16[4,4,4,32,2048]{4,3,2,1,0:T(8,128)(2,1)} %bitcast.7), custom_call_target="tpu_custom_call" | custom-call | tf_op jit(solution)/shard_map/pallas_call | solution.py:298
  (1 shorter events, 0.0 us)
Async XLA Ops:
  6.5 105.9 %all-gather.2.cloned.1.call-start = ((), (), s32[]{:S(2)}) async-start(), calls=%async_computation.4 | async-start | bytes 8912896 | tf_op jit(solution)/shard_map/all_gather | solution.py:273
  6.5 0.7 copy-start.3
  36.3 1.0 copy-start
  37.3 1.0 copy-start.1
  38.4 1.0 copy-start.2
  39.4 0.7 copy-start.4
  40.4 7.0 %collective-permute-start = (bf16[25,128,128]{2,1,0:T(8,128)(2,1)S(1)}, bf16[25,128,128]{2,1,0:T(8,128)(2,1)S(1)}, u32[]{:S(2)}, u32[]{:S(2)}) collective-permute-start(bf16[25,128,128]{2,1,0:T(8,128)(2,1)S(1)} %get-tuple-element.10), channel_id=1, source_target_pairs={{0,1},{1,0},{2,3},{3,2},{4,5},{5,4},{6,7},{7,6},{8,9},{9,8},{10,11... | collective-permute-start | bytes 2457608 | tf_op jit(solution)/shard_map/ppermute | solution.py:279
  65.8 23.9 %all-to-all-start.1 = ((bf16[16,72,128]{2,1,0:T(8,128)(2,1)}), bf16[16,72,128]{2,1,0:T(8,128)(2,1)S(1)}, u32[]{:S(2)}, u32[]{:S(2)}) async-start(bf16[16,72,128]{2,1,0:T(8,128)(2,1)} %shard_map.58), calls=%async_computation.1 | async-start | bytes 589824 | tf_op jit(solution)/shard_map/all_to_all | solution.py:211
  90.5 14.7 %all-to-all-start.2 = ((bf16[16,64,128]{2,1,0:T(8,128)(2,1)}), bf16[16,64,128]{2,1,0:T(8,128)(2,1)S(1)}, u32[]{:S(2)}, u32[]{:S(2)}) async-start(bf16[16,64,128]{2,1,0:T(8,128)(2,1)} %shard_map.59), calls=%async_computation.2 | async-start | bytes 524288 | tf_op jit(solution)/shard_map/all_to_all | solution.py:211
  106.5 6.0 %collective-permute-start.1 = (bf16[8,128,128]{2,1,0:T(8,128)(2,1)S(1)}, bf16[8,128,128]{2,1,0:T(8,128)(2,1)S(1)}, u32[]{:S(2)}, u32[]{:S(2)}) collective-permute-start(bf16[8,128,128]{2,1,0:T(8,128)(2,1)S(1)} %get-tuple-element.12), channel_id=1, source_target_pairs={{0,1},{1,0},{2,3},{3,2},{4,5},{5,4},{6,7},{7,6},{8,9},{9,8},{10,11... | collective-permute-start | bytes 786440 | tf_op jit(solution)/shard_map/ppermute | solution.py:293
Sparse Core Ops, SparseCore 0:
  36.4 68.7 all-gather.1

commit v6 on v5

--- a/solution.py
+++ b/solution.py
@@ -129,13 +129,13 @@
         out_ref[j, rows:, :] = parts
 
 
-def prior_kernel(place_ref, totals_ref, group_ref, out_ref):
+def prior_kernel(place_ref, planes_ref, lines_ref, group_ref, out_ref):
     rows = out_ref.shape[1]
-    place = place_ref[0]
     state = jnp.zeros((rows, HD), F32)
-    for i in range(totals_ref.shape[0]):
-        later = jnp.exp(total_of(totals_ref, i)) * state + totals_ref[i, :rows, :].astype(F32)
-        state = jnp.where(i < place, later, state)
+    for n, ref in enumerate((planes_ref, lines_ref)):
+        for i in range(ref.shape[0]):
+            later = jnp.exp(total_of(ref, i)) * state + ref[i, :rows, :].astype(F32)
+            state = jnp.where(i < place_ref[n], later, state)
     for i in range(group_ref.shape[0]):
         out_ref[i] = state.astype(BF16)
         state = jnp.exp(total_of(group_ref, i)) * state + group_ref[i, :rows, :].astype(F32)
@@ -217,6 +217,14 @@
     return jax.ShapeDtypeStruct(dims, kind)
 
 
+def summed(group, copies):
+    return pl.pallas_call(
+        group_kernel,
+        out_shape=shape(copies, *group.shape[1:], kind=BF16),
+        compiler_params=VMEM,
+    )(group)
+
+
 def call(kernel, out, *args, **options):
     vmem = pl.BlockSpec(memory_space=pltpu.VMEM)
     smem = pl.BlockSpec(memory_space=pltpu.SMEM)
@@ -241,7 +249,6 @@
     size = 2 * NEAR
     rows = HD * half // NEAR
     near = [list(range(i + c, i + size, 2)) for i in range(0, devices, size) for c in range(2)]
-    far = [list(range(i, devices, size)) for i in range(size)]
     lanes = groups // ROW
     chips = members // 2
 
@@ -258,9 +265,24 @@
         for x in range(lanes)
         for z in range(chips)
     ]
+    pairs = size // members
+    far = [
+        [device(x, pairs * i + y, z, c) for i in range(ROW // pairs)]
+        for x in range(lanes)
+        for y in range(pairs)
+        for z in range(chips)
+        for c in range(2)
+    ]
+    across = [
+        [device(x, y, z, c) for x in range(lanes)]
+        for y in range(ROW)
+        for z in range(chips)
+        for c in range(2)
+    ]
+    seq = lax.axis_index("seq")
+    place = jnp.stack([lax.div(seq, ROW), lax.div(lax.rem(seq, ROW), pairs)])
     partner = [(i, i ^ 1) for i in range(members)]
     core = (lax.axis_index("head") & 1).reshape(1)
-    place = (lax.axis_index("seq") // (size // members)).reshape(1)
 
     weight_rows = out_weight.shape[0]
     spread = pl.pallas_call(
@@ -280,13 +302,9 @@
     states = call(states_kernel, shape(NEAR, rows + PAD, HD, kind=BF16), core, own, other)
     local_part = call(local_kernel, shape(half, 2 * count, HD), core, own, other)
     group = swap(states, near)
-    totals = pl.pallas_call(
-        group_kernel,
-        out_shape=shape(len(far[0]), rows + PAD, HD, kind=BF16),
-        compiler_params=VMEM,
-    )(group)
-    totals = swap(totals, far)
-    prior = call(prior_kernel, shape(NEAR, rows, HD, kind=BF16), place, totals, group)
+    lines = swap(summed(group, len(far[0])), far)
+    planes = swap(summed(lines, lanes), across)
+    prior = call(prior_kernel, shape(NEAR, rows, HD, kind=BF16), place, planes, lines, group)
     prior = swap(prior, near).reshape(half, HD, HD)
     normed = shape(half, count, HD, kind=BF16)
     kept, sent = call(norm_kernel, (normed, normed), core, own, other, local_part, prior)

time: 125 us -> 123 us (0.984)
  waiting for transfers between devices: 29.9 us -> 23.4 us
  starting transfers between devices: 20.7 us -> 24.3 us
    all_to_all x2 -> x3, waiting for transfers between devices: 26.8 us -> 20.3 us  [swap(): lax.all_to_all(x, ('seq', 'head'), split_axis=0, concat_axis=0, axis_inde...]
    all_to_all x2 -> x3, starting transfers between devices: 10.9 us -> 13 us  [swap(): lax.all_to_all(x, ('seq', 'head'), split_axis=0, concat_axis=0, axis_inde...]
    ppermute x1, starting transfers between devices: 4.82 us -> 6.16 us  [mix(): got = lax.ppermute(sent, 'head', partner)]
  transfers between devices with their start and end apart: 5 -> 6, of which waited for: 4 -> 5; matrix products, arithmetic and copies ran while one was open for 0% -> 0% of each run, Pallas kernels for 4% -> 5%
where the time goes in v6:
time: 123 us; the launch traced here: 122 us
  blocking collectives  45 us (37%)
  starting transfers between devices  24.3 us (20%)
  waiting for transfers between devices  23.4 us (19%)
  between operations  13.5 us (11%)
  Pallas kernels  11.3 us (9%)
  local copies, waits for them, and re-layouts  4.52 us (4%)
    all_to_all x2, blocking collectives, swap(): lax.all_to_all(x, ('seq', 'head'), split_axis=0, concat_axis=0, axis_inde...  45 us
    all_to_all x3, waiting for transfers between devices, swap(): lax.all_to_all(x, ('seq', 'head'), split_axis=0, concat_axis=0, axis_inde...  20.3 us
    all_to_all x3, starting transfers between devices, swap(): lax.all_to_all(x, ('seq', 'head'), split_axis=0, concat_axis=0, axis_inde...  13 us
    ppermute x1, starting transfers between devices, mix(): got = lax.ppermute(sent, 'head', partner)  6.16 us
    ppermute x1, starting transfers between devices, mix(): other = lax.ppermute(other, 'head', partner)  5.04 us
    pallas_call x1, Pallas kernels, mix(): pl.pallas_call(project_kernel, out_shape=shape(count, width, kind=BF16),...  4.61 us
    unnamed x10, local copies, waits for them, and re-layouts  4.52 us
    pallas_call x5, Pallas kernels, call(): pl.pallas_call(kernel, out_shape=out, in_specs=[smem] + [vmem] * (len(arg...  4.37 us
  transfers between devices with their start and end apart: 6, of which 5 were waited for; matrix products, arithmetic and copies ran while one was open for 0% of the time, Pallas kernels for 5%

profile of v6, /device:TPU:1, one launch (start us, length us, event | category | flops | bytes accessed | tf_op | source)
XLA Modules:
  0.0 122.0 jit_solution(6416291510832593965)
XLA Ops:
  6.5 0.0 all-gather.2.cloned.1.call-start
  6.5 0.0 copy-start.3
  6.5 0.7 copy-done.3
  7.3 28.0 %all_to_all.25.in_ref = bf16[32,4,2048]{2,1,0:T(4,128)(2,1)S(1)} all-to-all(bf16[32,4,2048]{2,1,0:T(4,128)(2,1)S(1)} %shard_map.62), channel_id=1, replica_groups={{0,2,4,6,8,10,12,14,128,130,132,134,136,138,140,142,256,258,260,262,264..., dimensions={0} | all-to-all | bytes 1048576 | tf_op jit(solution)/shard_map/all_to_all | solution.py:211
  35.3 0.9 shard_map.63
  36.3 0.0 all-gather.2.cloned.1.call-update
  36.3 0.0 copy-start
  36.3 1.0 copy-done
  37.3 0.0 copy-start.1
  37.3 1.0 copy-done.1
  38.4 0.0 copy-start.2
  38.4 1.0 copy-done.2
  39.4 0.0 copy-start.4
  39.4 0.7 copy-done.4
  40.1 0.3 shard_map.55
  40.4 5.0 %collective-permute-start = (bf16[25,128,128]{2,1,0:T(8,128)(2,1)S(1)}, bf16[25,128,128]{2,1,0:T(8,128)(2,1)S(1)}, u32[]{:S(2)}, u32[]{:S(2)}) collective-permute-start(bf16[25,128,128]{2,1,0:T(8,128)(2,1)S(1)} %get-tuple-element.10), channel_id=1, source_target_pairs={{0,1},{1,0},{2,3},{3,2},{4,5},{5,4},{6,7},{7,6},{8,9},{9,8},{10,11... | collective-permute-start | bytes 2457608 | tf_op jit(solution)/shard_map/ppermute | solution.py:301
  45.4 1.9 %collective-permute-done.other_ref = bf16[25,128,128]{2,1,0:T(8,128)(2,1)S(1)} collective-permute-done((bf16[25,128,128]{2,1,0:T(8,128)(2,1)S(1)}, bf16[25,128,128]{2,1,0:T(8,128)(2,1)S(1)}, u32[]{:S(2)}, u32[]{:S(2)}) %collective-permute-start) | collective-permute-done | bytes 819232 | tf_op jit(solution)/shard_map/ppermute | solution.py:301
  47.4 0.6 shard_map.57
  48.0 17.0 %all_to_all.26.group_ref = bf16[16,72,128]{2,1,0:T(8,128)(2,1)S(1)} all-to-all(bf16[16,72,128]{2,1,0:T(8,128)(2,1)S(1)} %shard_map.57), channel_id=1, replica_groups={{0,2,4,6,8,10,12,14,16,18,20,22,24,26,28,30},{1,3,5,7,9,11,13,15,17,19,..., dimensions={0} | all-to-all | bytes 589824 | tf_op jit(solution)/shard_map/all_to_all | solution.py:211
  65.0 0.7 shard_map.58
  65.7 5.9 %all-to-all-start.1 = ((bf16[4,72,128]{2,1,0:T(8,128)(2,1)}), bf16[4,72,128]{2,1,0:T(8,128)(2,1)S(1)}, u32[]{:S(2)}, u32[]{:S(2)}) async-start(bf16[4,72,128]{2,1,0:T(8,128)(2,1)} %shard_map.58), calls=%async_computation.1 | async-start | bytes 147456 | tf_op jit(solution)/shard_map/all_to_all | solution.py:211
  71.6 8.0 %all-to-all-done.1.group_ref.lines_ref = bf16[4,72,128]{2,1,0:T(8,128)(2,1)S(1)} async-done(((bf16[4,72,128]{2,1,0:T(8,128)(2,1)}), bf16[4,72,128]{2,1,0:T(8,128)(2,1)S(1)}, u32[]{:S(2)}, u32[]{:S(2)}) %all-to-all-start.1) | async-done | bytes 73760 | tf_op jit(solution)/shard_map/all_to_all | solution.py:211
  79.5 0.7 shard_map.59
  80.2 3.3 %all-to-all-start.2 = ((bf16[4,72,128]{2,1,0:T(8,128)(2,1)}), bf16[4,72,128]{2,1,0:T(8,128)(2,1)S(1)}, u32[]{:S(2)}, u32[]{:S(2)}) async-start(bf16[4,72,128]{2,1,0:T(8,128)(2,1)} %shard_map.59), calls=%async_computation.2 | async-start | bytes 147456 | tf_op jit(solution)/shard_map/all_to_all | solution.py:211
  83.5 0.1 pad_add_fusion.place_ref
  83.6 4.5 %all-to-all-done.2.planes_ref = bf16[4,72,128]{2,1,0:T(8,128)(2,1)S(1)} async-done(((bf16[4,72,128]{2,1,0:T(8,128)(2,1)}), bf16[4,72,128]{2,1,0:T(8,128)(2,1)S(1)}, u32[]{:S(2)}, u32[]{:S(2)}) %all-to-all-start.2) | async-done | bytes 73760 | tf_op jit(solution)/shard_map/all_to_all | solution.py:211
  88.0 1.4 %shard_map.60 = bf16[16,64,128]{2,1,0:T(8,128)(2,1)} custom-call(s32[2]{0:T(128)S(1)} %pad_add_fusion.place_ref, bf16[4,72,128]{2,1,0:T(8,128)(2,1)S(1)} %all-to-all-done.2.planes_ref, bf16[4,72,128]{2,1,0:T(8,128)(2,1)S(1)} %all-to-all-done.1.group_ref.lines_ref, bf16[16,72,128]{2,1,0:T(8,128)(2,1)S(1)} %all_to_all.26.group_ref), custom_call_target="tpu_custom_call" | custom-call | tf_op jit(solution)/shard_map/pallas_call | solution.py:231
  89.4 3.8 %all-to-all-start.3 = ((bf16[16,64,128]{2,1,0:T(8,128)(2,1)}), bf16[16,64,128]{2,1,0:T(8,128)(2,1)S(1)}, u32[]{:S(2)}, u32[]{:S(2)}) async-start(bf16[16,64,128]{2,1,0:T(8,128)(2,1)} %shard_map.60), calls=%async_computation.3 | async-start | bytes 524288 | tf_op jit(solution)/shard_map/all_to_all | solution.py:211
  93.2 0.9 shard_map.56.local_ref
  94.1 7.8 %all-to-all-done.3 = bf16[16,64,128]{2,1,0:T(8,128)(2,1)S(1)} async-done(((bf16[16,64,128]{2,1,0:T(8,128)(2,1)}), bf16[16,64,128]{2,1,0:T(8,128)(2,1)S(1)}, u32[]{:S(2)}, u32[]{:S(2)}) %all-to-all-start.3) | async-done | bytes 262176 | tf_op jit(solution)/shard_map/all_to_all | solution.py:211
  102.0 1.2 %shard_map.61 = (bf16[8,128,128]{2,1,0:T(8,128)(2,1)S(1)}, bf16[8,128,128]{2,1,0:T(8,128)(2,1)S(1)}) custom-call(s32[1]{0:T(128)} %bitcast.core_ref, bf16[25,128,128]{2,1,0:T(8,128)(2,1)S(1)} %get-tuple-element.9.own_ref, bf16[25,128,128]{2,1,0:T(8,128)(2,1)S(1)} %collective-permute-done.other_ref, f32[8,256,128]{2,1,0:T(8,128)S(1)} %shard_map.56.local_ref, ...), custom_call_target="tpu_custom_call" | custom-call | tf_op jit(solution)/shard_map/pallas_call | solution.py:231
  103.2 6.2 %collective-permute-start.1 = (bf16[8,128,128]{2,1,0:T(8,128)(2,1)S(1)}, bf16[8,128,128]{2,1,0:T(8,128)(2,1)S(1)}, u32[]{:S(2)}, u32[]{:S(2)}) collective-permute-start(bf16[8,128,128]{2,1,0:T(8,128)(2,1)S(1)} %get-tuple-element.12), channel_id=1, source_target_pairs={{0,1},{1,0},{2,3},{3,2},{4,5},{5,4},{6,7},{7,6},{8,9},{9,8},{10,11... | collective-permute-start | bytes 786440 | tf_op jit(solution)/shard_map/ppermute | solution.py:311
  109.4 1.1 collective-permute-done.1.got_ref
  110.5 0.0 all-gather.2.cloned.1.call-done
  110.5 4.6 %shard_map.64 = bf16[128,2048]{1,0:T(8,128)(2,1)} custom-call(s32[1]{0:T(128)} %bitcast.core_ref, bf16[8,128,128]{2,1,0:T(8,128)(2,1)S(1)} %get-tuple-element.11.kept_ref, bf16[8,128,128]{2,1,0:T(8,128)(2,1)S(1)} %collective-permute-done.1.got_ref, bf16[4,4,4,32,2048]{4,3,2,1,0:T(8,128)(2,1)} %bitcast.8), custom_call_target="tpu_custom_call" | custom-call | tf_op jit(solution)/shard_map/pallas_call | solution.py:316
  (1 shorter events, 0.0 us)
Async XLA Ops:
  6.5 104.0 %all-gather.2.cloned.1.call-start = ((), (), s32[]{:S(2)}) async-start(), calls=%async_computation.5 | async-start | bytes 8912896 | tf_op jit(solution)/shard_map/all_gather | solution.py:295
  6.5 0.7 copy-start.3
  36.3 1.0 copy-start
  37.3 1.0 copy-start.1
  38.4 1.0 copy-start.2
  39.4 0.7 copy-start.4
  40.4 7.0 %collective-permute-start = (bf16[25,128,128]{2,1,0:T(8,128)(2,1)S(1)}, bf16[25,128,128]{2,1,0:T(8,128)(2,1)S(1)}, u32[]{:S(2)}, u32[]{:S(2)}) collective-permute-start(bf16[25,128,128]{2,1,0:T(8,128)(2,1)S(1)} %get-tuple-element.10), channel_id=1, source_target_pairs={{0,1},{1,0},{2,3},{3,2},{4,5},{5,4},{6,7},{7,6},{8,9},{9,8},{10,11... | collective-permute-start | bytes 2457608 | tf_op jit(solution)/shard_map/ppermute | solution.py:301
  65.7 13.9 %all-to-all-start.1 = ((bf16[4,72,128]{2,1,0:T(8,128)(2,1)}), bf16[4,72,128]{2,1,0:T(8,128)(2,1)S(1)}, u32[]{:S(2)}, u32[]{:S(2)}) async-start(bf16[4,72,128]{2,1,0:T(8,128)(2,1)} %shard_map.58), calls=%async_computation.1 | async-start | bytes 147456 | tf_op jit(solution)/shard_map/all_to_all | solution.py:211
  80.2 7.8 %all-to-all-start.2 = ((bf16[4,72,128]{2,1,0:T(8,128)(2,1)}), bf16[4,72,128]{2,1,0:T(8,128)(2,1)S(1)}, u32[]{:S(2)}, u32[]{:S(2)}) async-start(bf16[4,72,128]{2,1,0:T(8,128)(2,1)} %shard_map.59), calls=%async_computation.2 | async-start | bytes 147456 | tf_op jit(solution)/shard_map/all_to_all | solution.py:211
  89.4 12.6 %all-to-all-start.3 = ((bf16[16,64,128]{2,1,0:T(8,128)(2,1)}), bf16[16,64,128]{2,1,0:T(8,128)(2,1)S(1)}, u32[]{:S(2)}, u32[]{:S(2)}) async-start(bf16[16,64,128]{2,1,0:T(8,128)(2,1)} %shard_map.60), calls=%async_computation.3 | async-start | bytes 524288 | tf_op jit(solution)/shard_map/all_to_all | solution.py:211
  103.2 7.3 %collective-permute-start.1 = (bf16[8,128,128]{2,1,0:T(8,128)(2,1)S(1)}, bf16[8,128,128]{2,1,0:T(8,128)(2,1)S(1)}, u32[]{:S(2)}, u32[]{:S(2)}) collective-permute-start(bf16[8,128,128]{2,1,0:T(8,128)(2,1)S(1)} %get-tuple-element.12), channel_id=1, source_target_pairs={{0,1},{1,0},{2,3},{3,2},{4,5},{5,4},{6,7},{7,6},{8,9},{9,8},{10,11... | collective-permute-start | bytes 786440 | tf_op jit(solution)/shard_map/ppermute | solution.py:311
Sparse Core Ops, SparseCore 0:
  36.4 61.7 all-gather.1

commit v7 on v6

--- a/solution.py
+++ b/solution.py
@@ -114,16 +114,32 @@
             out_ref[h * pieces + j, rows:, :] = parts
 
 
-def group_kernel(group_ref, out_ref):
-    rows = group_ref.shape[1] - PAD
+def total_state(ref, rows):
     state = jnp.zeros((rows, HD), F32)
     total = jnp.zeros((1, HD), F32)
-    for i in range(group_ref.shape[0]):
-        step = total_of(group_ref, i)
-        state = jnp.exp(step) * state + group_ref[i, :rows, :].astype(F32)
+    for i in range(ref.shape[0]):
+        step = total_of(ref, i)
+        state = jnp.exp(step) * state + ref[i, :rows, :].astype(F32)
         total = total + step
-    state = state.astype(BF16)
-    parts = parts_of(total)
+    return state.astype(BF16), parts_of(total)
+
+
+def group_kernel(group_ref, out_ref):
+    rows = out_ref.shape[0] - PAD
+    out_ref[:rows, :], out_ref[rows:, :] = total_state(group_ref, rows)
+
+
+def plane_kernel(place_ref, *refs):
+    *group_refs, lines_ref, out_ref = refs
+    count = len(group_refs)
+    rows = lines_ref.shape[1] - PAD
+    for i in range(count):
+        away = lax.rem(place_ref[1] - i + count, count)
+        group = group_refs[0][...]
+        for k in range(1, count):
+            group = jnp.where(away == k, group_refs[k][...], group)
+        lines_ref[i] = group
+    state, parts = total_state(lines_ref, rows)
     for j in range(out_ref.shape[0]):
         out_ref[j, :rows, :] = state
         out_ref[j, rows:, :] = parts
@@ -217,14 +233,6 @@
     return jax.ShapeDtypeStruct(dims, kind)
 
 
-def summed(group, copies):
-    return pl.pallas_call(
-        group_kernel,
-        out_shape=shape(copies, *group.shape[1:], kind=BF16),
-        compiler_params=VMEM,
-    )(group)
-
-
 def call(kernel, out, *args, **options):
     vmem = pl.BlockSpec(memory_space=pltpu.VMEM)
     smem = pl.BlockSpec(memory_space=pltpu.SMEM)
@@ -266,12 +274,10 @@
         for z in range(chips)
     ]
     pairs = size // members
-    far = [
-        [device(x, pairs * i + y, z, c) for i in range(ROW // pairs)]
-        for x in range(lanes)
-        for y in range(pairs)
-        for z in range(chips)
-        for c in range(2)
+    lines = ROW // pairs
+    shifts = [
+        [(x * ROW + y, x * ROW + (y + pairs * k) % ROW) for x in range(lanes) for y in range(ROW)]
+        for k in range(1, lines)
     ]
     across = [
         [device(x, y, z, c) for x in range(lanes)]
@@ -302,9 +308,14 @@
     states = call(states_kernel, shape(NEAR, rows + PAD, HD, kind=BF16), core, own, other)
     local_part = call(local_kernel, shape(half, 2 * count, HD), core, own, other)
     group = swap(states, near)
-    lines = swap(summed(group, len(far[0])), far)
-    planes = swap(summed(lines, lanes), across)
-    prior = call(prior_kernel, shape(NEAR, rows, HD, kind=BF16), place, planes, lines, group)
+    own_sum = pl.pallas_call(
+        group_kernel, out_shape=shape(rows + PAD, HD, kind=BF16), compiler_params=VMEM
+    )(group)
+    sums = [own_sum] + [lax.ppermute(own_sum, "seq", shift) for shift in shifts]
+    outs = tuple(shape(n, rows + PAD, HD, kind=BF16) for n in (lines, lanes))
+    in_order, planes = call(plane_kernel, outs, place, *sums)
+    planes = swap(planes, across)
+    prior = call(prior_kernel, shape(NEAR, rows, HD, kind=BF16), place, planes, in_order, group)
     prior = swap(prior, near).reshape(half, HD, HD)
     normed = shape(half, count, HD, kind=BF16)
     kept, sent = call(norm_kernel, (normed, normed), core, own, other, local_part, prior)

time: 123 us -> 123 us (level)
  starting transfers between devices: 24.3 us -> 34.9 us
  blocking collectives: 45 us -> 35 us
    ppermute x0 -> x3, starting transfers between devices: none -> 13.9 us  [mix(): sums = [own_sum] + [lax.ppermute(own_sum, 'seq', shift) for shift in shifts]]
    all_to_all x2, blocking collectives: 45 us -> 35 us  [swap(): lax.all_to_all(x, ('seq', 'head'), split_axis=0, concat_axis=0, axis_inde...]
    all_to_all x3 -> x2, starting transfers between devices: 13 us -> 9.1 us  [swap(): lax.all_to_all(x, ('seq', 'head'), split_axis=0, concat_axis=0, axis_inde...]
    ppermute x0 -> x3, waiting for transfers between devices: none -> 1.54 us  [mix(): sums = [own_sum] + [lax.ppermute(own_sum, 'seq', shift) for shift in shifts]]
    all_to_all x3 -> x2, waiting for transfers between devices: 20.3 us -> 18.7 us  [swap(): lax.all_to_all(x, ('seq', 'head'), split_axis=0, concat_axis=0, axis_inde...]
    pallas_call x5 -> x6, Pallas kernels: 4.37 us -> 5.7 us  [call(): pl.pallas_call(kernel, out_shape=out, in_specs=[smem] + [vmem] * (len(arg...]
    pallas_call x2 -> x1, Pallas kernels: 1.36 us -> 0.09 us  [mix(): pl.pallas_call(group_kernel, out_shape=shape(rows + PAD, HD, kind=BF16),...]
  transfers between devices with their start and end apart: 6 -> 8, of which waited for: 5 -> 5; matrix products, arithmetic and copies ran while one was open for 0% -> 0% of each run, Pallas kernels for 5% -> 5%
where the time goes in v7:
time: 123 us
  blocking collectives  35 us (28%)
  starting transfers between devices  34.9 us (28%)
  waiting for transfers between devices  23.4 us (19%)
  between operations  13.5 us (11%)
  Pallas kernels  11.4 us (9%)
  local copies, waits for them, and re-layouts  4.52 us (4%)
    all_to_all x2, blocking collectives, swap(): lax.all_to_all(x, ('seq', 'head'), split_axis=0, concat_axis=0, axis_inde...  35 us
    all_to_all x2, waiting for transfers between devices, swap(): lax.all_to_all(x, ('seq', 'head'), split_axis=0, concat_axis=0, axis_inde...  18.7 us
    ppermute x3, starting transfers between devices, mix(): sums = [own_sum] + [lax.ppermute(own_sum, 'seq', shift) for shift in shifts]  13.9 us
    all_to_all x2, starting transfers between devices, swap(): lax.all_to_all(x, ('seq', 'head'), split_axis=0, concat_axis=0, axis_inde...  9.1 us
    ppermute x1, starting transfers between devices, mix(): got = lax.ppermute(sent, 'head', partner)  6.82 us
    pallas_call x6, Pallas kernels, call(): pl.pallas_call(kernel, out_shape=out, in_specs=[smem] + [vmem] * (len(arg...  5.7 us
    ppermute x1, starting transfers between devices, mix(): other = lax.ppermute(other, 'head', partner)  5.04 us
    pallas_call x1, Pallas kernels, mix(): pl.pallas_call(project_kernel, out_shape=shape(count, width, kind=BF16),...  4.62 us
  transfers between devices with their start and end apart: 8, of which 5 were waited for; matrix products, arithmetic and copies ran while one was open for 0% of the time, Pallas kernels for 5%

profile of v7, /device:TPU:1, one launch (start us, length us, event | category | flops | bytes accessed | tf_op | source)
XLA Modules:
  0.0 122.8 jit_solution(8949684529445328167)
XLA Ops:
  6.5 0.0 all-gather.2.cloned.1.call-start
  6.5 0.0 copy-start.3
  6.5 0.7 copy-done.3
  7.3 28.0 %all_to_all.20.in_ref = bf16[32,4,2048]{2,1,0:T(4,128)(2,1)S(1)} all-to-all(bf16[32,4,2048]{2,1,0:T(4,128)(2,1)S(1)} %shard_map.62), channel_id=1, replica_groups={{0,2,4,6,8,10,12,14,128,130,132,134,136,138,140,142,256,258,260,262,264..., dimensions={0} | all-to-all | bytes 1048576 | tf_op jit(solution)/shard_map/all_to_all | solution.py:227
  35.3 0.9 shard_map.63
  36.3 0.0 all-gather.2.cloned.1.call-update
  36.3 0.0 copy-start
  36.3 1.0 copy-done
  37.3 0.0 copy-start.1
  37.3 1.0 copy-done.1
  38.4 0.0 copy-start.2
  38.4 1.0 copy-done.2
  39.4 0.0 copy-start.4
  39.4 0.7 copy-done.4
  40.1 0.3 shard_map.55
  40.4 5.0 %collective-permute-start = (bf16[25,128,128]{2,1,0:T(8,128)(2,1)S(1)}, bf16[25,128,128]{2,1,0:T(8,128)(2,1)S(1)}, u32[]{:S(2)}, u32[]{:S(2)}) collective-permute-start(bf16[25,128,128]{2,1,0:T(8,128)(2,1)S(1)} %get-tuple-element.12), channel_id=1, source_target_pairs={{0,1},{1,0},{2,3},{3,2},{4,5},{5,4},{6,7},{7,6},{8,9},{9,8},{10,11... | collective-permute-start | bytes 2457608 | tf_op jit(solution)/shard_map/ppermute | solution.py:307
  45.4 1.9 %collective-permute-done.other_ref = bf16[25,128,128]{2,1,0:T(8,128)(2,1)S(1)} collective-permute-done((bf16[25,128,128]{2,1,0:T(8,128)(2,1)S(1)}, bf16[25,128,128]{2,1,0:T(8,128)(2,1)S(1)}, u32[]{:S(2)}, u32[]{:S(2)}) %collective-permute-start) | collective-permute-done | bytes 819232 | tf_op jit(solution)/shard_map/ppermute | solution.py:307
  47.4 1.3 %shard_map.57 = bf16[16,72,128]{2,1,0:T(8,128)(2,1)} custom-call(s32[1]{0:T(128)} %bitcast.core_ref, bf16[25,128,128]{2,1,0:T(8,128)(2,1)S(1)} %get-tuple-element.11.own_ref, bf16[25,128,128]{2,1,0:T(8,128)(2,1)S(1)} %collective-permute-done.other_ref), custom_call_target="tpu_custom_call" | custom-call | tf_op jit(solution)/shard_map/pallas_call | solution.py:239
  48.7 5.4 %all-to-all-start = ((bf16[16,72,128]{2,1,0:T(8,128)(2,1)}), bf16[16,72,128]{2,1,0:T(8,128)(2,1)S(1)}, u32[]{:S(2)}, u32[]{:S(2)}) async-start(bf16[16,72,128]{2,1,0:T(8,128)(2,1)} %shard_map.57), calls=%async_computation | async-start | bytes 589824 | tf_op jit(solution)/shard_map/all_to_all | solution.py:227
  54.1 11.8 %all-to-all-done.group_ref = bf16[16,72,128]{2,1,0:T(8,128)(2,1)S(1)} async-done(((bf16[16,72,128]{2,1,0:T(8,128)(2,1)}), bf16[16,72,128]{2,1,0:T(8,128)(2,1)S(1)}, u32[]{:S(2)}, u32[]{:S(2)}) %all-to-all-start) | async-done | bytes 294944 | tf_op jit(solution)/shard_map/all_to_all | solution.py:227
  65.9 0.1 shard_map.58.refs_0_
  66.0 4.2 %collective-permute-start.1 = (bf16[72,128]{1,0:T(8,128)(2,1)S(1)}, bf16[72,128]{1,0:T(8,128)(2,1)S(1)}, u32[]{:S(2)}, u32[]{:S(2)}) collective-permute-start(bf16[72,128]{1,0:T(8,128)(2,1)S(1)} %shard_map.58.refs_0_), channel_id=1, source_target_pairs={{0,32},{16,48},{32,64},{48,80},{64,96},{80,112},{96,0},{112,16},{1... | collective-permute-start | bytes 55304 | tf_op jit(solution)/shard_map/ppermute | solution.py:314
  70.2 4.8 %collective-permute-start.2 = (bf16[72,128]{1,0:T(8,128)(2,1)S(1)}, bf16[72,128]{1,0:T(8,128)(2,1)S(1)}, u32[]{:S(2)}, u32[]{:S(2)}) collective-permute-start(bf16[72,128]{1,0:T(8,128)(2,1)S(1)} %shard_map.58.refs_0_), channel_id=1, source_target_pairs={{0,64},{16,80},{32,96},{48,112},{64,0},{80,16},{96,32},{112,48},{1... | collective-permute-start | bytes 55304 | tf_op jit(solution)/shard_map/ppermute | solution.py:314
  75.0 5.0 %collective-permute-start.3 = (bf16[72,128]{1,0:T(8,128)(2,1)S(1)}, bf16[72,128]{1,0:T(8,128)(2,1)S(1)}, u32[]{:S(2)}, u32[]{:S(2)}) collective-permute-start(bf16[72,128]{1,0:T(8,128)(2,1)S(1)} %shard_map.58.refs_0_), channel_id=1, source_target_pairs={{0,96},{16,112},{32,0},{48,16},{64,32},{80,48},{96,64},{112,80},{1... | collective-permute-start | bytes 55304 | tf_op jit(solution)/shard_map/ppermute | solution.py:314
  79.9 0.1 pad_add_fusion.place_ref
  80.0 0.0 collective-permute-done.1.refs_1_
  80.0 0.0 collective-permute-done.2.refs_2_
  80.0 1.5 %collective-permute-done.3.refs_3_ = bf16[72,128]{1,0:T(8,128)(2,1)S(1)} collective-permute-done((bf16[72,128]{1,0:T(8,128)(2,1)S(1)}, bf16[72,128]{1,0:T(8,128)(2,1)S(1)}, u32[]{:S(2)}, u32[]{:S(2)}) %collective-permute-start.3) | collective-permute-done | bytes 18464 | tf_op jit(solution)/shard_map/ppermute | solution.py:314
  81.6 0.6 shard_map.59
  82.2 6.9 %all_to_all.21.planes_ref = bf16[4,72,128]{2,1,0:T(8,128)(2,1)S(1)} all-to-all(bf16[4,72,128]{2,1,0:T(8,128)(2,1)S(1)} %get-tuple-element.13), channel_id=1, replica_groups={{0,128,256,384},{1,129,257,385},{2,130,258,386},{3,131,259,387},{4,132,..., dimensions={0} | all-to-all | bytes 147456 | tf_op jit(solution)/shard_map/all_to_all | solution.py:227
  89.1 1.4 %shard_map.60 = bf16[16,64,128]{2,1,0:T(8,128)(2,1)} custom-call(s32[2]{0:T(128)S(1)} %pad_add_fusion.place_ref, bf16[4,72,128]{2,1,0:T(8,128)(2,1)S(1)} %all_to_all.21.planes_ref, bf16[4,72,128]{2,1,0:T(8,128)(2,1)S(1)} %get-tuple-element.14.lines_ref, bf16[16,72,128]{2,1,0:T(8,128)(2,1)S(1)} %all-to-all-done.group_ref), custom_call_target="tpu_custom_call" | custom-call | tf_op jit(solution)/shard_map/pallas_call | solution.py:239
  90.5 3.7 %all-to-all-start.2 = ((bf16[16,64,128]{2,1,0:T(8,128)(2,1)}), bf16[16,64,128]{2,1,0:T(8,128)(2,1)S(1)}, u32[]{:S(2)}, u32[]{:S(2)}) async-start(bf16[16,64,128]{2,1,0:T(8,128)(2,1)} %shard_map.60), calls=%async_computation.2 | async-start | bytes 524288 | tf_op jit(solution)/shard_map/all_to_all | solution.py:227
  94.2 0.9 shard_map.56.local_ref
  95.1 7.0 %all-to-all-done.2 = bf16[16,64,128]{2,1,0:T(8,128)(2,1)S(1)} async-done(((bf16[16,64,128]{2,1,0:T(8,128)(2,1)}), bf16[16,64,128]{2,1,0:T(8,128)(2,1)S(1)}, u32[]{:S(2)}, u32[]{:S(2)}) %all-to-all-start.2) | async-done | bytes 262176 | tf_op jit(solution)/shard_map/all_to_all | solution.py:227
  102.1 1.2 %shard_map.61 = (bf16[8,128,128]{2,1,0:T(8,128)(2,1)S(1)}, bf16[8,128,128]{2,1,0:T(8,128)(2,1)S(1)}) custom-call(s32[1]{0:T(128)} %bitcast.core_ref, bf16[25,128,128]{2,1,0:T(8,128)(2,1)S(1)} %get-tuple-element.11.own_ref, bf16[25,128,128]{2,1,0:T(8,128)(2,1)S(1)} %collective-permute-done.other_ref, f32[8,256,128]{2,1,0:T(8,128)S(1)} %shard_map.56.local_ref, ...), custom_call_target="tpu_custom_call" | custom-call | tf_op jit(solution)/shard_map/pallas_call | solution.py:239
  103.3 6.8 %collective-permute-start.4 = (bf16[8,128,128]{2,1,0:T(8,128)(2,1)S(1)}, bf16[8,128,128]{2,1,0:T(8,128)(2,1)S(1)}, u32[]{:S(2)}, u32[]{:S(2)}) collective-permute-start(bf16[8,128,128]{2,1,0:T(8,128)(2,1)S(1)} %get-tuple-element.16), channel_id=1, source_target_pairs={{0,1},{1,0},{2,3},{3,2},{4,5},{5,4},{6,7},{7,6},{8,9},{9,8},{10,11... | collective-permute-start | bytes 786440 | tf_op jit(solution)/shard_map/ppermute | solution.py:322
  110.1 1.1 collective-permute-done.4.got_ref
  111.3 0.0 all-gather.2.cloned.1.call-done
  111.3 4.6 %shard_map.64 = bf16[128,2048]{1,0:T(8,128)(2,1)} custom-call(s32[1]{0:T(128)} %bitcast.core_ref, bf16[8,128,128]{2,1,0:T(8,128)(2,1)S(1)} %get-tuple-element.15.kept_ref, bf16[8,128,128]{2,1,0:T(8,128)(2,1)S(1)} %collective-permute-done.4.got_ref, bf16[4,4,4,32,2048]{4,3,2,1,0:T(8,128)(2,1)} %bitcast.8), custom_call_target="tpu_custom_call" | custom-call | tf_op jit(solution)/shard_map/pallas_call | solution.py:327
  (1 shorter events, 0.0 us)
Async XLA Ops:
  6.5 104.8 %all-gather.2.cloned.1.call-start = ((), (), s32[]{:S(2)}) async-start(), calls=%async_computation.4 | async-start | bytes 8912896 | tf_op jit(solution)/shard_map/all_gather | solution.py:301
  6.5 0.7 copy-start.3
  36.3 1.0 copy-start
  37.3 1.0 copy-start.1
  38.4 1.0 copy-start.2
  39.4 0.7 copy-start.4
  40.4 7.0 %collective-permute-start = (bf16[25,128,128]{2,1,0:T(8,128)(2,1)S(1)}, bf16[25,128,128]{2,1,0:T(8,128)(2,1)S(1)}, u32[]{:S(2)}, u32[]{:S(2)}) collective-permute-start(bf16[25,128,128]{2,1,0:T(8,128)(2,1)S(1)} %get-tuple-element.12), channel_id=1, source_target_pairs={{0,1},{1,0},{2,3},{3,2},{4,5},{5,4},{6,7},{7,6},{8,9},{9,8},{10,11... | collective-permute-start | bytes 2457608 | tf_op jit(solution)/shard_map/ppermute | solution.py:307
  48.7 17.2 %all-to-all-start = ((bf16[16,72,128]{2,1,0:T(8,128)(2,1)}), bf16[16,72,128]{2,1,0:T(8,128)(2,1)S(1)}, u32[]{:S(2)}, u32[]{:S(2)}) async-start(bf16[16,72,128]{2,1,0:T(8,128)(2,1)} %shard_map.57), calls=%async_computation | async-start | bytes 589824 | tf_op jit(solution)/shard_map/all_to_all | solution.py:227
  66.0 14.1 %collective-permute-start.1 = (bf16[72,128]{1,0:T(8,128)(2,1)S(1)}, bf16[72,128]{1,0:T(8,128)(2,1)S(1)}, u32[]{:S(2)}, u32[]{:S(2)}) collective-permute-start(bf16[72,128]{1,0:T(8,128)(2,1)S(1)} %shard_map.58.refs_0_), channel_id=1, source_target_pairs={{0,32},{16,48},{32,64},{48,80},{64,96},{80,112},{96,0},{112,16},{1... | collective-permute-start | bytes 55304 | tf_op jit(solution)/shard_map/ppermute | solution.py:314
  70.2 9.8 %collective-permute-start.2 = (bf16[72,128]{1,0:T(8,128)(2,1)S(1)}, bf16[72,128]{1,0:T(8,128)(2,1)S(1)}, u32[]{:S(2)}, u32[]{:S(2)}) collective-permute-start(bf16[72,128]{1,0:T(8,128)(2,1)S(1)} %shard_map.58.refs_0_), channel_id=1, source_target_pairs={{0,64},{16,80},{32,96},{48,112},{64,0},{80,16},{96,32},{112,48},{1... | collective-permute-start | bytes 55304 | tf_op jit(solution)/shard_map/ppermute | solution.py:314
  75.0 6.6 %collective-permute-start.3 = (bf16[72,128]{1,0:T(8,128)(2,1)S(1)}, bf16[72,128]{1,0:T(8,128)(2,1)S(1)}, u32[]{:S(2)}, u32[]{:S(2)}) collective-permute-start(bf16[72,128]{1,0:T(8,128)(2,1)S(1)} %shard_map.58.refs_0_), channel_id=1, source_target_pairs={{0,96},{16,112},{32,0},{48,16},{64,32},{80,48},{96,64},{112,80},{1... | collective-permute-start | bytes 55304 | tf_op jit(solution)/shard_map/ppermute | solution.py:314
  90.5 11.6 %all-to-all-start.2 = ((bf16[16,64,128]{2,1,0:T(8,128)(2,1)}), bf16[16,64,128]{2,1,0:T(8,128)(2,1)S(1)}, u32[]{:S(2)}, u32[]{:S(2)}) async-start(bf16[16,64,128]{2,1,0:T(8,128)(2,1)} %shard_map.60), calls=%async_computation.2 | async-start | bytes 524288 | tf_op jit(solution)/shard_map/all_to_all | solution.py:227
  103.3 8.0 %collective-permute-start.4 = (bf16[8,128,128]{2,1,0:T(8,128)(2,1)S(1)}, bf16[8,128,128]{2,1,0:T(8,128)(2,1)S(1)}, u32[]{:S(2)}, u32[]{:S(2)}) collective-permute-start(bf16[8,128,128]{2,1,0:T(8,128)(2,1)S(1)} %get-tuple-element.16), channel_id=1, source_target_pairs={{0,1},{1,0},{2,3},{3,2},{4,5},{5,4},{6,7},{7,6},{8,9},{9,8},{10,11... | collective-permute-start | bytes 786440 | tf_op jit(solution)/shard_map/ppermute | solution.py:322
Sparse Core Ops, SparseCore 0:
  36.4 61.7 all-gather.1

commit v8 on v6

--- a/solution.py
+++ b/solution.py
@@ -50,24 +50,47 @@
     return parts[0:1, :] + parts[1:2, :] + parts[2:3, :]
 
 
-def spread_kernel(weight_ref, out_ref):
+def spread_kernel(weight_ref, out_ref, sems):
+    def copy(i):
+        return pltpu.make_async_copy(weight_ref, out_ref.at[i], sems.at[i])
+
     for i in range(out_ref.shape[0]):
-        out_ref[i] = weight_ref[...]
-
-
-def merge_kernel(in_ref, out_ref):
-    for i in range(0, in_ref.shape[0], 2):
-        pair = jnp.concatenate([in_ref[i], in_ref[i + 1]], axis=0)
-        out_ref[4 * i : 4 * i + 8, :] = pair
+        copy(i).start()
+    for i in range(out_ref.shape[0]):
+        copy(i).wait()
+
+
+def merge_kernel(in_ref, out_ref, work_ref, sems):
+    count = sems.shape[0]
+    rows = out_ref.shape[0] // count
+
+    def copy(n):
+        part = pl.ds(n * rows, rows)
+        return pltpu.make_async_copy(work_ref.at[part], out_ref.at[part], sems.at[n])
+
+    for n in range(count):
+        for row in range(n * rows, (n + 1) * rows, 8):
+            pair = jnp.concatenate([in_ref[row // 4], in_ref[row // 4 + 1]], axis=0)
+            work_ref[row : row + 8, :] = pair
+        copy(n).start()
+    for n in range(count):
+        copy(n).wait()
 
 
 def pack_kernel(core_ref, decay_ref, queries_ref, keys_ref, values_ref, own_ref, other_ref):
     first = core_ref[0] == 0
     half = (own_ref.shape[0] - 1) // 3
+    place = lax.broadcasted_iota(jnp.int32, (HD, HD), 1)
+    source = lax.broadcasted_iota(jnp.int32, (HD, HD), 0)
+    wanted = (place // 64) * 64 + (place % 32 // 4) * 8 + (place // 32 % 2) * 4 + place % 4
+    reorder = (source == wanted).astype(BF16)
     for n, ref in enumerate((keys_ref, values_ref, queries_ref)):
         for h in range(half):
             low = ref[:, h * HD : (h + 1) * HD]
             high = ref[:, (half + h) * HD : (half + h + 1) * HD]
+            if ref is values_ref:
+                low = dot(low, reorder, 1, 0).astype(BF16)
+                high = dot(high, reorder, 1, 0).astype(BF16)
             own_ref[n * half + h] = jnp.where(first, low, high)
             other_ref[n * half + h] = jnp.where(first, high, low)
     low = decay_ref[:half, :].astype(F32)
@@ -135,7 +158,7 @@
     for n, ref in enumerate((planes_ref, lines_ref)):
         for i in range(ref.shape[0]):
             later = jnp.exp(total_of(ref, i)) * state + ref[i, :rows, :].astype(F32)
-            state = jnp.where(i < place_ref[n], later, state)
+            state = jnp.where(i < place_ref[1 + n], later, state)
     for i in range(group_ref.shape[0]):
         out_ref[i] = state.astype(BF16)
         state = jnp.exp(total_of(group_ref, i)) * state + group_ref[i, :rows, :].astype(F32)
@@ -166,17 +189,12 @@
     heads = local_ref.shape[0]
     count = keep_ref.shape[1]
     scale = jnp.exp(within_cols(decays(first, own_ref, other_ref)))
-    place = lax.broadcasted_iota(jnp.int32, (HD, HD), 1)
-    source = lax.broadcasted_iota(jnp.int32, (HD, HD), 0)
-    wanted = (place // 64) * 64 + (place % 32 // 4) * 8 + (place // 32 % 2) * 4 + place % 4
-    reorder = (source == wanted).astype(BF16)
     for h in range(heads):
         queries = tokens(first, own_ref, other_ref, 2 * heads + h)
         carried = dot(queries, prior_ref[h], 1, 0) * scale[:, h : h + 1]
         combined = local_ref[h] + carried
         square = jnp.mean(combined * combined, axis=-1, keepdims=True)
         normed = (combined * lax.rsqrt(square + 1e-05)).astype(BF16)
-        normed = dot(normed, reorder, 1, 0).astype(BF16)
         keep_ref[h] = jnp.where(first, normed[:count], normed[count:])
         send_ref[h] = jnp.where(first, normed[count:], normed[:count])
 
@@ -279,18 +297,29 @@
         for z in range(chips)
         for c in range(2)
     ]
+    partner = [(i, i ^ 1) for i in range(members)]
     seq = lax.axis_index("seq")
-    place = jnp.stack([lax.div(seq, ROW), lax.div(lax.rem(seq, ROW), pairs)])
-    partner = [(i, i ^ 1) for i in range(members)]
-    core = (lax.axis_index("head") & 1).reshape(1)
+    core = lax.rem(lax.axis_index("head"), 2)
+    core = jnp.stack([core, lax.div(seq, ROW), lax.div(lax.rem(seq, ROW), pairs)])
 
     weight_rows = out_weight.shape[0]
     spread = pl.pallas_call(
-        spread_kernel, out_shape=shape(groups, weight_rows, width, kind=BF16), compiler_params=VMEM
+        spread_kernel,
+        out_shape=pltpu.HBM((groups, weight_rows, width), BF16),
+        out_specs=pl.BlockSpec(memory_space=pltpu.HBM),
+        scratch_shapes=[pltpu.SemaphoreType.DMA((groups,))],
+        compiler_params=VMEM,
     )(out_weight)
     spread = swap(spread, plane)
     spread = pl.pallas_call(
-        merge_kernel, out_shape=shape(groups * weight_rows, width, kind=BF16), compiler_params=VMEM
+        merge_kernel,
+        out_shape=pltpu.HBM((groups * weight_rows, width), BF16),
+        out_specs=pl.BlockSpec(memory_space=pltpu.HBM),
+        scratch_shapes=[
+            pltpu.VMEM((groups * weight_rows, width), BF16),
+            pltpu.SemaphoreType.DMA((4,)),
+        ],
+        compiler_params=VMEM,
     )(spread)
     weight = lax.all_gather(
         spread, ("seq", "head"), axis=0, axis_index_groups=ring, tiled=True
@@ -304,7 +333,7 @@
     group = swap(states, near)
     lines = swap(summed(group, len(far[0])), far)
     planes = swap(summed(lines, lanes), across)
-    prior = call(prior_kernel, shape(NEAR, rows, HD, kind=BF16), place, planes, lines, group)
+    prior = call(prior_kernel, shape(NEAR, rows, HD, kind=BF16), core, planes, lines, group)
     prior = swap(prior, near).reshape(half, HD, HD)
     normed = shape(half, count, HD, kind=BF16)
     kept, sent = call(norm_kernel, (normed, normed), core, own, other, local_part, prior)

time: 123 us -> 124 us (level)
  blocking collectives: 45 us -> 65.8 us
  waiting for transfers between devices: 23.4 us -> 10.9 us
  starting transfers between devices: 24.3 us -> 14.6 us
  Pallas kernels: 11.3 us -> 13.8 us
    all_to_all x2 -> x4, blocking collectives: 45 us -> 65.8 us  [swap(): lax.all_to_all(x, ('seq', 'head'), split_axis=0, concat_axis=0, axis_inde...]
    all_to_all x3 -> x1, waiting for transfers between devices: 20.3 us -> 7.84 us  [swap(): lax.all_to_all(x, ('seq', 'head'), split_axis=0, concat_axis=0, axis_inde...]
    all_to_all x3 -> x1, starting transfers between devices: 13 us -> 3.84 us  [swap(): lax.all_to_all(x, ('seq', 'head'), split_axis=0, concat_axis=0, axis_inde...]
    pallas_call x5, Pallas kernels: 4.37 us -> 6.61 us  [call(): pl.pallas_call(kernel, out_shape=out, in_specs=[smem] + [vmem] * (len(arg...]
    pallas_call x2, Pallas kernels: 1.36 us -> 0.12 us  [summed(): pl.pallas_call(group_kernel, out_shape=shape(copies, *group.shape[1:], ki...]
  transfers between devices with their start and end apart: 6 -> 4, of which waited for: 5 -> 3; matrix products, arithmetic and copies ran while one was open for 0% -> 0% of each run, Pallas kernels for 5% -> 5%
where the time goes in v8:
time: 124 us; the launch traced here: 123 us
  blocking collectives  65.8 us (53%)
  starting transfers between devices  14.6 us (12%)
  Pallas kernels  13.8 us (11%)
  between operations  13.5 us (11%)
  waiting for transfers between devices  10.9 us (9%)
  local copies, waits for them, and re-layouts  4.53 us (4%)
    all_to_all x4, blocking collectives, swap(): lax.all_to_all(x, ('seq', 'head'), split_axis=0, concat_axis=0, axis_inde...  65.8 us
    all_to_all x1, waiting for transfers between devices, swap(): lax.all_to_all(x, ('seq', 'head'), split_axis=0, concat_axis=0, axis_inde...  7.84 us
    pallas_call x5, Pallas kernels, call(): pl.pallas_call(kernel, out_shape=out, in_specs=[smem] + [vmem] * (len(arg...  6.61 us
    ppermute x1, starting transfers between devices, mix(): got = lax.ppermute(sent, 'head', partner)  5.71 us
    pallas_call x1, Pallas kernels, mix(): pl.pallas_call(project_kernel, out_shape=shape(count, width, kind=BF16),...  5.16 us
    ppermute x1, starting transfers between devices, mix(): other = lax.ppermute(other, 'head', partner)  5.04 us
    unnamed x10, local copies, waits for them, and re-layouts  4.53 us
    all_to_all x1, starting transfers between devices, swap(): lax.all_to_all(x, ('seq', 'head'), split_axis=0, concat_axis=0, axis_inde...  3.84 us
  transfers between devices with their start and end apart: 4, of which 3 were waited for; matrix products, arithmetic and copies ran while one was open for 0% of the time, Pallas kernels for 5%

profile of v8, /device:TPU:1, one launch (start us, length us, event | category | flops | bytes accessed | tf_op | source)
XLA Modules:
  0.0 123.3 jit_solution(14824849597981993481)
XLA Ops:
  6.5 0.0 all-gather.2.cloned.1.call-start
  6.5 0.0 copy-start.3
  6.5 0.7 copy-done.3
  7.3 1.1 shard_map.62
  8.3 28.2 %all_to_all.25.in_ref = bf16[32,4,2048]{2,1,0:T(4,128)(2,1)S(1)} all-to-all(bf16[32,4,2048]{2,1,0:T(4,128)(2,1)} %shard_map.62), channel_id=1, replica_groups={{0,2,4,6,8,10,12,14,128,130,132,134,136,138,140,142,256,258,260,262,264..., dimensions={0} | all-to-all | bytes 1048576 | tf_op jit(solution)/shard_map/all_to_all | solution.py:229
  36.6 0.9 shard_map.63
  37.4 0.0 all-gather.2.cloned.1.call-update
  37.5 0.1 pad_add_fusion.core_ref.place_ref
  37.5 0.0 copy-start
  37.5 1.0 copy-done
  38.6 0.0 copy-start.1
  38.6 1.0 copy-done.1
  39.6 0.0 copy-start.2
  39.6 1.0 copy-done.2
  40.7 0.0 copy-start.4
  40.7 0.7 copy-done.4
  41.4 0.9 shard_map.55
  42.3 5.0 %collective-permute-start = (bf16[25,128,128]{2,1,0:T(8,128)(2,1)S(1)}, bf16[25,128,128]{2,1,0:T(8,128)(2,1)S(1)}, u32[]{:S(2)}, u32[]{:S(2)}) collective-permute-start(bf16[25,128,128]{2,1,0:T(8,128)(2,1)S(1)} %get-tuple-element.10), channel_id=1, source_target_pairs={{0,1},{1,0},{2,3},{3,2},{4,5},{5,4},{6,7},{7,6},{8,9},{9,8},{10,11... | collective-permute-start | bytes 2457608 | tf_op jit(solution)/shard_map/ppermute | solution.py:330
  47.4 1.9 %collective-permute-done.other_ref = bf16[25,128,128]{2,1,0:T(8,128)(2,1)S(1)} collective-permute-done((bf16[25,128,128]{2,1,0:T(8,128)(2,1)S(1)}, bf16[25,128,128]{2,1,0:T(8,128)(2,1)S(1)}, u32[]{:S(2)}, u32[]{:S(2)}) %collective-permute-start) | collective-permute-done | bytes 819232 | tf_op jit(solution)/shard_map/ppermute | solution.py:330
  49.3 1.1 shard_map.57
  50.4 17.0 %all_to_all.26.group_ref = bf16[16,72,128]{2,1,0:T(8,128)(2,1)S(1)} all-to-all(bf16[16,72,128]{2,1,0:T(8,128)(2,1)S(1)} %shard_map.57), channel_id=1, replica_groups={{0,2,4,6,8,10,12,14,16,18,20,22,24,26,28,30},{1,3,5,7,9,11,13,15,17,19,..., dimensions={0} | all-to-all | bytes 589824 | tf_op jit(solution)/shard_map/all_to_all | solution.py:229
  67.4 0.1 shard_map.58
  67.5 13.7 %all_to_all.27.group_ref.lines_ref = bf16[4,72,128]{2,1,0:T(8,128)(2,1)S(1)} all-to-all(bf16[4,72,128]{2,1,0:T(8,128)(2,1)S(1)} %shard_map.58), channel_id=1, replica_groups={{0,32,64,96},{1,33,65,97},{2,34,66,98},{3,35,67,99},{4,36,68,100},{5,37..., dimensions={0} | all-to-all | bytes 147456 | tf_op jit(solution)/shard_map/all_to_all | solution.py:229
  81.2 6.9 %all_to_all.28.planes_ref = bf16[4,72,128]{2,1,0:T(8,128)(2,1)S(1)} all-to-all(bf16[4,72,128]{2,1,0:T(8,128)(2,1)S(1)} %shard_map.59), channel_id=1, replica_groups={{0,128,256,384},{1,129,257,385},{2,130,258,386},{3,131,259,387},{4,132,..., dimensions={0} | all-to-all | bytes 147456 | tf_op jit(solution)/shard_map/all_to_all | solution.py:229
  88.2 1.4 %shard_map.60 = bf16[16,64,128]{2,1,0:T(8,128)(2,1)} custom-call(s32[3]{0:T(128)S(1)} %pad_add_fusion.core_ref.place_ref, bf16[4,72,128]{2,1,0:T(8,128)(2,1)S(1)} %all_to_all.28.planes_ref, bf16[4,72,128]{2,1,0:T(8,128)(2,1)S(1)} %all_to_all.27.group_ref.lines_ref, bf16[16,72,128]{2,1,0:T(8,128)(2,1)S(1)} %all_to_all.26.group_ref), custom_call_target="tpu_custom_call" | custom-call | tf_op jit(solution)/shard_map/pallas_call | solution.py:249
  89.5 3.8 %all-to-all-start.3 = ((bf16[16,64,128]{2,1,0:T(8,128)(2,1)}), bf16[16,64,128]{2,1,0:T(8,128)(2,1)S(1)}, u32[]{:S(2)}, u32[]{:S(2)}) async-start(bf16[16,64,128]{2,1,0:T(8,128)(2,1)} %shard_map.60), calls=%async_computation.3 | async-start | bytes 524288 | tf_op jit(solution)/shard_map/all_to_all | solution.py:229
  93.4 1.5 %shard_map.56.local_ref = f32[8,256,128]{2,1,0:T(8,128)S(1)} custom-call(s32[3]{0:T(128)S(1)} %pad_add_fusion.core_ref.place_ref, bf16[25,128,128]{2,1,0:T(8,128)(2,1)S(1)} %get-tuple-element.9.own_ref, bf16[25,128,128]{2,1,0:T(8,128)(2,1)S(1)} %collective-permute-done.other_ref), custom_call_target="tpu_custom_call" | custom-call | tf_op jit(solution)/shard_map/pallas_call | solution.py:249
  94.9 7.8 %all-to-all-done.3 = bf16[16,64,128]{2,1,0:T(8,128)(2,1)S(1)} async-done(((bf16[16,64,128]{2,1,0:T(8,128)(2,1)}), bf16[16,64,128]{2,1,0:T(8,128)(2,1)S(1)}, u32[]{:S(2)}, u32[]{:S(2)}) %all-to-all-start.3) | async-done | bytes 262176 | tf_op jit(solution)/shard_map/all_to_all | solution.py:229
  102.7 1.7 %shard_map.61 = (bf16[8,128,128]{2,1,0:T(8,128)(2,1)S(1)}, bf16[8,128,128]{2,1,0:T(8,128)(2,1)S(1)}) custom-call(s32[3]{0:T(128)S(1)} %pad_add_fusion.core_ref.place_ref, bf16[25,128,128]{2,1,0:T(8,128)(2,1)S(1)} %get-tuple-element.9.own_ref, bf16[25,128,128]{2,1,0:T(8,128)(2,1)S(1)} %collective-permute-done.other_ref, ...), custom_call_target="tpu_custom_call" | custom-call | tf_op jit(solution)/shard_map/pallas_call | solution.py:249
  104.4 5.7 %collective-permute-start.1 = (bf16[8,128,128]{2,1,0:T(8,128)(2,1)S(1)}, bf16[8,128,128]{2,1,0:T(8,128)(2,1)S(1)}, u32[]{:S(2)}, u32[]{:S(2)}) collective-permute-start(bf16[8,128,128]{2,1,0:T(8,128)(2,1)S(1)} %get-tuple-element.12), channel_id=1, source_target_pairs={{0,1},{1,0},{2,3},{3,2},{4,5},{5,4},{6,7},{7,6},{8,9},{9,8},{10,11... | collective-permute-start | bytes 786440 | tf_op jit(solution)/shard_map/ppermute | solution.py:340
  110.1 1.1 collective-permute-done.1.got_ref
  111.3 0.0 all-gather.2.cloned.1.call-done
  111.3 5.2 %shard_map.64 = bf16[128,2048]{1,0:T(8,128)(2,1)} custom-call(s32[3]{0:T(128)S(1)} %pad_add_fusion.core_ref.place_ref, bf16[8,128,128]{2,1,0:T(8,128)(2,1)S(1)} %get-tuple-element.11.kept_ref, bf16[8,128,128]{2,1,0:T(8,128)(2,1)S(1)} %collective-permute-done.1.got_ref, bf16[4,4,4,32,2048]{4,3,2,1,0:T(8,128)(2,1)} %bitcast.8), custom_call_target="tpu_custom_call" | custom-call | tf_op jit(solution)/shard_map/pallas_call | solution.py:345
  (1 shorter events, 0.0 us)
Async XLA Ops:
  6.5 104.7 %all-gather.2.cloned.1.call-start = ((), (), s32[]{:S(2)}) async-start(), calls=%async_computation.5 | async-start | bytes 8912896 | tf_op jit(solution)/shard_map/all_gather | solution.py:324
  6.5 0.7 copy-start.3
  37.5 1.0 copy-start
  38.6 1.0 copy-start.1
  39.6 1.0 copy-start.2
  40.7 0.7 copy-start.4
  42.3 7.0 %collective-permute-start = (bf16[25,128,128]{2,1,0:T(8,128)(2,1)S(1)}, bf16[25,128,128]{2,1,0:T(8,128)(2,1)S(1)}, u32[]{:S(2)}, u32[]{:S(2)}) collective-permute-start(bf16[25,128,128]{2,1,0:T(8,128)(2,1)S(1)} %get-tuple-element.10), channel_id=1, source_target_pairs={{0,1},{1,0},{2,3},{3,2},{4,5},{5,4},{6,7},{7,6},{8,9},{9,8},{10,11... | collective-permute-start | bytes 2457608 | tf_op jit(solution)/shard_map/ppermute | solution.py:330
  89.5 13.1 %all-to-all-start.3 = ((bf16[16,64,128]{2,1,0:T(8,128)(2,1)}), bf16[16,64,128]{2,1,0:T(8,128)(2,1)S(1)}, u32[]{:S(2)}, u32[]{:S(2)}) async-start(bf16[16,64,128]{2,1,0:T(8,128)(2,1)} %shard_map.60), calls=%async_computation.3 | async-start | bytes 524288 | tf_op jit(solution)/shard_map/all_to_all | solution.py:229
  104.4 6.9 %collective-permute-start.1 = (bf16[8,128,128]{2,1,0:T(8,128)(2,1)S(1)}, bf16[8,128,128]{2,1,0:T(8,128)(2,1)S(1)}, u32[]{:S(2)}, u32[]{:S(2)}) collective-permute-start(bf16[8,128,128]{2,1,0:T(8,128)(2,1)S(1)} %get-tuple-element.12), channel_id=1, source_target_pairs={{0,1},{1,0},{2,3},{3,2},{4,5},{5,4},{6,7},{7,6},{8,9},{9,8},{10,11... | collective-permute-start | bytes 786440 | tf_op jit(solution)/shard_map/ppermute | solution.py:340
Sparse Core Ops, SparseCore 0:
  37.6 62.3 all-gather.1

commit v9 on v8

--- a/solution.py
+++ b/solution.py
@@ -50,14 +50,9 @@
     return parts[0:1, :] + parts[1:2, :] + parts[2:3, :]
 
 
-def spread_kernel(weight_ref, out_ref, sems):
-    def copy(i):
-        return pltpu.make_async_copy(weight_ref, out_ref.at[i], sems.at[i])
-
+def spread_kernel(weight_ref, out_ref):
     for i in range(out_ref.shape[0]):
-        copy(i).start()
-    for i in range(out_ref.shape[0]):
-        copy(i).wait()
+        out_ref[i] = weight_ref[...]
 
 
 def merge_kernel(in_ref, out_ref, work_ref, sems):
@@ -77,7 +72,7 @@
         copy(n).wait()
 
 
-def pack_kernel(core_ref, decay_ref, queries_ref, keys_ref, values_ref, own_ref, other_ref):
+def pack_kernel(core_ref, plane_ref, line_ref, decay_ref, queries_ref, keys_ref, values_ref, own_ref, other_ref):
     first = core_ref[0] == 0
     half = (own_ref.shape[0] - 1) // 3
     place = lax.broadcasted_iota(jnp.int32, (HD, HD), 1)
@@ -152,13 +147,13 @@
         out_ref[j, rows:, :] = parts
 
 
-def prior_kernel(place_ref, planes_ref, lines_ref, group_ref, out_ref):
+def prior_kernel(plane_ref, line_ref, planes_ref, lines_ref, group_ref, out_ref):
     rows = out_ref.shape[1]
     state = jnp.zeros((rows, HD), F32)
-    for n, ref in enumerate((planes_ref, lines_ref)):
+    for place_ref, ref in ((plane_ref, planes_ref), (line_ref, lines_ref)):
         for i in range(ref.shape[0]):
             later = jnp.exp(total_of(ref, i)) * state + ref[i, :rows, :].astype(F32)
-            state = jnp.where(i < place_ref[1 + n], later, state)
+            state = jnp.where(i < place_ref[0], later, state)
     for i in range(group_ref.shape[0]):
         out_ref[i] = state.astype(BF16)
         state = jnp.exp(total_of(group_ref, i)) * state + group_ref[i, :rows, :].astype(F32)
@@ -249,7 +244,7 @@
     return pl.pallas_call(
         kernel,
         out_shape=out,
-        in_specs=[smem] + [vmem] * (len(args) - 1),
+        in_specs=[smem if a.dtype == jnp.int32 else vmem for a in args],
         out_specs=jax.tree.map(lambda _: vmem, out),
         compiler_params=VMEM,
         **options,
@@ -300,15 +295,14 @@
     partner = [(i, i ^ 1) for i in range(members)]
     seq = lax.axis_index("seq")
     core = lax.rem(lax.axis_index("head"), 2)
-    core = jnp.stack([core, lax.div(seq, ROW), lax.div(lax.rem(seq, ROW), pairs)])
+    core = core.reshape(1)
+    plane_place = lax.div(seq, ROW).reshape(1)
+    line_place = lax.div(lax.rem(seq, ROW), pairs).reshape(1)
+    places = (plane_place, line_place)
 
     weight_rows = out_weight.shape[0]
     spread = pl.pallas_call(
-        spread_kernel,
-        out_shape=pltpu.HBM((groups, weight_rows, width), BF16),
-        out_specs=pl.BlockSpec(memory_space=pltpu.HBM),
-        scratch_shapes=[pltpu.SemaphoreType.DMA((groups,))],
-        compiler_params=VMEM,
+        spread_kernel, out_shape=shape(groups, weight_rows, width, kind=BF16), compiler_params=VMEM
     )(out_weight)
     spread = swap(spread, plane)
     spread = pl.pallas_call(
@@ -326,14 +320,14 @@
     )
 
     pair = shape(3 * half + 1, count, HD, kind=BF16)
-    own, other = call(pack_kernel, (pair, pair), core, decay_t, queries, keys, values)
+    own, other = call(pack_kernel, (pair, pair), core, *places, decay_t, queries, keys, values)
     other = lax.ppermute(other, "head", partner)
     states = call(states_kernel, shape(NEAR, rows + PAD, HD, kind=BF16), core, own, other)
     local_part = call(local_kernel, shape(half, 2 * count, HD), core, own, other)
     group = swap(states, near)
     lines = swap(summed(group, len(far[0])), far)
     planes = swap(summed(lines, lanes), across)
-    prior = call(prior_kernel, shape(NEAR, rows, HD, kind=BF16), core, planes, lines, group)
+    prior = call(prior_kernel, shape(NEAR, rows, HD, kind=BF16), *places, planes, lines, group)
     prior = swap(prior, near).reshape(half, HD, HD)
     normed = shape(half, count, HD, kind=BF16)
     kept, sent = call(norm_kernel, (normed, normed), core, own, other, local_part, prior)

time: 124 us -> 120 us (0.968)
  Pallas kernels: 13.8 us -> 9.48 us
    pallas_call x6, Pallas kernels: 7.67 us -> 3.89 us  [the longest x5 3.86 us: call(): pl.pallas_call(kernel, out_shape=out, in_specs=[smem if a.dtype == jnp.in...]
  transfers between devices with their start and end apart: 4 -> 4, of which waited for: 3 -> 3; matrix products, arithmetic and copies ran while one was open for 0% -> 0% of each run, Pallas kernels for 5% -> 3%
where the time goes in v9:
time: 120 us
  blocking collectives  65.6 us (55%)
  starting transfers between devices  14.5 us (12%)
  between operations  13.5 us (11%)
  waiting for transfers between devices  12.1 us (10%)
  Pallas kernels  9.48 us (8%)
  local copies, waits for them, and re-layouts  4.52 us (4%)
    all_to_all x4, blocking collectives, swap(): lax.all_to_all(x, ('seq', 'head'), split_axis=0, concat_axis=0, axis_inde...  65.6 us
    all_to_all x1, waiting for transfers between devices, swap(): lax.all_to_all(x, ('seq', 'head'), split_axis=0, concat_axis=0, axis_inde...  8.97 us
    ppermute x1, starting transfers between devices, mix(): got = lax.ppermute(sent, 'head', partner)  5.66 us
    ppermute x1, starting transfers between devices, mix(): other = lax.ppermute(other, 'head', partner)  5.04 us
    pallas_call x1, Pallas kernels, mix(): pl.pallas_call(project_kernel, out_shape=shape(count, width, kind=BF16),...  4.61 us
    unnamed x10, local copies, waits for them, and re-layouts  4.52 us
    pallas_call x5, Pallas kernels, call(): pl.pallas_call(kernel, out_shape=out, in_specs=[smem if a.dtype == jnp.in...  3.86 us
    all_to_all x1, starting transfers between devices, swap(): lax.all_to_all(x, ('seq', 'head'), split_axis=0, concat_axis=0, axis_inde...  3.83 us
  transfers between devices with their start and end apart: 4, of which 3 were waited for; matrix products, arithmetic and copies ran while one was open for 0% of the time, Pallas kernels for 3%

profile of v9, /device:TPU:1, one launch (start us, length us, event | category | flops | bytes accessed | tf_op | source)
XLA Modules:
  0.0 119.8 jit_solution(13596727815873863569)
XLA Ops:
  6.5 0.0 all-gather.2.cloned.1.call-start
  6.5 0.0 copy-start.3
  6.5 0.7 copy-done.3
  7.3 28.0 %all_to_all.25.in_ref = bf16[32,4,2048]{2,1,0:T(4,128)(2,1)S(1)} all-to-all(bf16[32,4,2048]{2,1,0:T(4,128)(2,1)S(1)} %shard_map.62), channel_id=1, replica_groups={{0,2,4,6,8,10,12,14,128,130,132,134,136,138,140,142,256,258,260,262,264..., dimensions={0} | all-to-all | bytes 1048576 | tf_op jit(solution)/shard_map/all_to_all | solution.py:224
  35.3 0.9 shard_map.63
  36.2 0.0 all-gather.2.cloned.1.call-update
  36.2 0.0 copy-start
  36.2 1.0 copy-done
  37.3 0.0 copy-start.1
  37.3 1.0 copy-done.1
  38.3 0.0 copy-start.2
  38.3 1.0 copy-done.2
  39.4 0.0 copy-start.4
  39.4 0.7 copy-done.4
  40.0 0.4 shard_map.55
  40.5 5.0 %collective-permute-start = (bf16[25,128,128]{2,1,0:T(8,128)(2,1)S(1)}, bf16[25,128,128]{2,1,0:T(8,128)(2,1)S(1)}, u32[]{:S(2)}, u32[]{:S(2)}) collective-permute-start(bf16[25,128,128]{2,1,0:T(8,128)(2,1)S(1)} %get-tuple-element.10), channel_id=1, source_target_pairs={{0,1},{1,0},{2,3},{3,2},{4,5},{5,4},{6,7},{7,6},{8,9},{9,8},{10,11... | collective-permute-start | bytes 2457608 | tf_op jit(solution)/shard_map/ppermute | solution.py:324
  45.5 1.9 %collective-permute-done.other_ref = bf16[25,128,128]{2,1,0:T(8,128)(2,1)S(1)} collective-permute-done((bf16[25,128,128]{2,1,0:T(8,128)(2,1)S(1)}, bf16[25,128,128]{2,1,0:T(8,128)(2,1)S(1)}, u32[]{:S(2)}, u32[]{:S(2)}) %collective-permute-start) | collective-permute-done | bytes 819232 | tf_op jit(solution)/shard_map/ppermute | solution.py:324
  47.4 0.6 shard_map.57
  48.0 17.0 %all_to_all.26.group_ref = bf16[16,72,128]{2,1,0:T(8,128)(2,1)S(1)} all-to-all(bf16[16,72,128]{2,1,0:T(8,128)(2,1)S(1)} %shard_map.57), channel_id=1, replica_groups={{0,2,4,6,8,10,12,14,16,18,20,22,24,26,28,30},{1,3,5,7,9,11,13,15,17,19,..., dimensions={0} | all-to-all | bytes 589824 | tf_op jit(solution)/shard_map/all_to_all | solution.py:224
  65.0 0.1 shard_map.58
  65.1 13.7 %all_to_all.27.group_ref.lines_ref = bf16[4,72,128]{2,1,0:T(8,128)(2,1)S(1)} all-to-all(bf16[4,72,128]{2,1,0:T(8,128)(2,1)S(1)} %shard_map.58), channel_id=1, replica_groups={{0,32,64,96},{1,33,65,97},{2,34,66,98},{3,35,67,99},{4,36,68,100},{5,37..., dimensions={0} | all-to-all | bytes 147456 | tf_op jit(solution)/shard_map/all_to_all | solution.py:224
  78.8 6.9 %all_to_all.28.planes_ref = bf16[4,72,128]{2,1,0:T(8,128)(2,1)S(1)} all-to-all(bf16[4,72,128]{2,1,0:T(8,128)(2,1)S(1)} %shard_map.59), channel_id=1, replica_groups={{0,128,256,384},{1,129,257,385},{2,130,258,386},{3,131,259,387},{4,132,..., dimensions={0} | all-to-all | bytes 147456 | tf_op jit(solution)/shard_map/all_to_all | solution.py:224
  85.8 0.8 shard_map.60
  86.6 3.8 %all-to-all-start.3 = ((bf16[16,64,128]{2,1,0:T(8,128)(2,1)}), bf16[16,64,128]{2,1,0:T(8,128)(2,1)S(1)}, u32[]{:S(2)}, u32[]{:S(2)}) async-start(bf16[16,64,128]{2,1,0:T(8,128)(2,1)} %shard_map.60), calls=%async_computation.3 | async-start | bytes 524288 | tf_op jit(solution)/shard_map/all_to_all | solution.py:224
  90.5 0.9 shard_map.56.local_ref
  91.4 9.0 %all-to-all-done.3 = bf16[16,64,128]{2,1,0:T(8,128)(2,1)S(1)} async-done(((bf16[16,64,128]{2,1,0:T(8,128)(2,1)}), bf16[16,64,128]{2,1,0:T(8,128)(2,1)S(1)}, u32[]{:S(2)}, u32[]{:S(2)}) %all-to-all-start.3) | async-done | bytes 262176 | tf_op jit(solution)/shard_map/all_to_all | solution.py:224
  100.3 1.1 shard_map.61
  101.5 5.7 %collective-permute-start.1 = (bf16[8,128,128]{2,1,0:T(8,128)(2,1)S(1)}, bf16[8,128,128]{2,1,0:T(8,128)(2,1)S(1)}, u32[]{:S(2)}, u32[]{:S(2)}) collective-permute-start(bf16[8,128,128]{2,1,0:T(8,128)(2,1)S(1)} %get-tuple-element.12), channel_id=1, source_target_pairs={{0,1},{1,0},{2,3},{3,2},{4,5},{5,4},{6,7},{7,6},{8,9},{9,8},{10,11... | collective-permute-start | bytes 786440 | tf_op jit(solution)/shard_map/ppermute | solution.py:334
  107.1 1.1 collective-permute-done.1.got_ref
  108.3 0.0 all-gather.2.cloned.1.call-done
  108.3 4.6 %shard_map.64 = bf16[128,2048]{1,0:T(8,128)(2,1)} custom-call(s32[1]{0:T(128)} %bitcast.core_ref, bf16[8,128,128]{2,1,0:T(8,128)(2,1)S(1)} %get-tuple-element.11.kept_ref, bf16[8,128,128]{2,1,0:T(8,128)(2,1)S(1)} %collective-permute-done.1.got_ref, bf16[4,4,4,32,2048]{4,3,2,1,0:T(8,128)(2,1)} %bitcast.8), custom_call_target="tpu_custom_call" | custom-call | tf_op jit(solution)/shard_map/pallas_call | solution.py:339
  (2 shorter events, 0.1 us)
Async XLA Ops:
  6.5 101.7 %all-gather.2.cloned.1.call-start = ((), (), s32[]{:S(2)}) async-start(), calls=%async_computation.5 | async-start | bytes 8912896 | tf_op jit(solution)/shard_map/all_gather | solution.py:318
  6.5 0.7 copy-start.3
  36.2 1.0 copy-start
  37.3 1.0 copy-start.1
  38.3 1.0 copy-start.2
  39.4 0.7 copy-start.4
  40.5 7.0 %collective-permute-start = (bf16[25,128,128]{2,1,0:T(8,128)(2,1)S(1)}, bf16[25,128,128]{2,1,0:T(8,128)(2,1)S(1)}, u32[]{:S(2)}, u32[]{:S(2)}) collective-permute-start(bf16[25,128,128]{2,1,0:T(8,128)(2,1)S(1)} %get-tuple-element.10), channel_id=1, source_target_pairs={{0,1},{1,0},{2,3},{3,2},{4,5},{5,4},{6,7},{7,6},{8,9},{9,8},{10,11... | collective-permute-start | bytes 2457608 | tf_op jit(solution)/shard_map/ppermute | solution.py:324
  86.6 13.7 %all-to-all-start.3 = ((bf16[16,64,128]{2,1,0:T(8,128)(2,1)}), bf16[16,64,128]{2,1,0:T(8,128)(2,1)S(1)}, u32[]{:S(2)}, u32[]{:S(2)}) async-start(bf16[16,64,128]{2,1,0:T(8,128)(2,1)} %shard_map.60), calls=%async_computation.3 | async-start | bytes 524288 | tf_op jit(solution)/shard_map/all_to_all | solution.py:224
  101.5 6.8 %collective-permute-start.1 = (bf16[8,128,128]{2,1,0:T(8,128)(2,1)S(1)}, bf16[8,128,128]{2,1,0:T(8,128)(2,1)S(1)}, u32[]{:S(2)}, u32[]{:S(2)}) collective-permute-start(bf16[8,128,128]{2,1,0:T(8,128)(2,1)S(1)} %get-tuple-element.12), channel_id=1, source_target_pairs={{0,1},{1,0},{2,3},{3,2},{4,5},{5,4},{6,7},{7,6},{8,9},{9,8},{10,11... | collective-permute-start | bytes 786440 | tf_op jit(solution)/shard_map/ppermute | solution.py:334
Sparse Core Ops, SparseCore 0:
  36.3 62.9 all-gather.1

commit v10 on v9

--- a/solution.py
+++ b/solution.py
@@ -159,12 +159,13 @@
         state = jnp.exp(total_of(group_ref, i)) * state + group_ref[i, :rows, :].astype(F32)
 
 
-def local_kernel(core_ref, own_ref, other_ref, out_ref):
+def local_kernel(core_ref, own_ref, other_ref, out_ref, scale_ref):
     first = core_ref[0] == 0
     heads, count, _ = out_ref.shape
     decay_t = decays(first, own_ref, other_ref)
     rows = within_rows(decay_t)
     cols = within_cols(decay_t)
+    scale_ref[...] = jnp.exp(cols)
     causal = lax.broadcasted_iota(jnp.int32, (count, count), 0) >= lax.broadcasted_iota(
         jnp.int32, (count, count), 1
     )
@@ -179,11 +180,13 @@
         out_ref[h] = dot(weights, values, 1, 0)
 
 
-def norm_kernel(core_ref, own_ref, other_ref, local_ref, prior_ref, keep_ref, send_ref):
+def norm_kernel(
+    core_ref, own_ref, other_ref, local_ref, scale_ref, prior_ref, keep_ref, send_ref
+):
     first = core_ref[0] == 0
     heads = local_ref.shape[0]
     count = keep_ref.shape[1]
-    scale = jnp.exp(within_cols(decays(first, own_ref, other_ref)))
+    scale = scale_ref[...]
     for h in range(heads):
         queries = tokens(first, own_ref, other_ref, 2 * heads + h)
         carried = dot(queries, prior_ref[h], 1, 0) * scale[:, h : h + 1]
@@ -323,14 +326,15 @@
     own, other = call(pack_kernel, (pair, pair), core, *places, decay_t, queries, keys, values)
     other = lax.ppermute(other, "head", partner)
     states = call(states_kernel, shape(NEAR, rows + PAD, HD, kind=BF16), core, own, other)
-    local_part = call(local_kernel, shape(half, 2 * count, HD), core, own, other)
+    parts = (shape(half, 2 * count, HD), shape(2 * count, half))
+    local_part, scale = call(local_kernel, parts, core, own, other)
     group = swap(states, near)
     lines = swap(summed(group, len(far[0])), far)
     planes = swap(summed(lines, lanes), across)
     prior = call(prior_kernel, shape(NEAR, rows, HD, kind=BF16), *places, planes, lines, group)
     prior = swap(prior, near).reshape(half, HD, HD)
     normed = shape(half, count, HD, kind=BF16)
-    kept, sent = call(norm_kernel, (normed, normed), core, own, other, local_part, prior)
+    kept, sent = call(norm_kernel, (normed, normed), core, own, other, local_part, scale, prior)
     got = lax.ppermute(sent, "head", partner)
     run = chips * weight_rows
     weight = weight.reshape(ROW // 2, 4, lanes, run, width)

time: 120 us -> 120 us (level)
  no operation moved by 1% of the time
where the time goes in v10:
time: 120 us
  blocking collectives  65.6 us (55%)
  starting transfers between devices  14.5 us (12%)
  between operations  13.5 us (11%)
  waiting for transfers between devices  12.1 us (10%)
  Pallas kernels  9.38 us (8%)
  local copies, waits for them, and re-layouts  4.52 us (4%)
    all_to_all x4, blocking collectives, swap(): lax.all_to_all(x, ('seq', 'head'), split_axis=0, concat_axis=0, axis_inde...  65.6 us
    all_to_all x1, waiting for transfers between devices, swap(): lax.all_to_all(x, ('seq', 'head'), split_axis=0, concat_axis=0, axis_inde...  8.98 us
    ppermute x1, starting transfers between devices, mix(): got = lax.ppermute(sent, 'head', partner)  5.66 us
    ppermute x1, starting transfers between devices, mix(): other = lax.ppermute(other, 'head', partner)  5.04 us
    pallas_call x1, Pallas kernels, mix(): pl.pallas_call(project_kernel, out_shape=shape(count, width, kind=BF16),...  4.61 us
    unnamed x10, local copies, waits for them, and re-layouts  4.52 us
    all_to_all x1, starting transfers between devices, swap(): lax.all_to_all(x, ('seq', 'head'), split_axis=0, concat_axis=0, axis_inde...  3.83 us
    pallas_call x5, Pallas kernels, call(): pl.pallas_call(kernel, out_shape=out, in_specs=[smem if a.dtype == jnp.in...  3.76 us
  transfers between devices with their start and end apart: 4, of which 3 were waited for; matrix products, arithmetic and copies ran while one was open for 0% of the time, Pallas kernels for 3%

profile of v10, /device:TPU:1, one launch (start us, length us, event | category | flops | bytes accessed | tf_op | source)
XLA Modules:
  0.0 119.7 jit_solution(17106056421554438302)
XLA Ops:
  6.5 0.0 all-gather.2.cloned.1.call-start
  6.5 0.0 copy-start.3
  6.5 0.7 copy-done.3
  7.3 28.0 %all_to_all.25.in_ref = bf16[32,4,2048]{2,1,0:T(4,128)(2,1)S(1)} all-to-all(bf16[32,4,2048]{2,1,0:T(4,128)(2,1)S(1)} %shard_map.62), channel_id=1, replica_groups={{0,2,4,6,8,10,12,14,128,130,132,134,136,138,140,142,256,258,260,262,264..., dimensions={0} | all-to-all | bytes 1048576 | tf_op jit(solution)/shard_map/all_to_all | solution.py:227
  35.3 0.9 shard_map.63
  36.2 0.0 all-gather.2.cloned.1.call-update
  36.2 0.0 copy-start
  36.2 1.0 copy-done
  37.3 0.0 copy-start.1
  37.3 1.0 copy-done.1
  38.3 0.0 copy-start.2
  38.3 1.0 copy-done.2
  39.4 0.0 copy-start.4
  39.4 0.7 copy-done.4
  40.0 0.4 shard_map.55
  40.5 5.0 %collective-permute-start = (bf16[25,128,128]{2,1,0:T(8,128)(2,1)S(1)}, bf16[25,128,128]{2,1,0:T(8,128)(2,1)S(1)}, u32[]{:S(2)}, u32[]{:S(2)}) collective-permute-start(bf16[25,128,128]{2,1,0:T(8,128)(2,1)S(1)} %get-tuple-element.12), channel_id=1, source_target_pairs={{0,1},{1,0},{2,3},{3,2},{4,5},{5,4},{6,7},{7,6},{8,9},{9,8},{10,11... | collective-permute-start | bytes 2457608 | tf_op jit(solution)/shard_map/ppermute | solution.py:327
  45.5 1.9 %collective-permute-done.other_ref = bf16[25,128,128]{2,1,0:T(8,128)(2,1)S(1)} collective-permute-done((bf16[25,128,128]{2,1,0:T(8,128)(2,1)S(1)}, bf16[25,128,128]{2,1,0:T(8,128)(2,1)S(1)}, u32[]{:S(2)}, u32[]{:S(2)}) %collective-permute-start) | collective-permute-done | bytes 819232 | tf_op jit(solution)/shard_map/ppermute | solution.py:327
  47.4 0.6 shard_map.57
  48.0 17.0 %all_to_all.26.group_ref = bf16[16,72,128]{2,1,0:T(8,128)(2,1)S(1)} all-to-all(bf16[16,72,128]{2,1,0:T(8,128)(2,1)S(1)} %shard_map.57), channel_id=1, replica_groups={{0,2,4,6,8,10,12,14,16,18,20,22,24,26,28,30},{1,3,5,7,9,11,13,15,17,19,..., dimensions={0} | all-to-all | bytes 589824 | tf_op jit(solution)/shard_map/all_to_all | solution.py:227
  65.0 0.1 shard_map.58
  65.1 13.7 %all_to_all.27.group_ref.lines_ref = bf16[4,72,128]{2,1,0:T(8,128)(2,1)S(1)} all-to-all(bf16[4,72,128]{2,1,0:T(8,128)(2,1)S(1)} %shard_map.58), channel_id=1, replica_groups={{0,32,64,96},{1,33,65,97},{2,34,66,98},{3,35,67,99},{4,36,68,100},{5,37..., dimensions={0} | all-to-all | bytes 147456 | tf_op jit(solution)/shard_map/all_to_all | solution.py:227
  78.8 6.9 %all_to_all.28.planes_ref = bf16[4,72,128]{2,1,0:T(8,128)(2,1)S(1)} all-to-all(bf16[4,72,128]{2,1,0:T(8,128)(2,1)S(1)} %shard_map.59), channel_id=1, replica_groups={{0,128,256,384},{1,129,257,385},{2,130,258,386},{3,131,259,387},{4,132,..., dimensions={0} | all-to-all | bytes 147456 | tf_op jit(solution)/shard_map/all_to_all | solution.py:227
  85.8 0.8 shard_map.60
  86.6 3.8 %all-to-all-start.3 = ((bf16[16,64,128]{2,1,0:T(8,128)(2,1)}), bf16[16,64,128]{2,1,0:T(8,128)(2,1)S(1)}, u32[]{:S(2)}, u32[]{:S(2)}) async-start(bf16[16,64,128]{2,1,0:T(8,128)(2,1)} %shard_map.60), calls=%async_computation.3 | async-start | bytes 524288 | tf_op jit(solution)/shard_map/all_to_all | solution.py:227
  90.5 0.9 shard_map.56
  91.4 9.0 %all-to-all-done.3 = bf16[16,64,128]{2,1,0:T(8,128)(2,1)S(1)} async-done(((bf16[16,64,128]{2,1,0:T(8,128)(2,1)}), bf16[16,64,128]{2,1,0:T(8,128)(2,1)S(1)}, u32[]{:S(2)}, u32[]{:S(2)}) %all-to-all-start.3) | async-done | bytes 262176 | tf_op jit(solution)/shard_map/all_to_all | solution.py:227
  100.3 1.0 shard_map.61
  101.4 5.7 %collective-permute-start.1 = (bf16[8,128,128]{2,1,0:T(8,128)(2,1)S(1)}, bf16[8,128,128]{2,1,0:T(8,128)(2,1)S(1)}, u32[]{:S(2)}, u32[]{:S(2)}) collective-permute-start(bf16[8,128,128]{2,1,0:T(8,128)(2,1)S(1)} %get-tuple-element.16), channel_id=1, source_target_pairs={{0,1},{1,0},{2,3},{3,2},{4,5},{5,4},{6,7},{7,6},{8,9},{9,8},{10,11... | collective-permute-start | bytes 786440 | tf_op jit(solution)/shard_map/ppermute | solution.py:338
  107.0 1.1 collective-permute-done.1.got_ref
  108.2 0.0 all-gather.2.cloned.1.call-done
  108.2 4.6 %shard_map.64 = bf16[128,2048]{1,0:T(8,128)(2,1)} custom-call(s32[1]{0:T(128)} %bitcast.core_ref, bf16[8,128,128]{2,1,0:T(8,128)(2,1)S(1)} %get-tuple-element.15.kept_ref, bf16[8,128,128]{2,1,0:T(8,128)(2,1)S(1)} %collective-permute-done.1.got_ref, bf16[4,4,4,32,2048]{4,3,2,1,0:T(8,128)(2,1)} %bitcast.8), custom_call_target="tpu_custom_call" | custom-call | tf_op jit(solution)/shard_map/pallas_call | solution.py:343
  (2 shorter events, 0.1 us)
Async XLA Ops:
  6.5 101.6 %all-gather.2.cloned.1.call-start = ((), (), s32[]{:S(2)}) async-start(), calls=%async_computation.5 | async-start | bytes 8912896 | tf_op jit(solution)/shard_map/all_gather | solution.py:321
  6.5 0.7 copy-start.3
  36.2 1.0 copy-start
  37.3 1.0 copy-start.1
  38.3 1.0 copy-start.2
  39.4 0.7 copy-start.4
  40.5 7.0 %collective-permute-start = (bf16[25,128,128]{2,1,0:T(8,128)(2,1)S(1)}, bf16[25,128,128]{2,1,0:T(8,128)(2,1)S(1)}, u32[]{:S(2)}, u32[]{:S(2)}) collective-permute-start(bf16[25,128,128]{2,1,0:T(8,128)(2,1)S(1)} %get-tuple-element.12), channel_id=1, source_target_pairs={{0,1},{1,0},{2,3},{3,2},{4,5},{5,4},{6,7},{7,6},{8,9},{9,8},{10,11... | collective-permute-start | bytes 2457608 | tf_op jit(solution)/shard_map/ppermute | solution.py:327
  86.6 13.7 %all-to-all-start.3 = ((bf16[16,64,128]{2,1,0:T(8,128)(2,1)}), bf16[16,64,128]{2,1,0:T(8,128)(2,1)S(1)}, u32[]{:S(2)}, u32[]{:S(2)}) async-start(bf16[16,64,128]{2,1,0:T(8,128)(2,1)} %shard_map.60), calls=%async_computation.3 | async-start | bytes 524288 | tf_op jit(solution)/shard_map/all_to_all | solution.py:227
  101.4 6.8 %collective-permute-start.1 = (bf16[8,128,128]{2,1,0:T(8,128)(2,1)S(1)}, bf16[8,128,128]{2,1,0:T(8,128)(2,1)S(1)}, u32[]{:S(2)}, u32[]{:S(2)}) collective-permute-start(bf16[8,128,128]{2,1,0:T(8,128)(2,1)S(1)} %get-tuple-element.16), channel_id=1, source_target_pairs={{0,1},{1,0},{2,3},{3,2},{4,5},{5,4},{6,7},{7,6},{8,9},{9,8},{10,11... | collective-permute-start | bytes 786440 | tf_op jit(solution)/shard_map/ppermute | solution.py:338
Sparse Core Ops, SparseCore 0:
  36.3 62.9 all-gather.1
